TPU v7x, 32 devices: a whole 2x2x4 slice. The times are simulated.
32 devices in a mesh: dp: 4 (over x, core), fsdp: 8 (over z, y).
Axes of the slice: x: 2, y: 2, z: 4, core: 2. Of those that a mesh axis runs over, the one named last changes fastest.
Arguments:
- block_in: bfloat16 [32, 1024, 1024], P(('dp', 'fsdp')), may hold values from -6 to 6
- images: bfloat16 [128, 588, 1024], P(('dp', 'fsdp')), may hold values from -6 to 6
- segment_ids: int32 [32, 1024], P(('dp', 'fsdp')), may hold values from 0 to 3, never falling along the last dimension, each value on 1 to 512 neighbouring positions
- page_map: int32 [32, 4], P(('dp', 'fsdp')), may hold values from 0 to 3, each once within a row
- ln1_gain: float32 [1024], P(('dp', 'fsdp')), may hold values from 0.25 to 1.75
- ln1_shift: float32 [1024], P(('dp', 'fsdp')), may hold values from -1.5 to 1.5
- ln2_gain: float32 [1024], P(('dp', 'fsdp')), may hold values from 0.25 to 1.75
- ln2_shift: float32 [1024], P(('dp', 'fsdp')), may hold values from -1.5 to 1.5
- ln3_gain: float32 [1024], P(('dp', 'fsdp')), may hold values from 0.25 to 1.75
- ln3_shift: float32 [1024], P(('dp', 'fsdp')), may hold values from -1.5 to 1.5
- self_query: float32 [1024, 1024], P(None, ('dp', 'fsdp')), may hold values from -0.1875 to 0.1875
- self_key: float32 [1024, 1024], P(None, ('dp', 'fsdp')), may hold values from -0.1875 to 0.1875
- self_value: float32 [1024, 1024], P(None, ('dp', 'fsdp')), may hold values from -0.1875 to 0.1875
- self_out: float32 [1024, 1024], P(None, ('dp', 'fsdp')), may hold values from -0.5 to 0.5
- cross_query: float32 [1024, 1024], P(None, ('dp', 'fsdp')), may hold values from -0.1875 to 0.1875
- cross_key: float32 [1024, 1024], P(None, ('dp', 'fsdp')), may hold values from -0.1875 to 0.1875
- cross_value: float32 [1024, 1024], P(None, ('dp', 'fsdp')), may hold values from -0.1875 to 0.1875
- cross_out: float32 [1024, 1024], P(None, ('dp', 'fsdp')), may hold values from -0.75 to 0.75
- mlp_in: float32 [1024, 4096], P(None, ('dp', 'fsdp')), may hold values from -0.1875 to 0.1875
- mlp_out: float32 [4096, 1024], P(None, ('dp', 'fsdp')), may hold values from -0.125 to 0.125
- cotangent: bfloat16 [32, 1024, 1024], P(('dp', 'fsdp')), may hold values from -6 to 6
Outputs:
- block_out: bfloat16 [32, 1024, 1024], P(('dp', 'fsdp'))
- grad_in: float32 [32, 1024, 1024], P(('dp', 'fsdp'))
- grad_images: float32 [128, 588, 1024], P(('dp', 'fsdp'))
- grad_ln1_gain: float32 [1024], P(('dp', 'fsdp'))
- grad_ln1_shift: float32 [1024], P(('dp', 'fsdp'))
- grad_ln2_gain: float32 [1024], P(('dp', 'fsdp'))
- grad_ln2_shift: float32 [1024], P(('dp', 'fsdp'))
- grad_ln3_gain: float32 [1024], P(('dp', 'fsdp'))
- grad_ln3_shift: float32 [1024], P(('dp', 'fsdp'))
- grad_self_query: float32 [1024, 1024], P(None, ('dp', 'fsdp'))
- grad_self_key: float32 [1024, 1024], P(None, ('dp', 'fsdp'))
- grad_self_value: float32 [1024, 1024], P(None, ('dp', 'fsdp'))
- grad_self_out: float32 [1024, 1024], P(None, ('dp', 'fsdp'))
- grad_cross_query: float32 [1024, 1024], P(None, ('dp', 'fsdp'))
- grad_cross_key: float32 [1024, 1024], P(None, ('dp', 'fsdp'))
- grad_cross_value: float32 [1024, 1024], P(None, ('dp', 'fsdp'))
- grad_cross_out: float32 [1024, 1024], P(None, ('dp', 'fsdp'))
- grad_mlp_in: float32 [1024, 4096], P(None, ('dp', 'fsdp'))
- grad_mlp_out: float32 [4096, 1024], P(None, ('dp', 'fsdp'))
Inputs may be any that keep to these rules, and one draw needn't show every extreme that they name: `segment_ids`: within each row segment ids never fall; each of the 4 segments holds 1 to 512 positions, and some segment of each row holds exactly 512. Each row lists every number 0 to 3 once; segment t of decoder row r reads image r * 4 + page_map[r, t].
All inputs are finite; a program needn't handle non-finite values.
Results may differ from a plain program's by a relative error of at most 0.02.
The roundings to bfloat16 on the way count: a program that leaves them out, or rounds other values in their place, can miss the bound.
Values may be sent and summed in bfloat16 or wider, within the bound.
A program may use at most 768 MiB of HBM per device.

v0:
```python
import jax
import jax.numpy as jnp
from jax import lax
from jax.sharding import PartitionSpec as P

HEADS = 16


EPSILON = 1e-05
NEGATIVE = -1e30


def layer_norm(values, norm_gain, norm_shift):
    average = jnp.mean(values, axis=-1, keepdims=True)
    centered = values - average
    variance = jnp.mean(centered * centered, axis=-1, keepdims=True)
    return centered * lax.rsqrt(variance + EPSILON) * norm_gain + norm_shift


def gelu_exact(values):
    return jax.nn.gelu(values, approximate=False)


def low_dot(left_side, right_side):
    return jnp.dot(left_side, right_side, preferred_element_type=jnp.float32)


def outer_dot(left_side, right_side):
    return lax.dot_general(
        left_side, right_side, (((0,), (0,)), ((), ())), preferred_element_type=jnp.float32
    )


def back_dot(left_side, right_side):
    return lax.dot_general(
        left_side, right_side, (((1,), (1,)), ((), ())), preferred_element_type=jnp.float32
    )


def masked_scores(query_heads, key_heads, query_tag, query_place, key_tag, key_place):
    score_scale = query_heads.shape[-1] ** (-0.5)
    scores = (
        jnp.einsum("qhd,khd->hqk", query_heads, key_heads, preferred_element_type=jnp.float32)
        * score_scale
    )
    allowed = (query_tag[:, None] == key_tag[None, :]) & (
        key_place[None, :] <= query_place[:, None]
    )
    return jnp.where(allowed[None], scores, NEGATIVE)


def attend_forward(
    queries, keys_all, values_all, query_tag, query_place, key_tag, key_place, head_count
):
    length, model_width = queries.shape
    head_size = model_width // head_count
    query_heads = queries.reshape(length, head_count, head_size)
    key_heads = keys_all.reshape(keys_all.shape[0], head_count, head_size)
    value_heads = values_all.reshape(values_all.shape[0], head_count, head_size)
    block_rows = min(512, length)
    mixed_parts = []
    total_parts = []
    for offset in range(0, length, block_rows):
        scores = masked_scores(
            query_heads[offset : offset + block_rows],
            key_heads,
            query_tag[offset : offset + block_rows],
            query_place[offset : offset + block_rows],
            key_tag,
            key_place,
        )
        row_peak = jnp.max(scores, axis=-1, keepdims=True)
        log_total = row_peak + jnp.log(jnp.sum(jnp.exp(scores - row_peak), axis=-1, keepdims=True))
        attention = jnp.exp(scores - log_total).astype(jnp.bfloat16)
        mixed_block = jnp.einsum(
            "hqk,khd->qhd", attention, value_heads, preferred_element_type=jnp.float32
        )
        mixed_parts.append(mixed_block.reshape(-1, model_width))
        total_parts.append(log_total)
    return (jnp.concatenate(mixed_parts, axis=0).astype(jnp.bfloat16), total_parts)


def attend_backward(
    queries,
    keys_all,
    values_all,
    query_tag,
    query_place,
    key_tag,
    key_place,
    head_count,
    total_parts,
    grad_mixed,
):
    length, model_width = queries.shape
    head_size = model_width // head_count
    score_scale = head_size ** (-0.5)
    key_count = keys_all.shape[0]
    query_heads = queries.reshape(length, head_count, head_size)
    key_heads = keys_all.reshape(key_count, head_count, head_size)
    value_heads = values_all.reshape(key_count, head_count, head_size)
    grad_heads = grad_mixed.reshape(length, head_count, head_size)
    grad_keys = jnp.zeros((key_count, head_count, head_size), jnp.float32)
    grad_values = jnp.zeros((key_count, head_count, head_size), jnp.float32)
    grad_query_parts = []
    block_rows = min(512, length)
    for block_index, offset in enumerate(range(0, length, block_rows)):
        query_block = query_heads[offset : offset + block_rows]
        grad_block = grad_heads[offset : offset + block_rows]
        scores = masked_scores(
            query_block,
            key_heads,
            query_tag[offset : offset + block_rows],
            query_place[offset : offset + block_rows],
            key_tag,
            key_place,
        )
        attention = jnp.exp(scores - total_parts[block_index])
        attention_low = attention.astype(jnp.bfloat16)
        grad_attention = jnp.einsum(
            "qhd,khd->hqk", grad_block, value_heads, preferred_element_type=jnp.float32
        )
        inner_sum = jnp.sum(grad_attention * attention, axis=-1, keepdims=True)
        grad_scores = (attention * (grad_attention - inner_sum)).astype(jnp.bfloat16)
        grad_query_block = (
            jnp.einsum("hqk,khd->qhd", grad_scores, key_heads, preferred_element_type=jnp.float32)
            * score_scale
        )
        grad_query_parts.append(grad_query_block.reshape(-1, model_width))
        grad_keys = (
            grad_keys
            + jnp.einsum(
                "hqk,qhd->khd", grad_scores, query_block, preferred_element_type=jnp.float32
            )
            * score_scale
        )
        grad_values = grad_values + jnp.einsum(
            "hqk,qhd->khd", attention_low, grad_block, preferred_element_type=jnp.float32
        )
    grad_queries = jnp.concatenate(grad_query_parts, axis=0).astype(jnp.bfloat16)
    return (
        grad_queries,
        grad_keys.reshape(key_count, model_width).astype(jnp.bfloat16),
        grad_values.reshape(key_count, model_width).astype(jnp.bfloat16),
    )


def per_device(
    block_in,
    images,
    segment_ids,
    page_map,
    ln1_gain,
    ln1_shift,
    ln2_gain,
    ln2_shift,
    ln3_gain,
    ln3_shift,
    self_query,
    self_key,
    self_value,
    self_out,
    cross_query,
    cross_key,
    cross_value,
    cross_out,
    mlp_in,
    mlp_out,
    cotangent,
):
    masters = (
        ln1_gain,
        ln1_shift,
        ln2_gain,
        ln2_shift,
        ln3_gain,
        ln3_shift,
        self_query,
        self_key,
        self_value,
        self_out,
        cross_query,
        cross_key,
        cross_value,
        cross_out,
        mlp_in,
        mlp_out,
    )
    lowered = [master.astype(jnp.bfloat16) for master in masters]
    gathered = (
        lax.all_gather(lowered[0], ("dp", "fsdp"), axis=0, tiled=True),
        lax.all_gather(lowered[1], ("dp", "fsdp"), axis=0, tiled=True),
        lax.all_gather(lowered[2], ("dp", "fsdp"), axis=0, tiled=True),
        lax.all_gather(lowered[3], ("dp", "fsdp"), axis=0, tiled=True),
        lax.all_gather(lowered[4], ("dp", "fsdp"), axis=0, tiled=True),
        lax.all_gather(lowered[5], ("dp", "fsdp"), axis=0, tiled=True),
        lax.all_gather(lowered[6], ("dp", "fsdp"), axis=1, tiled=True),
        lax.all_gather(lowered[7], ("dp", "fsdp"), axis=1, tiled=True),
        lax.all_gather(lowered[8], ("dp", "fsdp"), axis=1, tiled=True),
        lax.all_gather(lowered[9], ("dp", "fsdp"), axis=1, tiled=True),
        lax.all_gather(lowered[10], ("dp", "fsdp"), axis=1, tiled=True),
        lax.all_gather(lowered[11], ("dp", "fsdp"), axis=1, tiled=True),
        lax.all_gather(lowered[12], ("dp", "fsdp"), axis=1, tiled=True),
        lax.all_gather(lowered[13], ("dp", "fsdp"), axis=1, tiled=True),
        lax.all_gather(lowered[14], ("dp", "fsdp"), axis=1, tiled=True),
        lax.all_gather(lowered[15], ("dp", "fsdp"), axis=1, tiled=True),
    )
    norm_params = [param.astype(jnp.float32) for param in gathered[:6]]
    row_count, row_length, model_width = block_in.shape
    page_count = page_map.shape[1]
    image_tokens = images.shape[1]
    token_count = row_count * row_length
    image_span = page_count * image_tokens
    inputs = block_in.reshape(token_count, model_width).astype(jnp.float32)
    flat_images = images.reshape(row_count * image_span, model_width)
    places = jnp.arange(row_length, dtype=jnp.int32)
    zero_places = jnp.zeros((row_length,), jnp.int32)
    image_places = jnp.zeros((image_span,), jnp.int32)
    image_tags = jnp.arange(image_span, dtype=jnp.int32) // image_tokens
    page_index = jnp.arange(page_count, dtype=jnp.int32)
    query_images = jnp.sum(
        jnp.where(segment_ids[:, :, None] == page_index[None, None, :], page_map[:, None, :], 0),
        axis=2,
    )
    normed_one = layer_norm(inputs, norm_params[0], norm_params[1])
    low_one = normed_one.astype(jnp.bfloat16)
    self_queries = low_dot(low_one, gathered[6]).astype(jnp.bfloat16)
    self_keys = low_dot(low_one, gathered[7]).astype(jnp.bfloat16)
    self_values = low_dot(low_one, gathered[8]).astype(jnp.bfloat16)
    row_index = 0
    mixed_row, totals = attend_forward(
        self_queries,
        self_keys,
        self_values,
        segment_ids[row_index],
        places,
        segment_ids[row_index],
        places,
        HEADS,
    )
    self_parts = mixed_row
    self_totals = [totals]
    after_self = inputs + low_dot(self_parts, gathered[9])
    normed_two = layer_norm(after_self, norm_params[2], norm_params[3])
    low_two = normed_two.astype(jnp.bfloat16)
    cross_queries = low_dot(low_two, gathered[10]).astype(jnp.bfloat16)
    cross_keys = low_dot(flat_images, gathered[11]).astype(jnp.bfloat16)
    cross_values = low_dot(flat_images, gathered[12]).astype(jnp.bfloat16)
    row_index = 0
    mixed_row, totals = attend_forward(
        cross_queries,
        cross_keys,
        cross_values,
        query_images[row_index],
        zero_places,
        image_tags,
        image_places,
        HEADS,
    )
    cross_totals = [totals]
    after_cross = after_self + low_dot(mixed_row, gathered[13])
    normed_three = layer_norm(after_cross, norm_params[4], norm_params[5])
    low_three = normed_three.astype(jnp.bfloat16)
    pre_act = low_dot(low_three, gathered[14])
    hidden = gelu_exact(pre_act).astype(jnp.bfloat16)
    block_out = after_cross + low_dot(hidden, gathered[15])
    weights_back = (
        lax.all_gather(lowered[0], ("dp", "fsdp"), axis=0, tiled=True),
        lax.all_gather(lowered[1], ("dp", "fsdp"), axis=0, tiled=True),
        lax.all_gather(lowered[2], ("dp", "fsdp"), axis=0, tiled=True),
        lax.all_gather(lowered[3], ("dp", "fsdp"), axis=0, tiled=True),
        lax.all_gather(lowered[4], ("dp", "fsdp"), axis=0, tiled=True),
        lax.all_gather(lowered[5], ("dp", "fsdp"), axis=0, tiled=True),
        lax.all_gather(lowered[6], ("dp", "fsdp"), axis=1, tiled=True),
        lax.all_gather(lowered[7], ("dp", "fsdp"), axis=1, tiled=True),
        lax.all_gather(lowered[8], ("dp", "fsdp"), axis=1, tiled=True),
        lax.all_gather(lowered[9], ("dp", "fsdp"), axis=1, tiled=True),
        lax.all_gather(lowered[10], ("dp", "fsdp"), axis=1, tiled=True),
        lax.all_gather(lowered[11], ("dp", "fsdp"), axis=1, tiled=True),
        lax.all_gather(lowered[12], ("dp", "fsdp"), axis=1, tiled=True),
        lax.all_gather(lowered[13], ("dp", "fsdp"), axis=1, tiled=True),
        lax.all_gather(lowered[14], ("dp", "fsdp"), axis=1, tiled=True),
        lax.all_gather(lowered[15], ("dp", "fsdp"), axis=1, tiled=True),
    )
    norm_back = [param.astype(jnp.float32) for param in weights_back[:6]]
    grad_out = cotangent.reshape(token_count, model_width).astype(jnp.float32)
    grad_out_low = grad_out.astype(jnp.bfloat16)
    grad_mlp_out = outer_dot(hidden, grad_out_low)
    grad_hidden = back_dot(grad_out_low, weights_back[15])
    gelu_pull = jax.vjp(gelu_exact, pre_act)[1]
    grad_pre = gelu_pull(grad_hidden)[0].astype(jnp.bfloat16)
    grad_mlp_in = outer_dot(low_three, grad_pre)
    grad_low_three = back_dot(grad_pre, weights_back[14])
    norm_pull_three = jax.vjp(layer_norm, after_cross, norm_back[4], norm_back[5])[1]
    grad_cross_norm, grad_gain_three, grad_shift_three = norm_pull_three(grad_low_three)
    grad_after_cross = grad_out + grad_cross_norm
    grad_cross_low = grad_after_cross.astype(jnp.bfloat16)
    grad_cross_out = outer_dot(mixed_row, grad_cross_low)
    grad_cross_mixed = back_dot(grad_cross_low, weights_back[13]).astype(jnp.bfloat16)
    row_index = 0
    grad_q_row, grad_k_row, grad_v_row = attend_backward(
        cross_queries,
        cross_keys,
        cross_values,
        query_images[row_index],
        zero_places,
        image_tags,
        image_places,
        HEADS,
        cross_totals[row_index],
        grad_cross_mixed,
    )
    cross_query_parts = grad_q_row
    cross_key_parts = grad_k_row
    cross_value_parts = grad_v_row
    grad_cross_query = outer_dot(low_two, cross_query_parts)
    grad_cross_key = outer_dot(flat_images, cross_key_parts)
    grad_cross_value = outer_dot(flat_images, cross_value_parts)
    grad_images = back_dot(cross_key_parts, weights_back[11]) + back_dot(
        cross_value_parts, weights_back[12]
    )
    grad_low_two = back_dot(cross_query_parts, weights_back[10])
    norm_pull_two = jax.vjp(layer_norm, after_self, norm_back[2], norm_back[3])[1]
    grad_self_norm, grad_gain_two, grad_shift_two = norm_pull_two(grad_low_two)
    grad_after_self = grad_after_cross + grad_self_norm
    grad_self_low = grad_after_self.astype(jnp.bfloat16)
    grad_self_out = outer_dot(self_parts, grad_self_low)
    grad_self_mixed = back_dot(grad_self_low, weights_back[9]).astype(jnp.bfloat16)
    row_index = 0
    grad_q_row, grad_k_row, grad_v_row = attend_backward(
        self_queries,
        self_keys,
        self_values,
        segment_ids[row_index],
        places,
        segment_ids[row_index],
        places,
        HEADS,
        self_totals[row_index],
        grad_self_mixed,
    )
    grad_self_query = outer_dot(low_one, grad_q_row)
    grad_self_key = outer_dot(low_one, grad_k_row)
    grad_self_value = outer_dot(low_one, grad_v_row)
    grad_low_one = (
        back_dot(grad_q_row, weights_back[6])
        + back_dot(grad_k_row, weights_back[7])
        + back_dot(grad_v_row, weights_back[8])
    )
    norm_pull_one = jax.vjp(layer_norm, inputs, norm_back[0], norm_back[1])[1]
    grad_input_norm, grad_gain_one, grad_shift_one = norm_pull_one(grad_low_one)
    grad_in = grad_after_self + grad_input_norm
    summed = (
        lax.psum_scatter(grad_gain_one, ("dp", "fsdp"), scatter_dimension=0, tiled=True),
        lax.psum_scatter(grad_shift_one, ("dp", "fsdp"), scatter_dimension=0, tiled=True),
        lax.psum_scatter(grad_gain_two, ("dp", "fsdp"), scatter_dimension=0, tiled=True),
        lax.psum_scatter(grad_shift_two, ("dp", "fsdp"), scatter_dimension=0, tiled=True),
        lax.psum_scatter(grad_gain_three, ("dp", "fsdp"), scatter_dimension=0, tiled=True),
        lax.psum_scatter(grad_shift_three, ("dp", "fsdp"), scatter_dimension=0, tiled=True),
        lax.psum_scatter(grad_self_query, ("dp", "fsdp"), scatter_dimension=1, tiled=True),
        lax.psum_scatter(grad_self_key, ("dp", "fsdp"), scatter_dimension=1, tiled=True),
        lax.psum_scatter(grad_self_value, ("dp", "fsdp"), scatter_dimension=1, tiled=True),
        lax.psum_scatter(grad_self_out, ("dp", "fsdp"), scatter_dimension=1, tiled=True),
        lax.psum_scatter(grad_cross_query, ("dp", "fsdp"), scatter_dimension=1, tiled=True),
        lax.psum_scatter(grad_cross_key, ("dp", "fsdp"), scatter_dimension=1, tiled=True),
        lax.psum_scatter(grad_cross_value, ("dp", "fsdp"), scatter_dimension=1, tiled=True),
        lax.psum_scatter(grad_cross_out, ("dp", "fsdp"), scatter_dimension=1, tiled=True),
        lax.psum_scatter(grad_mlp_in, ("dp", "fsdp"), scatter_dimension=1, tiled=True),
        lax.psum_scatter(grad_mlp_out, ("dp", "fsdp"), scatter_dimension=1, tiled=True),
    )
    return (
        block_out.reshape(row_count, row_length, model_width).astype(jnp.bfloat16),
        grad_in.reshape(row_count, row_length, model_width),
        grad_images.reshape(images.shape),
        summed[0],
        summed[1],
        summed[2],
        summed[3],
        summed[4],
        summed[5],
        summed[6],
        summed[7],
        summed[8],
        summed[9],
        summed[10],
        summed[11],
        summed[12],
        summed[13],
        summed[14],
        summed[15],
    )


def solution(mesh):
    in_specs = (
        P(("dp", "fsdp"), None, None),
        P(("dp", "fsdp"), None, None),
        P(("dp", "fsdp"), None),
        P(("dp", "fsdp"), None),
        P(("dp", "fsdp")),
        P(("dp", "fsdp")),
        P(("dp", "fsdp")),
        P(("dp", "fsdp")),
        P(("dp", "fsdp")),
        P(("dp", "fsdp")),
        P(None, ("dp", "fsdp")),
        P(None, ("dp", "fsdp")),
        P(None, ("dp", "fsdp")),
        P(None, ("dp", "fsdp")),
        P(None, ("dp", "fsdp")),
        P(None, ("dp", "fsdp")),
        P(None, ("dp", "fsdp")),
        P(None, ("dp", "fsdp")),
        P(None, ("dp", "fsdp")),
        P(None, ("dp", "fsdp")),
        P(("dp", "fsdp"), None, None),
    )
    out_specs = (
        P(("dp", "fsdp"), None, None),
        P(("dp", "fsdp"), None, None),
        P(("dp", "fsdp"), None, None),
        P(("dp", "fsdp")),
        P(("dp", "fsdp")),
        P(("dp", "fsdp")),
        P(("dp", "fsdp")),
        P(("dp", "fsdp")),
        P(("dp", "fsdp")),
        P(None, ("dp", "fsdp")),
        P(None, ("dp", "fsdp")),
        P(None, ("dp", "fsdp")),
        P(None, ("dp", "fsdp")),
        P(None, ("dp", "fsdp")),
        P(None, ("dp", "fsdp")),
        P(None, ("dp", "fsdp")),
        P(None, ("dp", "fsdp")),
        P(None, ("dp", "fsdp")),
        P(None, ("dp", "fsdp")),
    )
    return jax.shard_map(
        per_device, mesh=mesh, in_specs=in_specs, out_specs=out_specs, check_vma=False
    )
```

profile of v0, /device:TPU:0, one launch (start us, length us, event | category | flops | bytes accessed | tf_op | source)
XLA Modules:
  0.0 2693.8 jit_solution(16701418115722663338)
XLA Ops:
  25.4 43.6 %all-reduce.13 = (bf16[1024]{0:T(1024)(128)(2,1)S(1)}, bf16[1024]{0:T(1024)(128)(2,1)S(1)}, bf16[1024]{0:T(1024)(128)(2,1)S(1)}, bf16[1024]{0:T(1024)(128)(2,1)S...) all-reduce(bf16[1024]{0:T(1024)(128)(2,1)S(1)} %dynamic-update-slic, ...), channel_id=1, replica_groups=mesh['dp'=4,'fsdp'=8] {'dp','fsdp'}, use_global_device_ids=true, to_apply=%add.1 | all-reduce | flops 6144 | bytes 24576
  98.6 31.3 %all-gather.23.cloned.1.call-done = bf16[1024,1024]{0,1:T(8,128)(2,1)} async-done(((bf16[1024,32]{0,1:T(8,128)(2,1)}), bf16[1024,1024]{0,1:T(8,128)(2,1)}) %all-gather.23.cloned.1.call-update) | async-done | bytes 2097168 | tf_op jit(solution)/shard_map/all_gather | solution.py:202
  146.7 41.9 %all-gather.19.cloned.1.call-done = bf16[1024,1024]{0,1:T(8,128)(2,1)} async-done(((bf16[1024,32]{0,1:T(8,128)(2,1)}), bf16[1024,1024]{0,1:T(8,128)(2,1)}) %all-gather.19.cloned.1.call-update) | async-done | bytes 2097168 | tf_op jit(solution)/shard_map/all_gather | solution.py:203
  205.8 41.5 %all-gather.15.cloned.1.call-done = bf16[1024,1024]{0,1:T(8,128)(2,1)} async-done(((bf16[1024,32]{0,1:T(8,128)(2,1)}), bf16[1024,1024]{0,1:T(8,128)(2,1)}) %all-gather.15.cloned.1.call-update) | async-done | bytes 2097168 | tf_op jit(solution)/shard_map/all_gather | solution.py:198
  372.0 51.4 %all-gather.21.cloned.1.call-done = bf16[1024,1024]{0,1:T(8,128)(2,1)} async-done(((bf16[1024,32]{0,1:T(8,128)(2,1)}), bf16[1024,1024]{0,1:T(8,128)(2,1)}) %all-gather.21.cloned.1.call-update) | async-done | bytes 2097168 | tf_op jit(solution)/shard_map/all_gather | solution.py:201
  428.9 30.5 %fusion.1 = (f32[16,512]{1,0:T(8,128)S(1)}, f32[16,512,2352]{1,2,0:T(8,128)}) fusion(pred[512,2352]{0,1:T(8,128)(4,1)S(1)} %get-tuple-element.128, bf16[512,16,64]{0,2,1:T(8,128)(2,1)S(1)} %bitcast.218, bf16[2352,16,64]{0,2,1:T(8,128)(2,1)} %bitcast.196), kind=kOutput, calls=%fused_computation.11 | convolution fusion | flops 2524045312 | bytes 84172800 | tf_op jit(solution)/shard_map/qhd,khd->hqk/dot_general | solution.py:43
  484.6 29.9 %fusion = (f32[16,512]{1,0:T(8,128)S(1)}, f32[16,512,2352]{1,2,0:T(8,128)}) fusion(pred[512,2352]{0,1:T(8,128)(4,1)S(1)} %copy-done, bf16[512,16,64]{0,2,1:T(8,128)(2,1)S(1)} %bitcast.216, bf16[2352,16,64]{0,2,1:T(8,128)(2,1)} %bitcast.197), kind=kOutput, calls=%fused_computation.10 | convolution fusion | flops 2524045312 | bytes 84172800 | tf_op jit(solution)/shard_map/qhd,khd->hqk/dot_general | solution.py:43
  540.5 32.6 %convolution_convert_fusion.8 = bf16[16,64,512]{2,1,0:T(8,128)(2,1)} fusion(bf16[2352,16,64]{0,2,1:T(8,128)(2,1)} %bitcast.204, f32[16,512,2352]{1,2,0:T(8,128)} %get-tuple-element.142, f32[16,512]{1,0:T(8,128)S(1)} %log_add_fusion, pred[512,2352]{0,1:T(8,128)(4,1)S(1)} %get-tuple-element.128), kind=kOutput, calls=%fused_computation.118 | convolution fusion | flops 2543845376 | bytes 84172800 | tf_op jit(solution)/shard_map/hqk,khd->qhd/dot_general | solution.py:75
  573.1 32.3 %convolution_convert_fusion.9 = bf16[16,64,512]{2,1,0:T(8,128)(2,1)S(1)} fusion(bf16[2352,16,64]{0,2,1:T(8,128)(2,1)} %bitcast.205, f32[16,512,2352]{1,2,0:T(8,128)} %get-tuple-element.144, f32[16,512]{1,0:T(8,128)S(1)} %log_add_fusion.1, pred[512,2352]{0,1:T(8,128)(4,1)S(1)} %copy-done), kind=kOutput, calls=%fused_computation.119 | convolution fusion | flops 2543845376 | bytes 84172800 | tf_op jit(solution)/shard_map/hqk,khd->qhd/dot_general | solution.py:75
  614.2 47.2 %multiply_convert_fusion.4 = (bf16[1024,4096]{1,0:T(8,128)(2,1)}, f32[1024,4096]{1,0:T(8,128)}, f32[1024,4096]{1,0:T(8,128)}) fusion(bf16[1024,4096]{1,0:T(8,128)(2,1)} %all-gather.27.cloned.1.call-done, bf16[1024,1024]{0,1:T(8,128)(2,1)S(1)} %add_convert_fusion.7.clone.4), kind=kOutput, calls=%fused_computation.31 | convolution fusion | flops 8862564352 | bytes 52428800 | tf_op jit(solution)/shard_map/dot_general | solution.py:25
  728.3 32.2 %fusion.53 = f32[16,64,2352]{2,1,0:T(8,128)} fusion(bf16[512,16,64]{0,2,1:T(8,128)(2,1)S(1)} %bitcast.228, f32[16,512,2352]{1,2,0:T(8,128)} %get-tuple-element.144, f32[16,512]{1,0:T(8,128)S(1)} %copy-done.41, pred[512,2352]{0,1:T(8,128)(4,1)S(1)} %copy-done.1), kind=kOutput, calls=%fused_computation.131 | convolution fusion | flops 2543321088 | bytes 88989696 | tf_op jit(solution)/shard_map/hqk,qhd->khd/dot_general | solution.py:137
  760.5 57.5 %multiply_reduce_fusion = (f32[16,512]{1,0:T(8,128)S(1)}, f32[16,512,2352]{1,2,0:T(8,128)}) fusion(f32[16,512,2352]{1,2,0:T(8,128)} %get-tuple-element.142, f32[16,512]{1,0:T(8,128)S(1)} %copy-done.39, pred[512,2352]{0,1:T(8,128)(4,1)S(1)} %copy-done.3, bf16[512,16,64]{0,2,1:T(8,128)(2,1)} %bitcast.230, bf16[2352,16,64]{0,2,1:T(8,128)(2,1)} %bitcast.206), kind=kOutput, calls=%fused_computation.1 | convolution fusion | flops 2562580480 | bytes 161275904 | tf_op jit(solution)/shard_map/qhd,khd->hqk/dot_general | solution.py:120
  818.0 33.7 %add_convert_fusion.1 = bf16[16,64,2352]{2,1,0:T(8,128)(2,1)} fusion(f32[16,64,2352]{2,1,0:T(8,128)} %fusion.53, bf16[512,16,64]{0,2,1:T(8,128)(2,1)} %bitcast.231, f32[16,512,2352]{1,2,0:T(8,128)} %get-tuple-element.142, f32[16,512]{1,0:T(8,128)S(1)} %copy-done.39, pred[512,2352]{0,1:T(8,128)(4,1)S(1)} %copy-done.3), kind=kOutput, calls=%fused_computation.45 | convolution fusion | flops 2548137984 | bytes 93806592 | tf_op jit(solution)/shard_map/hqk,qhd->khd/dot_general | solution.py:137
  861.9 57.7 %multiply_reduce_fusion.1 = (f32[16,512]{1,0:T(8,128)}, f32[16,512,2352]{1,2,0:T(8,128)}) fusion(f32[16,512,2352]{1,2,0:T(8,128)} %get-tuple-element.144, f32[16,512]{1,0:T(8,128)S(1)} %copy-done.41, pred[512,2352]{0,1:T(8,128)(4,1)S(1)} %copy-done.1, bf16[512,16,64]{0,2,1:T(8,128)(2,1)S(1)} %bitcast.229, bf16[2352,16,64]{0,2,1:T(8,128)(2,1)} %bitcast.207), kind=kOutput, calls=%fused_computation.3 | convolution fusion | flops 2562580480 | bytes 161275904 | tf_op jit(solution)/shard_map/qhd,khd->hqk/dot_general | solution.py:120
  919.7 62.3 %multiply_convert_fusion = bf16[16,512,2352]{1,2,0:T(8,128)(2,1)} fusion(f32[16,512,2352]{1,2,0:T(8,128)} %get-tuple-element.149, f32[16,512,2352]{1,2,0:T(8,128)} %get-tuple-element.142, f32[16,512]{1,0:T(8,128)S(1)} %get-tuple-element.148, f32[16,512]{1,0:T(8,128)S(1)} %copy-done.39, pred[512,2352]{0,1:T(8,128)(4,1)S(1)} %copy-done.3), kind=kLoop, calls=%fused_computation | loop fusion | flops 115605504 | bytes 193945600 | tf_op jit(solution)/shard_map/convert_element_type | solution.py:124
  982.0 61.4 %multiply_convert_fusion.1 = bf16[16,512,2352]{1,2,0:T(8,128)(2,1)} fusion(f32[16,512,2352]{1,2,0:T(8,128)} %get-tuple-element.151, f32[16,512,2352]{1,2,0:T(8,128)} %get-tuple-element.144, f32[16,512]{1,0:T(8,128)S(1)} %copy-done.48, f32[16,512]{1,0:T(8,128)S(1)} %copy-done.41, pred[512,2352]{0,1:T(8,128)(4,1)S(1)} %copy-done.1), kind=kLoop, calls=%fused_computation.2 | loop fusion | flops 115605504 | bytes 193945600 | tf_op jit(solution)/shard_map/convert_element_type | solution.py:124
  1212.1 26.2 multiply_reduce_fusion.2
  1264.6 54.6 %multiply_convert_fusion.2 = (bf16[16,512,1024]{2,1,0:T(8,128)(2,1)}, bf16[16,512,1024]{2,1,0:T(8,128)(2,1)}) fusion(f32[16,512,1024]{2,1,0:T(8,128)} %get-tuple-element.153, f32[16,512,1024]{2,1,0:T(8,128)} %get-tuple-element.136, f32[16,512]{1,0:T(8,128)S(1)} %get-tuple-element.152, f32[16,512]{1,0:T(8,128)S(1)} %copy-done.47, ...), kind=kLoop, calls=%fused_computation.14 | loop fusion | flops 100663296 | bytes 168951808 | tf_op jit(solution)/shard_map/convert_element_type | solution.py:124
  1486.2 38.9 %all-reduce.12 = (f32[1024]{0:T(1024)S(1)}, f32[1024]{0:T(1024)S(1)}, f32[1024]{0:T(1024)S(1)}, f32[1024]{0:T(1024)S(1)}, f32[1024]{0:T(1024)S(1)}, /*index=5*/f32[1024]{0:T(1024)S(1)}) all-reduce(f32[1024]{0:T(1024)S(1)} %get-tuple-element.99, ...), channel_id=2, replica_groups=mesh['dp'=4,'fsdp'=8] {'dp','fsdp'}, use_global_device_ids=true, to_apply=%region_26.27.clone | all-reduce | flops 6144 | bytes 49152
  1540.8 135.8 %reduce-scatter.15.cloned.1.call-done = f32[1024,32]{0,1:T(8,128)} async-done(((f32[1024,1024]{0,1:T(8,128)}), f32[1024,32]{0,1:T(8,128)}) %reduce-scatter.15.cloned.1.call-update) | async-done | bytes 131088 | tf_op jit(solution)/shard_map/reduce_scatter | solution.py:362
  1676.6 145.6 %reduce-scatter.11.cloned.1.call-done = f32[1024,32]{0,1:T(8,128)} async-done(((f32[1024,1024]{0,1:T(8,128)}), f32[1024,32]{0,1:T(8,128)}) %reduce-scatter.11.cloned.1.call-update) | async-done | bytes 131088 | tf_op jit(solution)/shard_map/reduce_scatter | solution.py:360
  1822.2 145.8 %reduce-scatter.13.cloned.1.call-done = f32[1024,32]{0,1:T(8,128)} async-done(((f32[1024,1024]{0,1:T(8,128)}), f32[1024,32]{0,1:T(8,128)}) %reduce-scatter.13.cloned.1.call-update) | async-done | bytes 131088 | tf_op jit(solution)/shard_map/reduce_scatter | solution.py:361
  1968.1 358.5 %reduce-scatter.27.cloned.1.call-done = f32[1024,128]{1,0:T(8,128)} async-done(((f32[1024,4096]{1,0:T(8,128)}), f32[1024,128]{1,0:T(8,128)}) %reduce-scatter.27.cloned.1.call-update) | async-done | bytes 524304 | tf_op jit(solution)/shard_map/reduce_scatter | solution.py:368
  2326.6 360.1 %reduce-scatter.29.cloned.1.call-done = f32[4096,32]{0,1:T(8,128)} async-done(((f32[4096,1024]{0,1:T(8,128)}), f32[4096,32]{0,1:T(8,128)}) %reduce-scatter.29.cloned.1.call-update) | async-done | bytes 524304 | tf_op jit(solution)/shard_map/reduce_scatter | solution.py:369
  (413 shorter events, 725.2 us)
Async XLA Ops:
  7.3 85.1 %all-gather.13.cloned.1.call-start = ((), (), s32[]{:S(2)}) async-start(), calls=%async_computation.11 | async-start | bytes 2162688 | tf_op jit(solution)/shard_map/all_gather | solution.py:197
  8.9 121.0 %all-gather.23.cloned.1.call-start = ((), (), s32[]{:S(2)}) async-start(), calls=%async_computation.16 | async-start | bytes 2162688 | tf_op jit(solution)/shard_map/all_gather | solution.py:202
  10.5 178.1 %all-gather.19.cloned.1.call-start = ((), (), s32[]{:S(2)}) async-start(), calls=%async_computation.14 | async-start | bytes 2162688 | tf_op jit(solution)/shard_map/all_gather | solution.py:203
  12.1 235.2 %all-gather.15.cloned.1.call-start = ((), (), s32[]{:S(2)}) async-start(), calls=%async_computation.12 | async-start | bytes 2162688 | tf_op jit(solution)/shard_map/all_gather | solution.py:198
  13.7 296.7 %all-gather.11.cloned.1.call-start = ((), (), s32[]{:S(2)}) async-start(), calls=%async_computation.10 | async-start | bytes 2162688 | tf_op jit(solution)/shard_map/all_gather | solution.py:199
  15.4 349.2 %all-gather.17.cloned.1.call-start = ((), (), s32[]{:S(2)}) async-start(), calls=%async_computation.13 | async-start | bytes 2162688 | tf_op jit(solution)/shard_map/all_gather | solution.py:200
  17.0 406.4 %all-gather.21.cloned.1.call-start = ((), (), s32[]{:S(2)}) async-start(), calls=%async_computation.15 | async-start | bytes 2162688 | tf_op jit(solution)/shard_map/all_gather | solution.py:201
  18.6 586.8 %all-gather.25.cloned.1.call-start = ((), (), s32[]{:S(2)}) async-start(), calls=%async_computation.17 | async-start | bytes 2162688 | tf_op jit(solution)/shard_map/all_gather | solution.py:204
  20.2 594.0 %all-gather.27.cloned.1.call-start = ((), (), s32[]{:S(2)}) async-start(), calls=%async_computation.18 | async-start | bytes 8650752 | tf_op jit(solution)/shard_map/all_gather | solution.py:205
  22.1 639.4 %all-gather.29.cloned.1.call-start = ((), (), s32[]{:S(2)}) async-start(), calls=%async_computation.19 | async-start | bytes 8650752 | tf_op jit(solution)/shard_map/all_gather | solution.py:206
  23.9 1516.8 %reduce-scatter.25.cloned.1.call-start = ((), (), s32[]{:S(2)}) async-start(), calls=%async_computation.27 | async-start | bytes 4325376 | tf_op jit(solution)/shard_map/reduce_scatter | solution.py:367
  69.0 241.5 %copy-start.66 = (f32[1024]{0:T(1024)}, f32[1024]{0:T(1024)S(1)}, u32[]{:S(2)}) copy-start(f32[1024]{0:T(1024)S(1)} %convert_element_type.217) | copy-start | bytes 12292
  69.0 354.4 %copy-start.54 = (f32[1024]{0:T(1024)}, f32[1024]{0:T(1024)S(1)}, u32[]{:S(2)}) copy-start(f32[1024]{0:T(1024)S(1)} %convert_element_type.233) | copy-start | bytes 12292
  69.6 353.8 %copy-start.86 = (f32[1024]{0:T(1024)}, f32[1024]{0:T(1024)S(1)}, u32[]{:S(2)}) copy-start(f32[1024]{0:T(1024)S(1)} %convert_element_type.235) | copy-start | bytes 12292
  91.1 449.4 %copy-start.2 = (pred[512,2352]{0,1:T(8,128)(4,1)}, pred[512,2352]{0,1:T(8,128)(4,1)S(1)}, u32[]{:S(2)}) copy-start(pred[512,2352]{0,1:T(8,128)(4,1)S(1)} %get-tuple-element.128) | copy-start | bytes 3612676
  727.8 813.0 %reduce-scatter.23.cloned.1.call-start = ((), (), s32[]{:S(2)}) async-start(), calls=%async_computation.26 | async-start | bytes 4325376 | tf_op jit(solution)/shard_map/reduce_scatter | solution.py:366
  919.6 621.1 %reduce-scatter.21.cloned.1.call-start = ((), (), s32[]{:S(2)}) async-start(), calls=%async_computation.25 | async-start | bytes 4325376 | tf_op jit(solution)/shard_map/reduce_scatter | solution.py:365
  1095.9 444.8 %reduce-scatter.19.cloned.1.call-start = ((), (), s32[]{:S(2)}) async-start(), calls=%async_computation.24 | async-start | bytes 4325376 | tf_op jit(solution)/shard_map/reduce_scatter | solution.py:364
  1137.5 403.3 %reduce-scatter.17.cloned.1.call-start = ((), (), s32[]{:S(2)}) async-start(), calls=%async_computation.23 | async-start | bytes 4325376 | tf_op jit(solution)/shard_map/reduce_scatter | solution.py:363
  1170.0 506.6 %reduce-scatter.15.cloned.1.call-start = ((), (), s32[]{:S(2)}) async-start(), calls=%async_computation.22 | async-start | bytes 4325376 | tf_op jit(solution)/shard_map/reduce_scatter | solution.py:362
  1264.5 557.7 %reduce-scatter.11.cloned.1.call-start = ((), (), s32[]{:S(2)}) async-start(), calls=%async_computation.20 | async-start | bytes 4325376 | tf_op jit(solution)/shard_map/reduce_scatter | solution.py:360
  1349.0 619.0 %reduce-scatter.13.cloned.1.call-start = ((), (), s32[]{:S(2)}) async-start(), calls=%async_computation.21 | async-start | bytes 4325376 | tf_op jit(solution)/shard_map/reduce_scatter | solution.py:361
  1374.1 952.4 %reduce-scatter.27.cloned.1.call-start = ((), (), s32[]{:S(2)}) async-start(), calls=%async_computation.28 | async-start | bytes 17301504 | tf_op jit(solution)/shard_map/reduce_scatter | solution.py:368
  1391.6 1295.2 %reduce-scatter.29.cloned.1.call-start = ((), (), s32[]{:S(2)}) async-start(), calls=%async_computation.29 | async-start | bytes 17301504 | tf_op jit(solution)/shard_map/reduce_scatter | solution.py:369
  (106 other events, 2837.3 us)
Sparse Core Ops, SparseCore 0:
  11.6 59.2 all-gather.12
  74.5 55.2 all-gather.22
  133.4 55.1 all-gather.18
  192.1 55.2 all-gather.14
  250.7 55.2 all-gather.10
  309.4 55.1 all-gather.16
  368.2 55.2 all-gather.20
  426.9 55.2 all-gather.24
  485.1 90.6 all-gather.26
  578.6 75.2 all-gather.28
  727.9 144.1 reduce-scatter.24
  919.8 144.5 reduce-scatter.22
  1096.0 143.3 reduce-scatter.20
  1242.2 143.4 reduce-scatter.18
  1388.4 142.9 reduce-scatter.16
  1534.1 142.4 reduce-scatter.14
  1679.3 142.8 reduce-scatter.10
  1824.9 143.0 reduce-scatter.12
  1970.9 355.6 reduce-scatter.26
  2329.3 357.3 reduce-scatter.28
where the time goes:
time: 2700 us; the launch traced here: 2690 us
  waiting for transfers between devices  1330 us (49%)
  matrix products  855 us (32%)
  other arithmetic  309 us (11%)
  local copies, waits for them, and re-layouts  101 us (4%)
  blocking collectives  82.5 us (3%)
    reduce_scatter x1, waiting for transfers between devices, per_device(): lax.psum_scatter(grad_mlp_out, ('dp', 'fsdp'), scatter_dimension=1, tiled...  360 us
    reduce_scatter x1, waiting for transfers between devices, per_device(): lax.psum_scatter(grad_mlp_in, ('dp', 'fsdp'), scatter_dimension=1, tiled=...  359 us
    convert_element_type x3, other arithmetic, attend_backward(): (attention * (grad_attention - inner_sum)).astype(jnp.bfloat16)  178 us
    dot_general x4, matrix products, attend_backward(): jnp.einsum('qhd,khd->hqk', grad_block, value_heads, preferred_element_typ...  168 us
    reduce_scatter x1, waiting for transfers between devices, per_device(): lax.psum_scatter(grad_self_key, ('dp', 'fsdp'), scatter_dimension=1, tile...  146 us
    reduce_scatter x1, waiting for transfers between devices, per_device(): lax.psum_scatter(grad_self_query, ('dp', 'fsdp'), scatter_dimension=1, ti...  146 us
    reduce_scatter x1, waiting for transfers between devices, per_device(): lax.psum_scatter(grad_self_value, ('dp', 'fsdp'), scatter_dimension=1, ti...  136 us
    dot_general x10, matrix products, low_dot(): return jnp.dot(left_side, right_side, preferred_element_type=jnp.float32)  113 us
  transfers between devices with their start and end apart: 20, of which 10 were waited for; matrix products, arithmetic and copies ran while one was open for 44% of the time, Pallas kernels for 0%

commit v1 on v0

v1 whole, which is shorter than its diff:
```python
import functools
import jax
import jax.numpy as jnp
from jax import lax
from jax.experimental import pallas as pl
from jax.experimental.pallas import tpu as pltpu
from jax.sharding import PartitionSpec as P

LANES = 128
HALF = 64
QB = 128


def dot_nt(a, b):
    return lax.dot_general(a, b, (((1,), (1,)), ((), ())), preferred_element_type=jnp.float32)


def dot_nn(a, b):
    return lax.dot_general(a, b, (((1,), (0,)), ((), ())), preferred_element_type=jnp.float32)


def head_stack(block, scale=None):
    lane = lax.broadcasted_iota(jnp.int32, block.shape, 1)
    wide = block.astype(jnp.float32)
    if scale is not None:
        wide = wide * scale
    first = jnp.where(lane < HALF, wide, 0.0).astype(jnp.bfloat16)
    second = jnp.where(lane < HALF, 0.0, wide).astype(jnp.bfloat16)
    return jnp.concatenate([first, second], axis=0)


def twice(row):
    return jnp.concatenate([row, row], axis=1)


def diagonal(pair):
    return jnp.concatenate([pair[:HALF, :QB], pair[HALF:, QB:]], axis=0)


def query_places(block):
    return block * QB + lax.broadcasted_iota(jnp.int32, (1, QB), 1)


def cross_forward_kernel(pairs, starts, pages, q_ref, k_ref, v_ref, o_ref, l_ref, vt_ref):
    page_count = k_ref.shape[0]
    for page in range(page_count):
        image = pages[page]
        low, high = starts[page], starts[page + 1]
        for pair in range(pairs):
            lanes = slice(pair * LANES, (pair + 1) * LANES)
            vt_ref[pair] = flip(v_ref[image, :, lanes])

        def body(block, carry):
            rows = pl.ds(pl.multiple_of(block * QB, QB), QB)
            place = query_places(block)
            member = (place >= low) & (place < high)
            for pair in range(pairs):
                lanes = slice(pair * LANES, (pair + 1) * LANES)
                stacked = head_stack(q_ref[rows, lanes], 0.125)
                scores = dot_nt(k_ref[image, :, lanes], stacked)
                peak = jnp.max(scores, axis=0, keepdims=True)
                raised = jnp.exp(scores - peak)
                total = jnp.sum(raised, axis=0, keepdims=True)
                attention = (raised * (1.0 / total)).astype(jnp.bfloat16)
                mixed = diagonal(dot_nn(vt_ref[pair], attention)).astype(jnp.bfloat16)
                lse = peak + jnp.log(total)
                o_ref[lanes, rows] = jnp.where(member, mixed, o_ref[lanes, rows])
                l_ref[0, 2 * pair : 2 * pair + 1, rows] = jnp.where(
                    member, lse[:, :QB], l_ref[0, 2 * pair : 2 * pair + 1, rows]
                )
                l_ref[0, 2 * pair + 1 : 2 * pair + 2, rows] = jnp.where(
                    member, lse[:, QB:], l_ref[0, 2 * pair + 1 : 2 * pair + 2, rows]
                )
            return carry

        lax.fori_loop(low // QB, (high - 1) // QB + 1, body, 0)


def flip(block):
    return jnp.transpose(block)


def cross_backward_kernel(
    pairs, starts, pages, q_ref, k_ref, v_ref, g_ref, l_ref, dq_ref, dk_ref, dv_ref,
    kt_ref, dka_ref, dva_ref,
):
    page_count = k_ref.shape[0]
    for page in range(page_count):
        image = pages[page]
        low, high = starts[page], starts[page + 1]
        for pair in range(pairs):
            lanes = slice(pair * LANES, (pair + 1) * LANES)
            kt_ref[pair] = flip(k_ref[image, :, lanes])
            dka_ref[pair] = jnp.zeros(dka_ref.shape[1:], jnp.float32)
            dva_ref[pair] = jnp.zeros(dva_ref.shape[1:], jnp.float32)

        def body(block, carry):
            rows = pl.ds(pl.multiple_of(block * QB, QB), QB)
            place = query_places(block)
            member = (place >= low) & (place < high)
            for pair in range(pairs):
                lanes = slice(pair * LANES, (pair + 1) * LANES)
                stacked = head_stack(q_ref[rows, lanes], 0.125)
                pulled = head_stack(g_ref[rows, lanes])
                lse = jnp.concatenate(
                    [
                        jnp.where(member, l_ref[0, 2 * pair : 2 * pair + 1, rows], 1e30),
                        jnp.where(member, l_ref[0, 2 * pair + 1 : 2 * pair + 2, rows], 1e30),
                    ],
                    axis=1,
                )
                scores = dot_nt(k_ref[image, :, lanes], stacked)
                attention = jnp.exp(scores - lse)
                pushed = dot_nt(v_ref[image, :, lanes], pulled)
                dva_ref[pair] += dot_nn(attention.astype(jnp.bfloat16), pulled)
                inner = jnp.sum(attention * pushed, axis=0, keepdims=True)
                grad = (attention * (pushed - inner)).astype(jnp.bfloat16)
                dka_ref[pair] += dot_nn(grad, stacked)
                turned = diagonal(dot_nn(kt_ref[pair], grad) * 0.125).astype(jnp.bfloat16)
                dq_ref[lanes, rows] = jnp.where(member, turned, dq_ref[lanes, rows])
            return carry

        lax.fori_loop(low // QB, (high - 1) // QB + 1, body, 0)
        for pair in range(pairs):
            lanes = slice(pair * LANES, (pair + 1) * LANES)
            dk_ref[image, :, lanes] = dka_ref[pair].astype(jnp.bfloat16)
            dv_ref[image, :, lanes] = dva_ref[pair].astype(jnp.bfloat16)


def self_window(starts, block):
    start = starts[0]
    for page in range(1, starts.shape[0] - 1):
        start = jnp.where(starts[page] <= block * QB, starts[page], start)
    first = start // QB
    return first, block + 1 - first


def self_allowed(starts, place, first, chunks):
    begin = jnp.zeros(place.shape, jnp.int32)
    for page in range(1, starts.shape[0] - 1):
        begin = jnp.where(place >= starts[page], starts[page], begin)
    begin, end = twice(begin), twice(place)
    key = first * QB + lax.broadcasted_iota(jnp.int32, (chunks * QB, 2 * QB), 0)
    return (key >= begin) & (key <= end)


def self_forward_kernel(pairs, most, starts, q_ref, k_ref, v_ref, o_ref, l_ref, vt_ref):
    for pair in range(pairs):
        lanes = slice(pair * LANES, (pair + 1) * LANES)
        vt_ref[pair] = flip(v_ref[:, lanes])

    def body(block, carry):
        rows = pl.ds(pl.multiple_of(block * QB, QB), QB)
        first, count = self_window(starts, block)
        for chunks in range(1, most + 1):

            @pl.when(count == chunks)
            def _():
                keys = pl.ds(pl.multiple_of(first * QB, QB), chunks * QB)
                allowed = self_allowed(starts, query_places(block), first, chunks)
                for pair in range(pairs):
                    lanes = slice(pair * LANES, (pair + 1) * LANES)
                    stacked = head_stack(q_ref[rows, lanes], 0.125)
                    scores = jnp.where(allowed, dot_nt(k_ref[keys, lanes], stacked), -1e30)
                    peak = jnp.max(scores, axis=0, keepdims=True)
                    raised = jnp.exp(scores - peak)
                    total = jnp.sum(raised, axis=0, keepdims=True)
                    attention = (raised * (1.0 / total)).astype(jnp.bfloat16)
                    mixed = diagonal(dot_nn(vt_ref[pair, :, keys], attention))
                    lse = peak + jnp.log(total)
                    o_ref[lanes, rows] = mixed.astype(jnp.bfloat16)
                    l_ref[0, 2 * pair : 2 * pair + 1, rows] = lse[:, :QB]
                    l_ref[0, 2 * pair + 1 : 2 * pair + 2, rows] = lse[:, QB:]

        return carry

    lax.fori_loop(0, q_ref.shape[0] // QB, body, 0)


def self_backward_kernel(
    pairs, most, starts, q_ref, k_ref, v_ref, g_ref, l_ref, dq_ref, dk_ref, dv_ref,
    kt_ref, dka_ref, dva_ref,
):
    for pair in range(pairs):
        lanes = slice(pair * LANES, (pair + 1) * LANES)
        kt_ref[pair] = flip(k_ref[:, lanes])
    dka_ref[...] = jnp.zeros(dka_ref.shape, jnp.float32)
    dva_ref[...] = jnp.zeros(dva_ref.shape, jnp.float32)

    def body(block, carry):
        rows = pl.ds(pl.multiple_of(block * QB, QB), QB)
        first, count = self_window(starts, block)
        for chunks in range(1, most + 1):

            @pl.when(count == chunks)
            def _():
                keys = pl.ds(pl.multiple_of(first * QB, QB), chunks * QB)
                allowed = self_allowed(starts, query_places(block), first, chunks)
                for pair in range(pairs):
                    lanes = slice(pair * LANES, (pair + 1) * LANES)
                    stacked = head_stack(q_ref[rows, lanes], 0.125)
                    pulled = head_stack(g_ref[rows, lanes])
                    lse = jnp.concatenate(
                        [l_ref[0, 2 * pair : 2 * pair + 1, rows], l_ref[0, 2 * pair + 1 : 2 * pair + 2, rows]],
                        axis=1,
                    )
                    scores = jnp.where(allowed, dot_nt(k_ref[keys, lanes], stacked), -1e30)
                    attention = jnp.exp(scores - lse)
                    pushed = dot_nt(v_ref[keys, lanes], pulled)
                    dva_ref[pair, keys, :] += dot_nn(attention.astype(jnp.bfloat16), pulled)
                    inner = jnp.sum(attention * pushed, axis=0, keepdims=True)
                    grad = (attention * (pushed - inner)).astype(jnp.bfloat16)
                    dka_ref[pair, keys, :] += dot_nn(grad, stacked)
                    turned = diagonal(dot_nn(kt_ref[pair, :, keys], grad) * 0.125)
                    dq_ref[lanes, rows] = turned.astype(jnp.bfloat16)

        return carry

    lax.fori_loop(0, q_ref.shape[0] // QB, body, 0)
    for pair in range(pairs):
        lanes = slice(pair * LANES, (pair + 1) * LANES)
        dk_ref[:, lanes] = dka_ref[pair].astype(jnp.bfloat16)
        dv_ref[:, lanes] = dva_ref[pair].astype(jnp.bfloat16)


def cost(flops, bytes_accessed, exps):
    return pl.CostEstimate(flops=flops, bytes_accessed=bytes_accessed, transcendentals=exps)


def specs(pairs, prefetch):
    wide = pairs * LANES

    def at(index):
        return lambda step, *scalars: index(step)

    return {
        "rows": lambda length: pl.BlockSpec((length, wide), at(lambda i: (0, i))),
        "turned": lambda length: pl.BlockSpec((wide, length), at(lambda i: (i, 0))),
        "images": lambda count, tokens: pl.BlockSpec((count, tokens, wide), at(lambda i: (0, 0, i))),
        "stats": lambda length: pl.BlockSpec((1, 2 * pairs, length), at(lambda i: (i, 0, 0))),
    }


def cross_forward(starts, pages, queries, keys_all, values_all, pairs=2):
    length, width = queries.shape
    count, tokens, _ = keys_all.shape
    steps = width // (pairs * LANES)
    s = specs(pairs, 2)
    return pl.pallas_call(
        functools.partial(cross_forward_kernel, pairs),
        out_shape=(
            jax.ShapeDtypeStruct((width, length), jnp.bfloat16),
            jax.ShapeDtypeStruct((steps, 2 * pairs, length), jnp.float32),
        ),
        grid_spec=pltpu.PrefetchScalarGridSpec(
            num_scalar_prefetch=2,
            grid=(steps,),
            in_specs=[s["rows"](length), s["images"](count, tokens), s["images"](count, tokens)],
            out_specs=[s["turned"](length), s["stats"](length)],
            scratch_shapes=[pltpu.VMEM((pairs, LANES, tokens), jnp.bfloat16)],
        ),
        cost_estimate=cost(11 * 128 * tokens * width * 4 * 4, 20 * 2**20, 2**24),
        name="cross_forward",
    )(starts, pages, queries, keys_all, values_all)


def cross_backward(starts, pages, queries, keys_all, values_all, grads, stats, pairs=2):
    length, width = queries.shape
    count, tokens, _ = keys_all.shape
    steps = width // (pairs * LANES)
    s = specs(pairs, 2)
    image_spec = s["images"](count, tokens)
    return pl.pallas_call(
        functools.partial(cross_backward_kernel, pairs),
        out_shape=(
            jax.ShapeDtypeStruct((width, length), jnp.bfloat16),
            jax.ShapeDtypeStruct(keys_all.shape, jnp.bfloat16),
            jax.ShapeDtypeStruct(values_all.shape, jnp.bfloat16),
        ),
        grid_spec=pltpu.PrefetchScalarGridSpec(
            num_scalar_prefetch=2,
            grid=(steps,),
            in_specs=[s["rows"](length), image_spec, image_spec, s["rows"](length), s["stats"](length)],
            out_specs=[s["turned"](length), image_spec, image_spec],
            scratch_shapes=[
                pltpu.VMEM((pairs, LANES, tokens), jnp.bfloat16),
                pltpu.VMEM((pairs, tokens, LANES), jnp.float32),
                pltpu.VMEM((pairs, tokens, LANES), jnp.float32),
            ],
        ),
        cost_estimate=cost(11 * 128 * tokens * width * 10 * 4, 30 * 2**20, 2**24),
        name="cross_backward",
    )(starts, pages, queries, keys_all, values_all, grads, stats)


def self_forward(starts, queries, keys_all, values_all, most, pairs=2):
    length, width = queries.shape
    steps = width // (pairs * LANES)
    s = specs(pairs, 1)
    rows = s["rows"](length)
    return pl.pallas_call(
        functools.partial(self_forward_kernel, pairs, most),
        out_shape=(
            jax.ShapeDtypeStruct((width, length), jnp.bfloat16),
            jax.ShapeDtypeStruct((steps, 2 * pairs, length), jnp.float32),
        ),
        grid_spec=pltpu.PrefetchScalarGridSpec(
            num_scalar_prefetch=1,
            grid=(steps,),
            in_specs=[rows, rows, rows],
            out_specs=[s["turned"](length), s["stats"](length)],
            scratch_shapes=[pltpu.VMEM((pairs, LANES, length), jnp.bfloat16)],
        ),
        cost_estimate=cost(20 * 128 * 128 * width * 4 * 4, 10 * 2**20, 2**23),
        name="self_forward",
    )(starts, queries, keys_all, values_all)


def self_backward(starts, queries, keys_all, values_all, grads, stats, most, pairs=2):
    length, width = queries.shape
    steps = width // (pairs * LANES)
    s = specs(pairs, 1)
    rows = s["rows"](length)
    return pl.pallas_call(
        functools.partial(self_backward_kernel, pairs, most),
        out_shape=(
            jax.ShapeDtypeStruct((width, length), jnp.bfloat16),
            jax.ShapeDtypeStruct((length, width), jnp.bfloat16),
            jax.ShapeDtypeStruct((length, width), jnp.bfloat16),
        ),
        grid_spec=pltpu.PrefetchScalarGridSpec(
            num_scalar_prefetch=1,
            grid=(steps,),
            in_specs=[rows, rows, rows, rows, s["stats"](length)],
            out_specs=[s["turned"](length), rows, rows],
            scratch_shapes=[
                pltpu.VMEM((pairs, LANES, length), jnp.bfloat16),
                pltpu.VMEM((pairs, length, LANES), jnp.float32),
                pltpu.VMEM((pairs, length, LANES), jnp.float32),
            ],
        ),
        cost_estimate=cost(20 * 128 * 128 * width * 10 * 4, 16 * 2**20, 2**23),
        name="self_backward",
    )(starts, queries, keys_all, values_all, grads, stats)


EPSILON = 1e-05
ROOT_HALF = 0.7071067811865476
ROOT_TAU = 0.3989422804014327
AXES = ("dp", "fsdp")
LONGEST = 512


def contract(a, b, left, right, out=jnp.float32):
    return lax.dot_general(
        a, b, ((left, right), ((), ())), preferred_element_type=jnp.float32
    ).astype(out)


def normalise(values):
    average = jnp.mean(values, axis=-1, keepdims=True)
    centered = values - average
    variance = jnp.mean(centered * centered, axis=-1, keepdims=True)
    scale = lax.rsqrt(variance + EPSILON)
    return centered * scale, scale


def norm_back(values, gain, grads):
    hat, scale = normalise(values)
    pulled = grads * gain
    first = jnp.mean(pulled, axis=-1, keepdims=True)
    second = jnp.mean(pulled * hat, axis=-1, keepdims=True)
    back = scale * (pulled - first - hat * second)
    return back, jnp.sum(grads * hat, axis=0), jnp.sum(grads, axis=0)


def swap(value, axis, size, bit):
    return lax.ppermute(value, axis, [(i, i ^ bit) for i in range(size)])


def butterfly_sum(value, sizes):
    for axis, size in sizes:
        bit = 1
        while bit < size:
            value = value + swap(value, axis, size, bit)
            bit *= 2
    return value


def pick(value, index, axis):
    return lax.dynamic_index_in_dim(value, index, axis, keepdims=False)


def reduce_rows(grads, sizes):
    dp_size, inner = sizes
    place = lax.axis_index("dp")
    low, high = place % 2, place // 2
    count = len(grads)
    rows, columns = grads[0].shape
    own = rows // (dp_size * inner)
    sends = [g.reshape(dp_size // 2, 2, inner * own, columns) for g in grads]
    keeps = [pick(g, low, 1) for g in sends]
    sends = [pick(g, 1 - low, 1) for g in sends]
    got = [swap(s, "dp", dp_size, 1) for s in sends]

    def half(index):
        return [
            (pick(k, index, 0).astype(jnp.float32) + pick(r, index, 0).astype(jnp.float32))
            for k, r in zip(keeps, got)
        ]

    out = [s.astype(jnp.bfloat16) for s in half(1 - high)]
    mine = half(high)
    came = [swap(s, "dp", dp_size, 2) for s in out]
    both = [(m + c.astype(jnp.float32)).astype(jnp.bfloat16) for m, c in zip(mine, came)]
    packed = jnp.stack([b.reshape(inner, own, columns) for b in both], axis=1)
    packed = packed.reshape(inner * count * own, columns)
    summed = lax.psum_scatter(packed, "fsdp", scatter_dimension=0, tiled=True)
    summed = summed.reshape(count, own, columns).astype(jnp.float32)
    return [summed[i] for i in range(count)]


def layer(
    sizes, block_in, images, segment_ids, page_map, ln1_gain, ln1_shift, ln2_gain, ln2_shift,
    ln3_gain, ln3_shift, self_query, self_key, self_value, self_out, cross_query, cross_key,
    cross_value, cross_out, mlp_in, mlp_out, cotangent,
):
    dp_size, inner = sizes
    axes = (("dp", dp_size), ("fsdp", inner))
    _, length, width = block_in.shape
    low = jnp.bfloat16

    def turned(master):
        return master.astype(low).T

    def gather(*masters):
        stacked = jnp.stack([turned(m) for m in masters])
        return lax.all_gather(stacked, AXES, axis=1, tiled=True)

    norms = jnp.stack([ln1_gain, ln1_shift, ln2_gain, ln2_shift, ln3_gain, ln3_shift])
    norms = norms.astype(low).astype(jnp.float32)
    mine = norms.shape[1]
    offset = (lax.axis_index("dp") * inner + lax.axis_index("fsdp")) * mine
    spread = lax.dynamic_update_slice(jnp.zeros((6, width), jnp.float32), norms, (0, offset))
    norms = butterfly_sum(spread, axes)
    w_sqkv = gather(self_query, self_key, self_value)
    w_rest = gather(self_out, cross_query, cross_key, cross_value, cross_out)
    w_in = lax.all_gather(turned(mlp_in), AXES, axis=0, tiled=True)
    w_out = lax.all_gather(turned(mlp_out), AXES, axis=0, tiled=True)
    w_so, w_cq, w_ck, w_cv, w_co = [w_rest[i] for i in range(5)]

    starts = jnp.sum(
        segment_ids[0][None, :] < jnp.arange(page_map.shape[1] + 1, dtype=jnp.int32)[:, None],
        axis=1,
    ).astype(jnp.int32)
    pages = page_map[0]
    most = LONGEST // QB + 1

    rows = block_in[0].astype(jnp.float32)
    a1 = (normalise(rows)[0] * norms[0] + norms[1]).astype(low)
    sq, sk, sv = [contract(a1, w_sqkv[i], (1,), (1,), low) for i in range(3)]
    so, s_stats = self_forward(starts, sq, sk, sv, most)
    x1 = rows + contract(so, w_so, (0,), (1,))
    a2 = (normalise(x1)[0] * norms[2] + norms[3]).astype(low)
    cq = contract(a2, w_cq, (1,), (1,), low)
    ck = contract(images, w_ck, (2,), (1,), low)
    cv = contract(images, w_cv, (2,), (1,), low)
    co, c_stats = cross_forward(starts, pages, cq, ck, cv)
    x2 = x1 + contract(co, w_co, (0,), (1,))
    a3 = (normalise(x2)[0] * norms[4] + norms[5]).astype(low)
    u = contract(a3, w_in, (1,), (1,))
    phi = 0.5 * (1.0 + lax.erf(u * ROOT_HALF))
    hidden = (u * phi).astype(low)
    slope = (phi + u * (ROOT_TAU * jnp.exp(-0.5 * u * u))).astype(low)
    block_out = (x2 + contract(hidden, w_out, (1,), (1,))).astype(low)

    eb = cotangent[0]
    e = eb.astype(jnp.float32)
    du = (contract(eb, w_out, (1,), (0,)) * slope.astype(jnp.float32)).astype(low)
    g_out = contract(eb, hidden, (0,), (0,), low)
    g_in = contract(du, a3, (0,), (0,), low)
    d3 = contract(du, w_in, (1,), (0,))
    (g_mlp_out,) = reduce_rows([g_out], sizes)
    (g_mlp_in,) = reduce_rows([g_in], sizes)
    back, gg3, gs3 = norm_back(x2, norms[4], d3)
    e2 = e + back
    e2b = e2.astype(low)
    g_co = contract(e2b, co, (0,), (1,), low)
    d_co = contract(e2b, w_co, (1,), (0,), low)
    dcq, dck, dcv = cross_backward(starts, pages, cq, ck, cv, d_co, c_stats)
    g_cq = contract(dcq, a2, (1,), (0,), low)
    g_ck = contract(dck, images, (0, 1), (0, 1), low)
    g_cv = contract(dcv, images, (0, 1), (0, 1), low)
    g_cross = reduce_rows([g_cq, g_ck, g_cv, g_co], sizes)
    grad_images = contract(dck, w_ck, (2,), (0,)) + contract(dcv, w_cv, (2,), (0,))
    d2 = contract(dcq, w_cq, (0,), (0,))
    back, gg2, gs2 = norm_back(x1, norms[2], d2)
    e1 = e2 + back
    e1b = e1.astype(low)
    g_so = contract(e1b, so, (0,), (1,), low)
    d_so = contract(e1b, w_so, (1,), (0,), low)
    dsq, dsk, dsv = self_backward(starts, sq, sk, sv, d_so, s_stats, most)
    g_sq = contract(dsq, a1, (1,), (0,), low)
    g_sk = contract(dsk, a1, (0,), (0,), low)
    g_sv = contract(dsv, a1, (0,), (0,), low)
    g_self = reduce_rows([g_sq, g_sk, g_sv, g_so], sizes)
    d1 = (
        contract(dsq, w_sqkv[0], (0,), (0,))
        + contract(dsk, w_sqkv[1], (1,), (0,))
        + contract(dsv, w_sqkv[2], (1,), (0,))
    )
    back, gg1, gs1 = norm_back(rows, norms[0], d1)
    grad_in = e1 + back
    norm_grads = butterfly_sum(jnp.stack([gg1, gs1, gg2, gs2, gg3, gs3]), axes)
    norm_grads = lax.dynamic_slice(norm_grads, (0, offset), (6, mine))
    weight_grads = [g.T for g in g_self + g_cross + [g_mlp_in, g_mlp_out]]
    return (
        block_out[None], grad_in[None], grad_images, *[norm_grads[i] for i in range(6)],
        *weight_grads,
    )


def solution(mesh):
    sizes = (mesh.shape["dp"], mesh.shape["fsdp"])
    rows3 = P(AXES, None, None)
    rows2 = P(AXES, None)
    vector = P(AXES)
    columns = P(None, AXES)
    return jax.shard_map(
        functools.partial(layer, sizes),
        mesh=mesh,
        in_specs=(rows3, rows3, rows2, rows2) + (vector,) * 6 + (columns,) * 10 + (rows3,),
        out_specs=(rows3,) * 3 + (vector,) * 6 + (columns,) * 10,
        check_vma=False,
    )
```

time: 2700 us -> 944 us (0.35)
  waiting for transfers between devices: 1330 us -> 296 us
  matrix products: 855 us -> 235 us
  other arithmetic: 309 us -> 76.5 us
  Pallas kernels: 0 us -> 179 us
  blocking collectives: 82.5 us -> 0 us
  starting transfers between devices: 1.22 us -> 41.4 us
    reduce_scatter x10 -> x3, waiting for transfers between devices: 1150 us -> 24.2 us  [reduce_rows(): summed = lax.psum_scatter(packed, 'fsdp', scatter_dimension=0, tiled=True)]
    dot_general x54 -> x30, matrix products: 855 us -> 235 us  [contract(): lax.dot_general(a, b, ((left, right), ((), ())), preferred_element_type=j...]
    pallas_call x0 -> x4, Pallas kernels: none -> 179 us  [the longest x1 56.4 us: cross_backward(): pl.pallas_call(functools.partial(cross_backward_kernel, pairs), out_shape...]
    convert_element_type x27 -> x23, other arithmetic: 197 us -> 38.7 us  [the longest x10 19.1 us: reduce_rows(): (m + c.astype(jnp.float32)).astype(jnp.bfloat16)]
    ppermute x0 -> x30, waiting for transfers between devices: none -> 130 us  [swap(): return lax.ppermute(value, axis, [(i, i ^ bit) for i in range(size)])]
    reduce_sum x14 -> x7, other arithmetic: 98.9 us -> 13 us  [the longest x2 10.4 us: norm_back(): return (back, jnp.sum(grads * hat, axis=0), jnp.sum(grads, axis=0))]
    unnamed x2 -> x0, blocking collectives: 82.5 us -> none
    ppermute x0 -> x30, starting transfers between devices: none -> 41 us  [swap(): return lax.ppermute(value, axis, [(i, i ^ bit) for i in range(size)])]
  transfers between devices with their start and end apart: 20 -> 38, of which waited for: 10 -> 20; matrix products, arithmetic and copies ran while one was open for 44% -> 37% of each run, Pallas kernels for 0% -> 19%
where the time goes in v1:
time: 944 us; the launch traced here: 933 us
  waiting for transfers between devices  296 us (31%)
  matrix products  235 us (25%)
  Pallas kernels  179 us (19%)
  local copies, waits for them, and re-layouts  88.7 us (9%)
  other arithmetic  76.5 us (8%)
  starting transfers between devices  41.4 us (4%)
  between operations  15.8 us (2%)
    dot_general x30, matrix products, contract(): lax.dot_general(a, b, ((left, right), ((), ())), preferred_element_type=j...  235 us
    ppermute x30, waiting for transfers between devices, swap(): return lax.ppermute(value, axis, [(i, i ^ bit) for i in range(size)])  130 us
    all_gather x2, waiting for transfers between devices, gather(): return lax.all_gather(stacked, AXES, axis=1, tiled=True)  81.2 us
    all_gather x1, waiting for transfers between devices, layer(): w_out = lax.all_gather(turned(mlp_out), AXES, axis=0, tiled=True)  57.8 us
    pallas_call x1, Pallas kernels, cross_backward(): pl.pallas_call(functools.partial(cross_backward_kernel, pairs), out_shape...  56.4 us
    pallas_call x1, Pallas kernels, cross_forward(): pl.pallas_call(functools.partial(cross_forward_kernel, pairs), out_shape=...  55.7 us
    unnamed x165, local copies, waits for them, and re-layouts  52 us
    ppermute x30, starting transfers between devices, swap(): return lax.ppermute(value, axis, [(i, i ^ bit) for i in range(size)])  41 us
  transfers between devices with their start and end apart: 38, of which 20 were waited for; matrix products, arithmetic and copies ran while one was open for 37% of the time, Pallas kernels for 19%

profile of v1, /device:TPU:0, one launch (start us, length us, event | category | flops | bytes accessed | tf_op | source)
XLA Modules:
  0.0 932.9 jit_solution(3428847963206843479)
XLA Ops:
  43.8 40.0 %all-gather.5.cloned.1.call-done = bf16[3,1024,1024]{2,1,0:T(8,128)(2,1)} async-done(((bf16[3,32,1024]{2,1,0:T(8,128)(2,1)}), bf16[3,1024,1024]{2,1,0:T(8,128)(2,1)}) %all-gather.5.cloned.1.call-update) | async-done | bytes 6291472 | tf_op jit(solution)/shard_map/all_gather | solution.py:438
  97.7 33.5 %self_forward.1 = (bf16[1024,1024]{1,0:T(8,128)(2,1)}, f32[4,4,1024]{2,1,0:T(4,128)}) custom-call(s32[5]{0:T(128)} %convert_reduce_fusion.1.starts, bf16[1024,1024]{1,0:T(8,128)(2,1)} %convolution_convert_fusion.13.q_ref, bf16[1024,1024]{1,0:T(8,128)(2,1)} %convolution_convert_fusion.12.k_ref, bf16[1024,1024]{1,0:T(8,128)(2,1)} %convolution_convert_fusion.11.v_ref), custom_call_target="tpu_custom_call" | custom-call | flops 5368709120 | bytes 10485760 | tf_op jit(solution)/shard_map/self_forward/pallas_call | solution.py:301
  131.2 41.1 %all-gather.7.cloned.1.call-done = bf16[5,1024,1024]{2,1,0:T(8,128)(2,1)} async-done(((bf16[5,32,1024]{2,1,0:T(8,128)(2,1)}), bf16[5,1024,1024]{2,1,0:T(8,128)(2,1)}) %all-gather.7.cloned.1.call-update) | async-done | bytes 10485776 | tf_op jit(solution)/shard_map/all_gather | solution.py:438
  198.9 55.7 %cross_forward.1 = (bf16[1024,1024]{1,0:T(8,128)(2,1)}, f32[4,4,1024]{2,1,0:T(4,128)}) custom-call(s32[5]{0:T(128)} %convert_reduce_fusion.1.starts, s32[4]{0:T(128)} %bitcast.479, bf16[1024,1024]{1,0:T(8,128)(2,1)} %convolution_convert_fusion.10.q_ref, bf16[4,588,1024]{2,1,0:T(8,128)(2,1)} %convert_bitcast_fusion.2.k_ref, ...), custom_call_target="tpu_custom_call" | custom-call | flops 13564379136 | bytes 20971520 | tf_op jit(solution)/shard_map/cross_forward/pallas_call | solution.py:249
  266.2 20.3 %multiply_convert_fusion.1 = (bf16[1024,4096]{1,0:T(8,128)(2,1)}, f32[1024,4096]{1,0:T(8,128)}) fusion(bf16[4096,1024]{0,1:T(8,128)(2,1)} %all-gather.9.cloned.1.call-done, f32[1024,1024]{0,1:T(8,128)} %copy-done, f32[1024]{0:T(1024)S(1)} %bitcast.472, f32[1024]{0:T(1024)S(1)} %bitcast.442, f32[1024]{0:T(1024)S(1)} %add_rsqrt_fusion, ...), kind=kOutput, calls=%fused_computation.7 | convolution fusion | flops 8616148992 | bytes 37765120 | tf_op jit(solution)/shard_map/dot_general | solution.py:355
  286.5 57.8 %all-gather.11.cloned.1.call-done = bf16[1024,4096]{1,0:T(8,128)(2,1)} async-done(((bf16[32,4096]{1,0:T(8,128)(2,1)}), bf16[1024,4096]{1,0:T(8,128)(2,1)}) %all-gather.11.cloned.1.call-update) | async-done | bytes 8388624 | tf_op jit(solution)/shard_map/all_gather | solution.py:449
  344.3 17.8 %multiply_convert_fusion = bf16[1024,4096]{1,0:T(8,128)(2,1)} fusion(bf16[1024,4096]{1,0:T(8,128)(2,1)} %all-gather.11.cloned.1.call-done, f32[1024,4096]{1,0:T(8,128)} %get-tuple-element.133, bf16[1,1024,1024]{2,1,0:T(8,128)(2,1)S(1)} %copy-done.32), kind=kOutput, calls=%fused_computation.6 | convolution fusion | flops 8640266240 | bytes 35651584 | tf_op jit(solution)/shard_map/dot_general | solution.py:355
  362.1 12.8 %convolution_convert_fusion.1 = bf16[4096,1024]{1,0:T(8,128)(2,1)S(1)} fusion(bf16[1024,4096]{1,0:T(8,128)(2,1)} %multiply_convert_fusion, f32[1024,1024]{0,1:T(8,128)S(1)} %copy-done.1, f32[1024]{0:T(1024)S(1)} %bitcast.473, f32[1024]{0:T(1024)S(1)} %bitcast.443, f32[1024]{0:T(1024)S(1)} %add_rsqrt_fusion, f32[1024]{0:T(1024)S(1)} %broadcast_multiply_fusion.6), kind=kOutput, calls=%fused_computation.10 | convolution fusion | flops 8599371776 | bytes 20987904 | tf_op jit(solution)/shard_map/dot_general | solution.py:355
  387.0 15.7 %fusion.97 = (f32[1024]{0:T(1024)}, f32[1024,1024]{1,0:T(8,128)}) fusion(bf16[1024,4096]{1,0:T(8,128)(2,1)} %multiply_convert_fusion, bf16[4096,1024]{0,1:T(8,128)(2,1)} %all-gather.9.cloned.1.call-done), kind=kOutput, calls=%fused_computation.219 | convolution fusion | flops 8590982144 | bytes 20975616 | tf_op jit(solution)/shard_map/dot_general | solution.py:355
  424.2 56.4 %cross_backward.1 = (bf16[1024,1024]{1,0:T(8,128)(2,1)}, bf16[4,588,1024]{2,1,0:T(8,128)(2,1)}, bf16[4,588,1024]{2,1,0:T(8,128)(2,1)}) custom-call(s32[5]{0:T(128)} %convert_reduce_fusion.1.starts, s32[4]{0:T(128)} %bitcast.480, bf16[1024,1024]{1,0:T(8,128)(2,1)} %convolution_convert_fusion.10.q_ref, bf16[4,588,1024]{2,1,0:T(8,128)(2,1)} %convert_bitcast_fusion.2.k_ref, ...), custom_call_target="tpu_custom_call" | custom-call | flops 33910947840 | bytes 31457280 | tf_op jit(solution)/shard_map/cross_backward/pallas_call | solution.py:273
  491.3 8.0 bitcast_convert_fusion.1
  540.9 33.5 %self_backward.1 = (bf16[1024,1024]{1,0:T(8,128)(2,1)}, bf16[1024,1024]{1,0:T(8,128)(2,1)}, bf16[1024,1024]{1,0:T(8,128)(2,1)}) custom-call(s32[5]{0:T(128)} %convert_reduce_fusion.1.starts, bf16[1024,1024]{1,0:T(8,128)(2,1)} %convolution_convert_fusion.13.q_ref, bf16[1024,1024]{1,0:T(8,128)(2,1)} %convolution_convert_fusion.12.k_ref, ...), custom_call_target="tpu_custom_call" | custom-call | flops 13421772800 | bytes 16777216 | tf_op jit(solution)/shard_map/self_backward/pallas_call | solution.py:324
  629.3 9.9 %collective-permute-done.25 = bf16[256,1024]{1,0:T(8,128)(2,1)S(1)} collective-permute-done((bf16[256,1024]{1,0:T(8,128)(2,1)S(1)}, bf16[256,1024]{1,0:T(8,128)(2,1)S(1)}, u32[]{:S(2)}, u32[]{:S(2)}) %collective-permute-start.25) | collective-permute-done | bytes 524320 | tf_op jit(solution)/shard_map/ppermute | solution.py:378
  646.5 11.5 %convolution_convert_fusion = bf16[4096,1024]{0,1:T(8,128)(2,1)S(1)} fusion(bf16[1024,4096]{1,0:T(8,128)(2,1)} %get-tuple-element.132, bf16[1,1024,1024]{2,1,0:T(8,128)(2,1)S(1)} %copy-done.33), kind=kOutput, calls=%fused_computation.9 | convolution fusion | flops 8594128896 | bytes 18874368 | tf_op jit(solution)/shard_map/dot_general | solution.py:355
  675.9 9.9 %collective-permute-done.13 = bf16[256,1024]{1,0:T(8,128)(2,1)S(1)} collective-permute-done((bf16[256,1024]{1,0:T(8,128)(2,1)S(1)}, bf16[256,1024]{1,0:T(8,128)(2,1)S(1)}, u32[]{:S(2)}, u32[]{:S(2)}) %collective-permute-start.13) | collective-permute-done | bytes 524320 | tf_op jit(solution)/shard_map/ppermute | solution.py:378
  687.2 9.9 %collective-permute-done.15 = bf16[256,1024]{1,0:T(8,128)(2,1)S(1)} collective-permute-done((bf16[256,1024]{1,0:T(8,128)(2,1)S(1)}, bf16[256,1024]{1,0:T(8,128)(2,1)S(1)}, u32[]{:S(2)}, u32[]{:S(2)}) %collective-permute-start.15) | collective-permute-done | bytes 524320 | tf_op jit(solution)/shard_map/ppermute | solution.py:378
  697.4 10.7 %collective-permute-done.17 = bf16[256,1024]{1,0:T(8,128)(2,1)S(1)} collective-permute-done((bf16[256,1024]{1,0:T(8,128)(2,1)S(1)}, bf16[256,1024]{1,0:T(8,128)(2,1)S(1)}, u32[]{:S(2)}, u32[]{:S(2)}) %collective-permute-start.17) | collective-permute-done | bytes 524320 | tf_op jit(solution)/shard_map/ppermute | solution.py:378
  742.4 29.6 %collective-permute-done.27 = bf16[1024,1024]{0,1:T(8,128)(2,1)} collective-permute-done((bf16[1024,1024]{0,1:T(8,128)(2,1)}, bf16[1024,1024]{0,1:T(8,128)(2,1)}, u32[]{:S(2)}, u32[]{:S(2)}) %collective-permute-start.27) | collective-permute-done | bytes 2097184 | tf_op jit(solution)/shard_map/ppermute | solution.py:378
  787.4 8.0 fusion.18
  795.5 15.4 %fusion.44 = bf16[1,1024,1024]{1,2,0:T(8,128)(2,1)} fusion(f32[1024,1024]{0,1:T(8,128)} %copy-done, bf16[1024,4096]{1,0:T(8,128)(2,1)} %get-tuple-element.132, bf16[1024,4096]{1,0:T(8,128)(2,1)} %all-gather.11.cloned.1.call-done), kind=kOutput, calls=%fused_computation.76 | convolution fusion | flops 8592031744 | bytes 23068672 | tf_op jit(solution)/shard_map/dot_general | solution.py:355
  810.9 22.2 %collective-permute-done.29 = bf16[256,4096]{1,0:T(8,128)(2,1)} collective-permute-done((bf16[256,4096]{1,0:T(8,128)(2,1)}, bf16[256,4096]{1,0:T(8,128)(2,1)}, u32[]{:S(2)}, u32[]{:S(2)}) %collective-permute-start.29) | collective-permute-done | bytes 2097184 | tf_op jit(solution)/shard_map/ppermute | solution.py:378
  848.0 11.3 %convolution_add_fusion = f32[4,588,1024]{2,1,0:T(8,128)} fusion(f32[4,588,1024]{2,1,0:T(8,128)S(1)} %fusion.55, bf16[4,588,1024]{2,1,0:T(8,128)(2,1)} %get-tuple-element.38, bf16[5,1024,1024]{2,1,0:T(8,128)(2,1)} %all-gather.7.cloned.1.call-done), kind=kOutput, calls=%fused_computation.75 | convolution fusion | flops 4934909952 | bytes 26214400 | tf_op jit(solution)/shard_map/dot_general | solution.py:355
  871.5 13.8 %copy.123 = f32[4,588,1024]{2,0,1:T(4,128)} copy(f32[4,588,1024]{2,1,0:T(8,128)} %convolution_add_fusion) | data formatting | bytes 19267584
  899.6 24.2 %reduce-scatter.11.cloned.1.call-done = bf16[32,4096]{1,0:T(8,128)(2,1)} async-done(((bf16[256,4096]{1,0:T(8,128)(2,1)}), bf16[32,4096]{1,0:T(8,128)(2,1)}) %reduce-scatter.11.cloned.1.call-update) | async-done | bytes 262160 | tf_op jit(solution)/shard_map/reduce_scatter | solution.py:418
  (357 shorter events, 348.1 us)
Async XLA Ops:
  7.3 76.6 %all-gather.5.cloned.1.call-start = ((), (), s32[]{:S(2)}) async-start(), calls=%async_computation.4 | async-start | bytes 6488064 | tf_op jit(solution)/shard_map/all_gather | solution.py:438
  9.9 162.4 %all-gather.7.cloned.1.call-start = ((), (), s32[]{:S(2)}) async-start(), calls=%async_computation.5 | async-start | bytes 10813440 | tf_op jit(solution)/shard_map/all_gather | solution.py:438
  15.3 250.9 %all-gather.9.cloned.1.call-start = ((), (), s32[]{:S(2)}) async-start(), calls=%async_computation.6 | async-start | bytes 8650752 | tf_op jit(solution)/shard_map/all_gather | solution.py:448
  17.1 327.2 %all-gather.11.cloned.1.call-start = ((), (), s32[]{:S(2)}) async-start(), calls=%async_computation.7 | async-start | bytes 8650752 | tf_op jit(solution)/shard_map/all_gather | solution.py:449
  19.0 875.0 %reduce-scatter.9.cloned.1.call-start = ((), (), s32[]{:S(2)}) async-start(), calls=%async_computation.9 | async-start | bytes 2359296 | tf_op jit(solution)/shard_map/reduce_scatter | solution.py:418
  386.7 332.2 %collective-permute-start.26 = (bf16[2,1024,1024]{1,2,0:T(8,128)(2,1)}, bf16[2,1024,1024]{1,2,0:T(8,128)(2,1)}, u32[]{:S(2)}, u32[]{:S(2)}) collective-permute-start(bf16[2,1024,1024]{1,2,0:T(8,128)(2,1)} %bitcast.409), channel_id=1, source_target_pairs={{0,8},{8,0},{16,24},{24,16},{1,9},{9,1},{17,25},{25,17},{2,10},{10... | collective-permute-start | bytes 12582920 | tf_op jit(solution)/shard_map/ppermute | solution.py:378
  486.2 103.2 %collective-permute-start.18 = (bf16[2,256,1024]{2,1,0:T(8,128)(2,1)S(1)}, bf16[2,256,1024]{2,1,0:T(8,128)(2,1)}, u32[]{:S(2)}, u32[]{:S(2)}) collective-permute-start(bf16[2,256,1024]{2,1,0:T(8,128)(2,1)S(1)} %dynamic-slice_bitcast_fusion.4), channel_id=1, source_target_pairs={{0,8},{8,0},{16,24},{24,16},{1,9},{9,1},{17,25},{25,17},{2,10},{10... | collective-permute-start | bytes 3145736 | tf_op jit(solution)/shard_map/ppermute | solution.py:378
  500.4 93.5 %collective-permute-start.20 = (bf16[2,256,1024]{2,1,0:T(8,128)(2,1)}, bf16[2,256,1024]{2,1,0:T(8,128)(2,1)}, u32[]{:S(2)}, u32[]{:S(2)}) collective-permute-start(bf16[2,256,1024]{2,1,0:T(8,128)(2,1)} %dynamic-slice_bitcast_fusion.3), channel_id=1, source_target_pairs={{0,8},{8,0},{16,24},{24,16},{1,9},{9,1},{17,25},{25,17},{2,10},{10... | collective-permute-start | bytes 3145736 | tf_op jit(solution)/shard_map/ppermute | solution.py:378
  511.3 85.1 %collective-permute-start.22 = (bf16[2,256,1024]{2,1,0:T(8,128)(2,1)}, bf16[2,256,1024]{2,1,0:T(8,128)(2,1)}, u32[]{:S(2)}, u32[]{:S(2)}) collective-permute-start(bf16[2,256,1024]{2,1,0:T(8,128)(2,1)} %dynamic-slice_bitcast_fusion.2), channel_id=1, source_target_pairs={{0,8},{8,0},{16,24},{24,16},{1,9},{9,1},{17,25},{25,17},{2,10},{10... | collective-permute-start | bytes 3145736 | tf_op jit(solution)/shard_map/ppermute | solution.py:378
  512.8 86.4 %collective-permute-start.24 = (bf16[2,256,1024]{2,1,0:T(8,128)(2,1)}, bf16[2,256,1024]{2,1,0:T(8,128)(2,1)}, u32[]{:S(2)}, u32[]{:S(2)}) collective-permute-start(bf16[2,256,1024]{2,1,0:T(8,128)(2,1)} %dynamic-slice_bitcast_fusion.1), channel_id=1, source_target_pairs={{0,8},{8,0},{16,24},{24,16},{1,9},{9,1},{17,25},{25,17},{2,10},{10... | collective-permute-start | bytes 3145736 | tf_op jit(solution)/shard_map/ppermute | solution.py:378
  596.3 61.7 %collective-permute-start.10 = (bf16[2,256,1024]{2,1,0:T(8,128)(2,1)S(1)}, bf16[2,256,1024]{2,1,0:T(8,128)(2,1)}, u32[]{:S(2)}, u32[]{:S(2)}) collective-permute-start(bf16[2,256,1024]{2,1,0:T(8,128)(2,1)S(1)} %dynamic-slice_bitcast_fusion.8), channel_id=1, source_target_pairs={{0,8},{8,0},{16,24},{24,16},{1,9},{9,1},{17,25},{25,17},{2,10},{10... | collective-permute-start | bytes 3145736 | tf_op jit(solution)/shard_map/ppermute | solution.py:378
  599.2 28.8 %collective-permute-start.23 = (bf16[256,1024]{1,0:T(8,128)(2,1)S(1)}, bf16[256,1024]{1,0:T(8,128)(2,1)S(1)}, u32[]{:S(2)}, u32[]{:S(2)}) collective-permute-start(bf16[256,1024]{1,0:T(8,128)(2,1)S(1)} %fusion.59), channel_id=1, source_target_pairs={{0,16},{8,24},{16,0},{24,8},{1,17},{9,25},{17,1},{25,9},{2,18},{10... | collective-permute-start | bytes 1572872 | tf_op jit(solution)/shard_map/ppermute | solution.py:378
  605.5 33.7 %collective-permute-start.25 = (bf16[256,1024]{1,0:T(8,128)(2,1)S(1)}, bf16[256,1024]{1,0:T(8,128)(2,1)S(1)}, u32[]{:S(2)}, u32[]{:S(2)}) collective-permute-start(bf16[256,1024]{1,0:T(8,128)(2,1)S(1)} %fusion.56), channel_id=1, source_target_pairs={{0,16},{8,24},{16,0},{24,8},{1,17},{9,25},{17,1},{25,9},{2,18},{10... | collective-permute-start | bytes 1572872 | tf_op jit(solution)/shard_map/ppermute | solution.py:378
  616.8 45.1 %collective-permute-start.12 = (bf16[2,256,1024]{2,1,0:T(8,128)(2,1)}, bf16[2,256,1024]{2,1,0:T(8,128)(2,1)}, u32[]{:S(2)}, u32[]{:S(2)}) collective-permute-start(bf16[2,256,1024]{2,1,0:T(8,128)(2,1)} %dynamic-slice_bitcast_fusion.7), channel_id=1, source_target_pairs={{0,8},{8,0},{16,24},{24,16},{1,9},{9,1},{17,25},{25,17},{2,10},{10... | collective-permute-start | bytes 3145736 | tf_op jit(solution)/shard_map/ppermute | solution.py:378
  642.6 252.4 %reduce-scatter.7.cloned.1.call-start = ((), (), s32[]{:S(2)}) async-start(), calls=%async_computation.8 | async-start | bytes 2359296 | tf_op jit(solution)/shard_map/reduce_scatter | solution.py:418
  666.5 30.6 %collective-permute-start.15 = (bf16[256,1024]{1,0:T(8,128)(2,1)S(1)}, bf16[256,1024]{1,0:T(8,128)(2,1)S(1)}, u32[]{:S(2)}, u32[]{:S(2)}) collective-permute-start(bf16[256,1024]{1,0:T(8,128)(2,1)S(1)} %fusion.71), channel_id=1, source_target_pairs={{0,16},{8,24},{16,0},{24,8},{1,17},{9,25},{17,1},{25,9},{2,18},{10... | collective-permute-start | bytes 1572872 | tf_op jit(solution)/shard_map/ppermute | solution.py:378
  668.3 39.8 %collective-permute-start.17 = (bf16[256,1024]{1,0:T(8,128)(2,1)S(1)}, bf16[256,1024]{1,0:T(8,128)(2,1)S(1)}, u32[]{:S(2)}, u32[]{:S(2)}) collective-permute-start(bf16[256,1024]{1,0:T(8,128)(2,1)S(1)} %fusion.68), channel_id=1, source_target_pairs={{0,16},{8,24},{16,0},{24,8},{1,17},{9,25},{17,1},{25,9},{2,18},{10... | collective-permute-start | bytes 1572872 | tf_op jit(solution)/shard_map/ppermute | solution.py:378
  710.0 187.7 %reduce-scatter.13.cloned.1.call-start = ((), (), s32[]{:S(2)}) async-start(), calls=%async_computation.11 | async-start | bytes 2359296
  710.1 71.0 %collective-permute-start.28 = (bf16[2,256,4096]{2,1,0:T(8,128)(2,1)}, bf16[2,256,4096]{2,1,0:T(8,128)(2,1)}, u32[]{:S(2)}, u32[]{:S(2)}) collective-permute-start(bf16[2,256,4096]{2,1,0:T(8,128)(2,1)} %dynamic-slice_bitcast_fusion), channel_id=1, source_target_pairs={{0,8},{8,0},{16,24},{24,16},{1,9},{9,1},{17,25},{25,17},{2,10},{10... | collective-permute-start | bytes 12582920 | tf_op jit(solution)/shard_map/ppermute | solution.py:378
  723.7 48.3 %collective-permute-start.27 = (bf16[1024,1024]{0,1:T(8,128)(2,1)}, bf16[1024,1024]{0,1:T(8,128)(2,1)}, u32[]{:S(2)}, u32[]{:S(2)}) collective-permute-start(bf16[1024,1024]{0,1:T(8,128)(2,1)} %fusion.29), channel_id=1, source_target_pairs={{0,16},{8,24},{16,0},{24,8},{1,17},{9,25},{17,1},{25,9},{2,18},{10... | collective-permute-start | bytes 6291464 | tf_op jit(solution)/shard_map/ppermute | solution.py:378
  781.0 142.8 %reduce-scatter.11.cloned.1.call-start = ((), (), s32[]{:S(2)}) async-start(), calls=%async_computation.10 | async-start | bytes 2359296 | tf_op jit(solution)/shard_map/reduce_scatter | solution.py:418
  785.6 47.5 %collective-permute-start.29 = (bf16[256,4096]{1,0:T(8,128)(2,1)}, bf16[256,4096]{1,0:T(8,128)(2,1)}, u32[]{:S(2)}, u32[]{:S(2)}) collective-permute-start(bf16[256,4096]{1,0:T(8,128)(2,1)} %fusion.26), channel_id=1, source_target_pairs={{0,16},{8,24},{16,0},{24,8},{1,17},{9,25},{17,1},{25,9},{2,18},{10... | collective-permute-start | bytes 6291464 | tf_op jit(solution)/shard_map/ppermute | solution.py:378
  795.4 50.7 %collective-permute-start.5 = (f32[6,1024]{1,0:T(8,128)S(1)}, f32[6,1024]{1,0:T(8,128)S(1)}, u32[]{:S(2)}, u32[]{:S(2)}) collective-permute-start(f32[6,1024]{1,0:T(8,128)S(1)} %stack.108), channel_id=1, source_target_pairs={{0,8},{8,0},{16,24},{24,16},{1,9},{9,1},{17,25},{25,17},{2,10},{10... | collective-permute-start | bytes 73736 | tf_op jit(solution)/shard_map/ppermute | solution.py:378
  867.7 25.7 %collective-permute-start.9 = (f32[6,1024]{1,0:T(8,128)S(1)}, f32[6,1024]{1,0:T(8,128)S(1)}, u32[]{:S(2)}, u32[]{:S(2)}) collective-permute-start(f32[6,1024]{1,0:T(8,128)S(1)} %add.434), channel_id=1, source_target_pairs={{0,4},{1,5},{2,6},{3,7},{4,0},{5,1},{6,2},{7,3},{8,12},{9,13},{10,... | collective-permute-start | bytes 73736 | tf_op jit(solution)/shard_map/ppermute | solution.py:378
  (92 other events, 1878.4 us)
Sparse Core Ops, SparseCore 0:
  11.7 72.1 all-gather.4
  87.5 84.8 all-gather.6
  175.8 90.3 all-gather.8
  269.0 75.2 all-gather.10
  642.7 67.9 reduce-scatter.8
  714.2 67.2 reduce-scatter.6
  785.0 67.3 reduce-scatter.12
  855.9 67.8 reduce-scatter.10

commit v2 on v1

--- a/solution.py
+++ b/solution.py
@@ -391,33 +391,55 @@
     return lax.dynamic_index_in_dim(value, index, axis, keepdims=False)
 
 
-def reduce_rows(grads, sizes):
-    dp_size, inner = sizes
-    place = lax.axis_index("dp")
-    low, high = place % 2, place // 2
-    count = len(grads)
-    rows, columns = grads[0].shape
-    own = rows // (dp_size * inner)
-    sends = [g.reshape(dp_size // 2, 2, inner * own, columns) for g in grads]
-    keeps = [pick(g, low, 1) for g in sends]
-    sends = [pick(g, 1 - low, 1) for g in sends]
-    got = [swap(s, "dp", dp_size, 1) for s in sends]
-
-    def half(index):
-        return [
-            (pick(k, index, 0).astype(jnp.float32) + pick(r, index, 0).astype(jnp.float32))
-            for k, r in zip(keeps, got)
-        ]
-
-    out = [s.astype(jnp.bfloat16) for s in half(1 - high)]
-    mine = half(high)
-    came = [swap(s, "dp", dp_size, 2) for s in out]
-    both = [(m + c.astype(jnp.float32)).astype(jnp.bfloat16) for m, c in zip(mine, came)]
-    packed = jnp.stack([b.reshape(inner, own, columns) for b in both], axis=1)
-    packed = packed.reshape(inner * count * own, columns)
-    summed = lax.psum_scatter(packed, "fsdp", scatter_dimension=0, tiled=True)
-    summed = summed.reshape(count, own, columns).astype(jnp.float32)
-    return [summed[i] for i in range(count)]
+def fence(*values):
+    return lax.optimization_barrier(values)
+
+
+class Partial:
+    def __init__(self, value, sizes):
+        dp_size, inner = sizes
+        keys, places = [], {}
+        for axis, size in (("dp", dp_size), ("fsdp", inner)):
+            bit = size // 2
+            while bit:
+                keys.append((axis, bit))
+                places[(axis, bit)] = (lax.axis_index(axis) // bit) % 2
+                bit //= 2
+        own = value.shape[0] // (dp_size * inner)
+        self.sizes = {"dp": dp_size, "fsdp": inner}
+        self.keys, self.places = keys, places
+        self.value = value.reshape((2,) * len(keys) + (own, value.shape[1]))
+
+    def send(self, key):
+        axis = self.keys.index(key)
+        self.keys.remove(key)
+        out = pick(self.value, 1 - self.places[key], axis).astype(jnp.bfloat16)
+        self.value = pick(self.value, self.places[key], axis).astype(jnp.float32)
+        return swap(out, key[0], self.sizes[key[0]], key[1])
+
+    def take(self, received):
+        self.value = self.value + received.astype(jnp.float32)
+
+    def rest(self):
+        return self.value.astype(jnp.bfloat16)
+
+
+CORE = ("dp", 1)
+ACROSS = ("dp", 2)
+
+
+def scatter(parts, sizes):
+    inner = sizes[1]
+    rests = []
+    for part in parts:
+        rest = part.rest()
+        own, columns = rest.shape[-2:]
+        rests.append(rest.reshape(inner, own, columns))
+    packed = rests[0] if len(rests) == 1 else jnp.concatenate(rests, axis=1)
+    summed = lax.psum_scatter(
+        packed.reshape(-1, columns), "fsdp", scatter_dimension=0, tiled=True
+    ).astype(jnp.float32)
+    return [summed[i * own : (i + 1) * own] for i in range(len(parts))]
 
 
 def layer(
@@ -472,45 +494,121 @@
     phi = 0.5 * (1.0 + lax.erf(u * ROOT_HALF))
     hidden = (u * phi).astype(low)
     slope = (phi + u * (ROOT_TAU * jnp.exp(-0.5 * u * u))).astype(low)
-    block_out = (x2 + contract(hidden, w_out, (1,), (1,))).astype(low)
 
     eb = cotangent[0]
     e = eb.astype(jnp.float32)
+    g_out = contract(eb, hidden, (0,), (0,), low)
+    p_out = Partial(g_out, sizes)
+    flying = p_out.send(CORE)
+    eb, hidden, g_out = fence(eb, hidden, g_out)
     du = (contract(eb, w_out, (1,), (0,)) * slope.astype(jnp.float32)).astype(low)
-    g_out = contract(eb, hidden, (0,), (0,), low)
+    du, flying = fence(du, flying)
+    p_out.take(flying)
+    flying = p_out.send(ACROSS)
     g_in = contract(du, a3, (0,), (0,), low)
+    du, g_in = fence(du, g_in)
+    p_in = Partial(g_in, sizes)
+    flying_in = p_in.send(CORE)
     d3 = contract(du, w_in, (1,), (0,))
-    (g_mlp_out,) = reduce_rows([g_out], sizes)
-    (g_mlp_in,) = reduce_rows([g_in], sizes)
     back, gg3, gs3 = norm_back(x2, norms[4], d3)
     e2 = e + back
     e2b = e2.astype(low)
-    g_co = contract(e2b, co, (0,), (1,), low)
+    e2, e2b, flying, flying_in = fence(e2, e2b, flying, flying_in)
+    p_out.take(flying)
+    (g_mlp_out,) = scatter([p_out], sizes)
+    p_in.take(flying_in)
+    flying_in = p_in.send(ACROSS)
     d_co = contract(e2b, w_co, (1,), (0,), low)
     dcq, dck, dcv = cross_backward(starts, pages, cq, ck, cv, d_co, c_stats)
+    dcq, dck, dcv, flying_in = fence(dcq, dck, dcv, flying_in)
+    p_in.take(flying_in)
+    (g_mlp_in,) = scatter([p_in], sizes)
+    g_co = contract(e2b, co, (0,), (1,), low)
     g_cq = contract(dcq, a2, (1,), (0,), low)
     g_ck = contract(dck, images, (0, 1), (0, 1), low)
     g_cv = contract(dcv, images, (0, 1), (0, 1), low)
-    g_cross = reduce_rows([g_cq, g_ck, g_cv, g_co], sizes)
-    grad_images = contract(dck, w_ck, (2,), (0,)) + contract(dcv, w_cv, (2,), (0,))
+    dcq, g_cq, g_ck, g_cv, g_co = fence(dcq, g_cq, g_ck, g_cv, g_co)
+    p_cross = [Partial(g, sizes) for g in (g_cq, g_ck, g_cv, g_co)]
+    flying = [p.send(CORE) for p in p_cross]
     d2 = contract(dcq, w_cq, (0,), (0,))
     back, gg2, gs2 = norm_back(x1, norms[2], d2)
     e1 = e2 + back
     e1b = e1.astype(low)
+    e1, e1b, *flying = fence(e1, e1b, *flying)
+    for p, f in zip(p_cross, flying):
+        p.take(f)
+    flying = [p.send(ACROSS) for p in p_cross]
     g_so = contract(e1b, so, (0,), (1,), low)
+    p_so = Partial(g_so, sizes)
+    flying_so = p_so.send(CORE)
     d_so = contract(e1b, w_so, (1,), (0,), low)
     dsq, dsk, dsv = self_backward(starts, sq, sk, sv, d_so, s_stats, most)
+    dsq, dsk, dsv, flying_so, *flying = fence(dsq, dsk, dsv, flying_so, *flying)
+    for p, f in zip(p_cross, flying):
+        p.take(f)
+    g_cross = scatter(p_cross, sizes)
+    orders = []
+    keys = [ACROSS] + [("fsdp", 1 << i) for i in range(inner.bit_length() - 1)]
+    for shift in range(3):
+        orders.append(keys[shift:] + keys[:shift])
+    p_so.take(flying_so)
+    flying_so = p_so.send(keys[0])
     g_sq = contract(dsq, a1, (1,), (0,), low)
     g_sk = contract(dsk, a1, (0,), (0,), low)
     g_sv = contract(dsv, a1, (0,), (0,), low)
-    g_self = reduce_rows([g_sq, g_sk, g_sv, g_so], sizes)
+    dsq, dsk, dsv, g_sq, g_sk, g_sv, flying_so = fence(dsq, dsk, dsv, g_sq, g_sk, g_sv, flying_so)
+    p_so.take(flying_so)
+    p_self = [Partial(g, sizes) for g in (g_sq, g_sk, g_sv)]
+    flying = [p.send(CORE) for p in p_self]
+    flying_so = p_so.send(keys[1])
     d1 = (
         contract(dsq, w_sqkv[0], (0,), (0,))
         + contract(dsk, w_sqkv[1], (1,), (0,))
         + contract(dsv, w_sqkv[2], (1,), (0,))
     )
-    back, gg1, gs1 = norm_back(rows, norms[0], d1)
-    grad_in = e1 + back
+
+    def norm_one(d1):
+        back, gg1, gs1 = norm_back(rows, norms[0], d1)
+        return e1 + back, gg1, gs1
+
+    def image_grads(dck, dcv):
+        both = jnp.concatenate([dck, dcv], axis=2).transpose(1, 0, 2)
+        tokens, count, _ = both.shape
+        flat = contract(
+            both.reshape(tokens * count, 2 * width), w_rest[2:4].reshape(2 * width, width), (1,), (0,)
+        )
+        return flat.reshape(tokens, count, width).transpose(1, 0, 2)
+
+    def finish(hidden):
+        return (x2 + contract(hidden, w_out, (1,), (1,))).astype(low)
+
+    fillers = [(norm_one, (d1,)), (finish, (hidden,)), (image_grads, (dck, dcv))]
+    results = []
+    waits = (d1,)
+    parts = p_self + [p_so]
+    flights = flying + [flying_so]
+    for stage in range(len(keys)):
+        if stage < 3:
+            job, needs = fillers[stage]
+            fenced = fence(*(flights + list(waits) + list(needs)))
+            needs = fenced[-len(needs) :]
+        else:
+            fenced = fence(*(flights + list(waits)))
+        for p, f in zip(parts, fenced):
+            p.take(f)
+        parts = [p for p in parts if len(p.keys)]
+        flights = [p.send(o[stage]) for p, o in zip(p_self, orders)]
+        if len(p_so.keys):
+            flights.append(p_so.send(p_so.keys[-1] if len(p_so.keys) == 1 else keys[stage + 2]))
+        if stage < 3:
+            done = job(*needs)
+            waits = jax.tree.leaves(done)[:1]
+            results.append(done)
+    for p, f in zip(parts, flights):
+        p.take(f)
+    grad_in, gg1, gs1 = results[0]
+    block_out, grad_images = results[1], results[2]
+    g_self = [p.value for p in p_self + [p_so]]
     norm_grads = butterfly_sum(jnp.stack([gg1, gs1, gg2, gs2, gg3, gs3]), axes)
     norm_grads = lax.dynamic_slice(norm_grads, (0, offset), (6, mine))
     weight_grads = [g.T for g in g_self + g_cross + [g_mlp_in, g_mlp_out]]

time: 944 us -> 821 us (0.87)
  waiting for transfers between devices: 296 us -> 160 us
  starting transfers between devices: 41.4 us -> 56.9 us
  other arithmetic: 76.5 us -> 90.1 us
  matrix products: 235 us -> 225 us
    ppermute x30 -> x42, waiting for transfers between devices: 130 us -> 38.6 us  [swap(): return lax.ppermute(value, axis, [(i, i ^ bit) for i in range(size)])]
    add x2 -> x23, other arithmetic: 4.69 us -> 31.1 us  [the longest x22 24.2 us: take(): self.value = self.value + received.astype(jnp.float32)]
    reduce_scatter x3 -> x2, waiting for transfers between devices: 24.2 us -> 0.02 us  [scatter(): lax.psum_scatter(packed.reshape(-1, columns), 'fsdp', scatter_dimension=0...]
    all_gather x1, waiting for transfers between devices: 57.8 us -> 35.4 us  [layer(): w_out = lax.all_gather(turned(mlp_out), AXES, axis=0, tiled=True)]
    ppermute x30 -> x42, starting transfers between devices: 41 us -> 56.2 us  [swap(): return lax.ppermute(value, axis, [(i, i ^ bit) for i in range(size)])]
    convert_element_type x22 -> x9, other arithmetic: 38.7 us -> 25.8 us  [the longest x6 14.6 us: rest(): return self.value.astype(jnp.bfloat16)]
    convert_element_type x0 -> x22, local copies, waits for them, and re-layouts: none -> 12.7 us  [send(): out = pick(self.value, 1 - self.places[key], axis).astype(jnp.bfloat16)]
    dynamic_slice x3 -> x8, local copies, waits for them, and re-layouts: 13.3 us -> 2.15 us  [pick(): return lax.dynamic_index_in_dim(value, index, axis, keepdims=False)]
  transfers between devices with their start and end apart: 38 -> 49, of which waited for: 20 -> 16; matrix products, arithmetic and copies ran while one was open for 37% -> 45% of each run, Pallas kernels for 19% -> 22%
where the time goes in v2:
time: 821 us; the launch traced here: 810 us
  matrix products  225 us (27%)
  Pallas kernels  176 us (21%)
  waiting for transfers between devices  160 us (19%)
  other arithmetic  90.1 us (11%)
  local copies, waits for them, and re-layouts  85.8 us (10%)
  starting transfers between devices  56.9 us (7%)
  between operations  16.3 us (2%)
    dot_general x29, matrix products, contract(): lax.dot_general(a, b, ((left, right), ((), ())), preferred_element_type=j...  225 us
    all_gather x2, waiting for transfers between devices, gather(): return lax.all_gather(stacked, AXES, axis=1, tiled=True)  82.6 us
    ppermute x42, starting transfers between devices, swap(): return lax.ppermute(value, axis, [(i, i ^ bit) for i in range(size)])  56.2 us
    pallas_call x1, Pallas kernels, cross_backward(): pl.pallas_call(functools.partial(cross_backward_kernel, pairs), out_shape...  55.8 us
    pallas_call x1, Pallas kernels, cross_forward(): pl.pallas_call(functools.partial(cross_forward_kernel, pairs), out_shape=...  55.7 us
    unnamed x190, local copies, waits for them, and re-layouts  41 us
    ppermute x42, waiting for transfers between devices, swap(): return lax.ppermute(value, axis, [(i, i ^ bit) for i in range(size)])  38.6 us
    all_gather x1, waiting for transfers between devices, layer(): w_out = lax.all_gather(turned(mlp_out), AXES, axis=0, tiled=True)  35.4 us
  transfers between devices with their start and end apart: 49, of which 16 were waited for; matrix products, arithmetic and copies ran while one was open for 45% of the time, Pallas kernels for 22%

profile of v2, /device:TPU:0, one launch (start us, length us, event | category | flops | bytes accessed | tf_op | source)
XLA Modules:
  0.0 810.2 jit_solution(13190293289106567962)
XLA Ops:
  43.1 40.5 %all-gather.5.cloned.1.call-done = bf16[3,1024,1024]{2,1,0:T(8,128)(2,1)} async-done(((bf16[3,32,1024]{2,1,0:T(8,128)(2,1)}), bf16[3,1024,1024]{2,1,0:T(8,128)(2,1)}) %all-gather.5.cloned.1.call-update) | async-done | bytes 6291472 | tf_op jit(solution)/shard_map/all_gather | solution.py:460
  97.4 32.2 %self_forward.1 = (bf16[1024,1024]{1,0:T(8,128)(2,1)}, f32[4,4,1024]{2,1,0:T(4,128)}) custom-call(s32[5]{0:T(128)} %convert_reduce_fusion.1.starts, bf16[1024,1024]{1,0:T(8,128)(2,1)} %convolution_convert_fusion.13.q_ref, bf16[1024,1024]{1,0:T(8,128)(2,1)} %convolution_convert_fusion.12.k_ref, bf16[1024,1024]{1,0:T(8,128)(2,1)} %convolution_convert_fusion.11.v_ref), custom_call_target="tpu_custom_call" | custom-call | flops 5368709120 | bytes 10485760 | tf_op jit(solution)/shard_map/self_forward/pallas_call | solution.py:301
  129.6 42.1 %all-gather.7.cloned.1.call-done = bf16[5,1024,1024]{2,1,0:T(8,128)(2,1)} async-done(((bf16[5,32,1024]{2,1,0:T(8,128)(2,1)}), bf16[5,1024,1024]{2,1,0:T(8,128)(2,1)}) %all-gather.7.cloned.1.call-update) | async-done | bytes 10485776 | tf_op jit(solution)/shard_map/all_gather | solution.py:460
  182.9 7.6 convert_bitcast_fusion.2.k_ref
  190.5 7.8 convert_bitcast_fusion.1.v_ref
  198.2 55.7 %cross_forward.1 = (bf16[1024,1024]{1,0:T(8,128)(2,1)}, f32[4,4,1024]{2,1,0:T(4,128)}) custom-call(s32[5]{0:T(128)} %convert_reduce_fusion.1.starts, s32[4]{0:T(128)} %bitcast.495, bf16[1024,1024]{1,0:T(8,128)(2,1)} %convolution_convert_fusion.10.q_ref, bf16[4,588,1024]{2,1,0:T(8,128)(2,1)} %convert_bitcast_fusion.2.k_ref, ...), custom_call_target="tpu_custom_call" | custom-call | flops 13564379136 | bytes 20971520 | tf_op jit(solution)/shard_map/cross_forward/pallas_call | solution.py:249
  265.7 18.8 %multiply_convert_fusion.1 = (bf16[1024,4096]{1,0:T(8,128)(2,1)S(1)}, f32[1024,4096]{1,0:T(8,128)}) fusion(bf16[4096,1024]{0,1:T(8,128)(2,1)} %all-gather.9.cloned.1.call-done, f32[1024,1024]{0,1:T(8,128)} %copy-done.2, f32[1024]{0:T(1024)S(1)} %bitcast.486, f32[1024]{0:T(1024)S(1)} %bitcast.468, f32[1024]{0:T(1024)S(1)} %add_rsqrt_fusion, ...), kind=kOutput, calls=%fused_computation.7 | convolution fusion | flops 8616148992 | bytes 37765120 | tf_op jit(solution)/shard_map/dot_general | solution.py:355
  284.5 9.6 %convolution_convert_fusion = bf16[4096,1024]{0,1:T(8,128)(2,1)S(1)} fusion(bf16[1024,4096]{1,0:T(8,128)(2,1)S(1)} %get-tuple-element.137, bf16[1,1024,1024]{2,1,0:T(8,128)(2,1)S(1)} %copy-done.38), kind=kOutput, calls=%fused_computation.15 | convolution fusion | flops 8594128896 | bytes 18874368 | tf_op jit(solution)/shard_map/dot_general | solution.py:355
  308.3 35.4 %all-gather.11.cloned.1.call-done = bf16[1024,4096]{1,0:T(8,128)(2,1)} async-done(((bf16[32,4096]{1,0:T(8,128)(2,1)}), bf16[1024,4096]{1,0:T(8,128)(2,1)}) %all-gather.11.cloned.1.call-update) | async-done | bytes 8388624 | tf_op jit(solution)/shard_map/all_gather | solution.py:471
  343.7 19.5 %multiply_convert_fusion = bf16[1024,4096]{1,0:T(8,128)(2,1)} fusion(bf16[1024,1024]{0,1:T(8,128)(2,1)S(1)} %bitcast.432, bf16[1024,4096]{1,0:T(8,128)(2,1)} %all-gather.11.cloned.1.call-done, f32[1024,4096]{1,0:T(8,128)} %get-tuple-element.257), kind=kOutput, calls=%fused_computation.6 | convolution fusion | flops 8640266240 | bytes 35651584 | tf_op jit(solution)/shard_map/dot_general | solution.py:355
  363.2 12.6 %convolution_convert_fusion.1 = bf16[4096,1024]{1,0:T(8,128)(2,1)S(1)} fusion(bf16[1024,4096]{1,0:T(8,128)(2,1)} %multiply_convert_fusion, f32[1024,1024]{0,1:T(8,128)S(1)} %copy-done.3, f32[1024]{0:T(1024)S(1)} %bitcast.487, f32[1024]{0:T(1024)S(1)} %bitcast.469, f32[1024]{0:T(1024)S(1)} %add_rsqrt_fusion, f32[1024]{0:T(1024)S(1)} %broadcast_multiply_fusion.6), kind=kOutput, calls=%fused_computation.16 | convolution fusion | flops 8599371776 | bytes 20987904 | tf_op jit(solution)/shard_map/dot_general | solution.py:355
  389.0 15.9 %fusion.99 = (f32[1024]{0:T(1024)}, f32[1024,1024]{1,0:T(8,128)}) fusion(bf16[1024,4096]{1,0:T(8,128)(2,1)} %multiply_convert_fusion, bf16[4096,1024]{0,1:T(8,128)(2,1)} %all-gather.9.cloned.1.call-done), kind=kOutput, calls=%fused_computation.260 | convolution fusion | flops 8590982144 | bytes 20975616 | tf_op jit(solution)/shard_map/dot_general | solution.py:355
  419.3 16.3 %collective-permute-done.6 = bf16[2,2,2,32,4096]{4,3,2,1,0:T(8,128)(2,1)} collective-permute-done((bf16[2,2,2,32,4096]{4,3,2,1,0:T(8,128)(2,1)}, bf16[2,2,2,32,4096]{4,3,2,1,0:T(8,128)(2,1)}, u32[]{:S(2)}, u32[]{:S(2)}) %collective-permute-start.6) | collective-permute-done | bytes 2097184 | tf_op jit(solution)/shard_map/ppermute | solution.py:378
  442.9 6.3 convolution_convert_fusion.7
  454.1 6.1 convolution_convert_fusion.9.g_ref
  460.2 55.8 %cross_backward.1 = (bf16[1024,1024]{1,0:T(8,128)(2,1)}, bf16[4,588,1024]{2,1,0:T(8,128)(2,1)}, bf16[4,588,1024]{2,1,0:T(8,128)(2,1)}) custom-call(s32[5]{0:T(128)} %convert_reduce_fusion.1.starts, s32[4]{0:T(128)} %bitcast.496, bf16[1024,1024]{1,0:T(8,128)(2,1)} %convolution_convert_fusion.10.q_ref, bf16[4,588,1024]{2,1,0:T(8,128)(2,1)} %convert_bitcast_fusion.2.k_ref, ...), custom_call_target="tpu_custom_call" | custom-call | flops 33910947840 | bytes 31457280 | tf_op jit(solution)/shard_map/cross_backward/pallas_call | solution.py:273
  516.1 10.9 %bitcast_convert_fusion.1 = bf16[1024,1024]{1,0:T(8,128)(2,1)} fusion(bf16[4,588,1024]{2,1,0:T(8,128)(2,1)} %get-tuple-element.142, bf16[4,588,1024]{2,0,1:T(4,128)(2,1)} %param.22), kind=kOutput, calls=%fused_computation.47 | convolution fusion | flops 4933550080 | bytes 11730944 | tf_op jit(solution)/shard_map/dot_general | solution.py:355
  531.1 7.5 bitcast_convert_fusion
  569.4 7.1 fusion.93
  598.8 32.2 %self_backward.1 = (bf16[1024,1024]{1,0:T(8,128)(2,1)}, bf16[1024,1024]{1,0:T(8,128)(2,1)}, bf16[1024,1024]{1,0:T(8,128)(2,1)}) custom-call(s32[5]{0:T(128)} %convert_reduce_fusion.1.starts, bf16[1024,1024]{1,0:T(8,128)(2,1)} %convolution_convert_fusion.13.q_ref, bf16[1024,1024]{1,0:T(8,128)(2,1)} %convolution_convert_fusion.12.k_ref, ...), custom_call_target="tpu_custom_call" | custom-call | flops 13421772800 | bytes 16777216 | tf_op jit(solution)/shard_map/self_backward/pallas_call | solution.py:324
  705.9 6.9 fusion.21
  731.9 14.9 %add_convert_fusion = bf16[1024,1024]{0,1:T(8,128)(2,1)} fusion(f32[1024,1024]{0,1:T(8,128)S(1)} %copy-done.5, bf16[1024,4096]{1,0:T(8,128)(2,1)} %copy-done.69, bf16[1024,4096]{1,0:T(8,128)(2,1)} %all-gather.11.cloned.1.call-done), kind=kOutput, calls=%fused_computation.50 | convolution fusion | flops 8592031744 | bytes 23068672 | tf_op jit(solution)/shard_map/dot_general | solution.py:355
  750.8 16.6 %fusion.30 = f32[4,588,1024]{2,1,0:T(8,128)} fusion(bf16[2048,1024,1]{1,0,2:T(8,128)(2,1)} %bitcast.433, bf16[4,588,1024]{2,1,0:T(8,128)(2,1)} %get-tuple-element.143, bf16[4,588,1024]{2,1,0:T(8,128)(2,1)} %get-tuple-element.142), kind=kOutput, calls=%fused_computation.69 | convolution fusion | flops 9884270592 | bytes 23461888 | tf_op jit(solution)/shard_map/dot_general | solution.py:355
  767.4 13.8 %copy.117 = f32[4,588,1024]{2,0,1:T(4,128)} copy(f32[4,588,1024]{2,1,0:T(8,128)} %fusion.30) | data formatting | bytes 19267584
  (441 shorter events, 301.6 us)
Async XLA Ops:
  7.2 76.4 %all-gather.5.cloned.1.call-start = ((), (), s32[]{:S(2)}) async-start(), calls=%async_computation.3 | async-start | bytes 6488064 | tf_op jit(solution)/shard_map/all_gather | solution.py:460
  9.9 161.9 %all-gather.7.cloned.1.call-start = ((), (), s32[]{:S(2)}) async-start(), calls=%async_computation.4 | async-start | bytes 10813440 | tf_op jit(solution)/shard_map/all_gather | solution.py:460
  15.2 250.4 %all-gather.9.cloned.1.call-start = ((), (), s32[]{:S(2)}) async-start(), calls=%async_computation.5 | async-start | bytes 8650752 | tf_op jit(solution)/shard_map/all_gather | solution.py:470
  17.1 326.6 %all-gather.11.cloned.1.call-start = ((), (), s32[]{:S(2)}) async-start(), calls=%async_computation.6 | async-start | bytes 8650752 | tf_op jit(solution)/shard_map/all_gather | solution.py:471
  21.8 609.2 %reduce-scatter.8.cloned.1.call-start = ((), (), s32[]{:S(2)}) async-start(), calls=%async_computation.8 | async-start | bytes 2359296 | tf_op jit(solution)/shard_map/reduce_scatter | solution.py:439
  298.6 64.6 %collective-permute-start.5 = (bf16[2,2,2,2,32,4096]{5,4,3,2,1,0:T(8,128)(2,1)}, bf16[2,2,2,2,32,4096]{5,4,3,2,1,0:T(8,128)(2,1)}, u32[]{:S(2)}, u32[]{:S(2)}) collective-permute-start(bf16[2,2,2,2,32,4096]{5,4,3,2,1,0:T(8,128)(2,1)} %dynamic-slice_bitcast_fusion.1), channel_id=1, source_target_pairs={{0,8},{8,0},{16,24},{24,16},{1,9},{9,1},{17,25},{25,17},{2,10},{10... | collective-permute-start | bytes 12582920 | tf_op jit(solution)/shard_map/ppermute | solution.py:378
  380.4 55.3 %collective-permute-start.7 = (bf16[2,2,2,2,128,1024]{5,4,3,2,1,0:T(8,128)(2,1)}, bf16[2,2,2,2,128,1024]{5,4,3,2,1,0:T(8,128)(2,1)}, u32[]{:S(2)}, u32[]{:S(2)}) collective-permute-start(bf16[2,2,2,2,128,1024]{5,4,3,2,1,0:T(8,128)(2,1)} %dynamic-slice_bitcast_fusion), channel_id=1, source_target_pairs={{0,8},{8,0},{16,24},{24,16},{1,9},{9,1},{17,25},{25,17},{2,10},{10... | collective-permute-start | bytes 12582920 | tf_op jit(solution)/shard_map/ppermute | solution.py:378
  387.6 48.0 %collective-permute-start.6 = (bf16[2,2,2,32,4096]{4,3,2,1,0:T(8,128)(2,1)}, bf16[2,2,2,32,4096]{4,3,2,1,0:T(8,128)(2,1)}, u32[]{:S(2)}, u32[]{:S(2)}) collective-permute-start(bf16[2,2,2,32,4096]{4,3,2,1,0:T(8,128)(2,1)} %fusion.43), channel_id=1, source_target_pairs={{0,16},{8,24},{16,0},{24,8},{1,17},{9,25},{17,1},{25,9},{2,18},{10... | collective-permute-start | bytes 6291464 | tf_op jit(solution)/shard_map/ppermute | solution.py:378
  441.5 74.5 %collective-permute-start.8 = (bf16[2,2,2,128,1024]{4,3,2,1,0:T(8,128)(2,1)}, bf16[2,2,2,128,1024]{4,3,2,1,0:T(8,128)(2,1)}, u32[]{:S(2)}, u32[]{:S(2)}) collective-permute-start(bf16[2,2,2,128,1024]{4,3,2,1,0:T(8,128)(2,1)} %fusion.44), channel_id=1, source_target_pairs={{0,16},{8,24},{16,0},{24,8},{1,17},{9,25},{17,1},{25,9},{2,18},{10... | collective-permute-start | bytes 6291464 | tf_op jit(solution)/shard_map/ppermute | solution.py:378
  453.6 265.4 %reduce-scatter.10.cloned.1.call-start = ((), (), s32[]{:S(2)}) async-start(), calls=%async_computation.9 | async-start | bytes 2359296
  552.4 24.1 %collective-permute-start.9 = (bf16[2,2,2,2,32,1024]{5,4,3,2,1,0:T(8,128)(2,1)}, bf16[2,2,2,2,32,1024]{5,4,3,2,1,0:T(8,128)(2,1)}, u32[]{:S(2)}, u32[]{:S(2)}) collective-permute-start(bf16[2,2,2,2,32,1024]{5,4,3,2,1,0:T(8,128)(2,1)} %dynamic-slice_bitcast_fusion.5), channel_id=1, source_target_pairs={{0,8},{8,0},{16,24},{24,16},{1,9},{9,1},{17,25},{25,17},{2,10},{10... | collective-permute-start | bytes 3145736 | tf_op jit(solution)/shard_map/ppermute | solution.py:378
  569.3 231.7 %reduce-scatter.6.cloned.1.call-start = ((), (), s32[]{:S(2)}) async-start(), calls=%async_computation.7 | async-start | bytes 2359296 | tf_op jit(solution)/shard_map/reduce_scatter | solution.py:439
  580.3 52.8 %collective-permute-start.13 = (bf16[2,2,2,2,32,1024]{5,4,1,2,3,0:T(8,128)(2,1)}, bf16[2,2,2,2,32,1024]{5,4,1,2,3,0:T(8,128)(2,1)}, u32[]{:S(2)}, u32[]{:S(2)}) collective-permute-start(bf16[2,2,2,2,32,1024]{5,4,1,2,3,0:T(8,128)(2,1)} %bitcast.419), channel_id=1, source_target_pairs={{0,8},{8,0},{16,24},{24,16},{1,9},{9,1},{17,25},{25,17},{2,10},{10... | collective-permute-start | bytes 3145736 | tf_op jit(solution)/shard_map/ppermute | solution.py:378
  583.5 49.5 %collective-permute-start.14 = (bf16[2,2,2,32,1024]{4,3,2,1,0:T(8,128)(2,1)}, bf16[2,2,2,32,1024]{4,3,2,1,0:T(8,128)(2,1)}, u32[]{:S(2)}, u32[]{:S(2)}) collective-permute-start(bf16[2,2,2,32,1024]{4,3,2,1,0:T(8,128)(2,1)} %fusion.59), channel_id=1, source_target_pairs={{0,16},{8,24},{16,0},{24,8},{1,17},{9,25},{17,1},{25,9},{2,18},{10... | collective-permute-start | bytes 1572872 | tf_op jit(solution)/shard_map/ppermute | solution.py:378
  587.2 45.8 %collective-permute-start.15 = (bf16[2,2,2,32,1024]{4,3,2,1,0:T(8,128)(2,1)}, bf16[2,2,2,32,1024]{4,3,2,1,0:T(8,128)(2,1)}, u32[]{:S(2)}, u32[]{:S(2)}) collective-permute-start(bf16[2,2,2,32,1024]{4,3,2,1,0:T(8,128)(2,1)} %fusion.60), channel_id=1, source_target_pairs={{0,16},{8,24},{16,0},{24,8},{1,17},{9,25},{17,1},{25,9},{2,18},{10... | collective-permute-start | bytes 1572872 | tf_op jit(solution)/shard_map/ppermute | solution.py:378
  589.5 43.5 %collective-permute-start.16 = (bf16[2,2,2,32,1024]{4,3,2,1,0:T(8,128)(2,1)}, bf16[2,2,2,32,1024]{4,3,2,1,0:T(8,128)(2,1)}, u32[]{:S(2)}, u32[]{:S(2)}) collective-permute-start(bf16[2,2,2,32,1024]{4,3,2,1,0:T(8,128)(2,1)} %fusion.61), channel_id=1, source_target_pairs={{0,16},{8,24},{16,0},{24,8},{1,17},{9,25},{17,1},{25,9},{2,18},{10... | collective-permute-start | bytes 1572872 | tf_op jit(solution)/shard_map/ppermute | solution.py:378
  592.5 40.5 %collective-permute-start.17 = (bf16[2,2,2,32,1024]{4,3,2,1,0:T(8,128)(2,1)}, bf16[2,2,2,32,1024]{4,3,2,1,0:T(8,128)(2,1)}, u32[]{:S(2)}, u32[]{:S(2)}) collective-permute-start(bf16[2,2,2,32,1024]{4,3,2,1,0:T(8,128)(2,1)} %fusion.62), channel_id=1, source_target_pairs={{0,16},{8,24},{16,0},{24,8},{1,17},{9,25},{17,1},{25,9},{2,18},{10... | collective-permute-start | bytes 1572872 | tf_op jit(solution)/shard_map/ppermute | solution.py:378
  678.8 42.2 %collective-permute-start.23 = (bf16[2,2,2,32,1024]{4,3,0,1,2:T(8,128)(2,1)}, bf16[2,2,2,32,1024]{4,3,0,1,2:T(8,128)(2,1)}, u32[]{:S(2)}, u32[]{:S(2)}) collective-permute-start(bf16[2,2,2,32,1024]{4,3,0,1,2:T(8,128)(2,1)} %fusion.64), channel_id=1, source_target_pairs={{0,16},{8,24},{16,0},{24,8},{1,17},{9,25},{17,1},{25,9},{2,18},{10... | collective-permute-start | bytes 1572872 | tf_op jit(solution)/shard_map/ppermute | solution.py:378
  681.0 40.0 %collective-permute-start.24 = (bf16[2,2,2,32,1024]{4,3,0,1,2:T(8,128)(2,1)}, bf16[2,2,2,32,1024]{4,3,0,1,2:T(8,128)(2,1)}, u32[]{:S(2)}, u32[]{:S(2)}) collective-permute-start(bf16[2,2,2,32,1024]{4,3,0,1,2:T(8,128)(2,1)} %fusion.65), channel_id=1, source_target_pairs={{0,1},{1,0},{2,3},{3,2},{4,5},{5,4},{6,7},{7,6},{8,9},{9,8},{10,11... | collective-permute-start | bytes 1572872 | tf_op jit(solution)/shard_map/ppermute | solution.py:378
  684.3 36.7 %collective-permute-start.25 = (bf16[2,2,2,32,1024]{4,3,2,0,1:T(8,128)(2,1)}, bf16[2,2,2,32,1024]{4,3,2,0,1:T(8,128)(2,1)}, u32[]{:S(2)}, u32[]{:S(2)}) collective-permute-start(bf16[2,2,2,32,1024]{4,3,2,0,1:T(8,128)(2,1)} %fusion.66), channel_id=1, source_target_pairs={{0,2},{1,3},{2,0},{3,1},{4,6},{5,7},{6,4},{7,5},{8,10},{9,11},{10,... | collective-permute-start | bytes 1572872 | tf_op jit(solution)/shard_map/ppermute | solution.py:378
  689.7 31.3 %collective-permute-start.26 = (bf16[2,32,1024]{2,1,0:T(8,128)(2,1)S(1)}, bf16[2,32,1024]{2,1,0:T(8,128)(2,1)S(1)}, u32[]{:S(2)}, u32[]{:S(2)}) collective-permute-start(bf16[2,32,1024]{2,1,0:T(8,128)(2,1)S(1)} %fusion.71), channel_id=1, source_target_pairs={{0,2},{1,3},{2,0},{3,1},{4,6},{5,7},{6,4},{7,5},{8,10},{9,11},{10,... | collective-permute-start | bytes 393224 | tf_op jit(solution)/shard_map/ppermute | solution.py:378
  723.6 27.1 %collective-permute-start.27 = (bf16[2,2,32,1024]{3,2,0,1:T(8,128)(2,1)}, bf16[2,2,32,1024]{3,2,0,1:T(8,128)(2,1)}, u32[]{:S(2)}, u32[]{:S(2)}) collective-permute-start(bf16[2,2,32,1024]{3,2,0,1:T(8,128)(2,1)} %fusion.68), channel_id=1, source_target_pairs={{0,1},{1,0},{2,3},{3,2},{4,5},{5,4},{6,7},{7,6},{8,9},{9,8},{10,11... | collective-permute-start | bytes 786440 | tf_op jit(solution)/shard_map/ppermute | solution.py:378
  726.2 24.6 %collective-permute-start.28 = (bf16[2,2,32,1024]{3,2,0,1:T(8,128)(2,1)}, bf16[2,2,32,1024]{3,2,0,1:T(8,128)(2,1)}, u32[]{:S(2)}, u32[]{:S(2)}) collective-permute-start(bf16[2,2,32,1024]{3,2,0,1:T(8,128)(2,1)} %fusion.69), channel_id=1, source_target_pairs={{0,2},{1,3},{2,0},{3,1},{4,6},{5,7},{6,4},{7,5},{8,10},{9,11},{10,... | collective-permute-start | bytes 786440 | tf_op jit(solution)/shard_map/ppermute | solution.py:378
  728.8 21.9 %collective-permute-start.29 = (bf16[2,2,32,1024]{3,2,1,0:T(8,128)(2,1)}, bf16[2,2,32,1024]{3,2,1,0:T(8,128)(2,1)}, u32[]{:S(2)}, u32[]{:S(2)}) collective-permute-start(bf16[2,2,32,1024]{3,2,1,0:T(8,128)(2,1)} %fusion.70), channel_id=1, source_target_pairs={{0,4},{1,5},{2,6},{3,7},{4,0},{5,1},{6,2},{7,3},{8,12},{9,13},{10,... | collective-permute-start | bytes 786440 | tf_op jit(solution)/shard_map/ppermute | solution.py:378
  (117 other events, 1593.5 us)
Sparse Core Ops, SparseCore 0:
  11.6 71.9 all-gather.4
  87.2 84.5 all-gather.6
  175.2 90.3 all-gather.8
  268.5 75.1 all-gather.10
  453.8 67.0 reduce-scatter.7
  569.5 68.1 reduce-scatter.9
  651.0 72.4 reduce-scatter.5

commit v3 on v2

--- a/solution.py
+++ b/solution.py
@@ -3,6 +3,7 @@
 import jax.numpy as jnp
 from jax import lax
 from jax.experimental import pallas as pl
+from jax.experimental.layout import Layout, with_layout_constraint
 from jax.experimental.pallas import tpu as pltpu
 from jax.sharding import PartitionSpec as P
 
@@ -37,6 +38,36 @@
     return jnp.concatenate([pair[:HALF, :QB], pair[HALF:, QB:]], axis=0)
 
 
+def attend(scores, values_turned):
+    peaks = [jnp.max(s, axis=0, keepdims=True) for s in scores]
+    raised = [jnp.exp(s - peak) for s, peak in zip(scores, peaks)]
+    totals = [jnp.sum(r, axis=0, keepdims=True) for r in raised]
+    low = [(r * (1.0 / total)).astype(jnp.bfloat16) for r, total in zip(raised, totals)]
+    mixed = [diagonal(dot_nn(vt, p)).astype(jnp.bfloat16) for vt, p in zip(values_turned, low)]
+    stats = []
+    for peak, total in zip(peaks, totals):
+        lse = peak + jnp.log(total)
+        stats += [lse[:, :QB], lse[:, QB:]]
+    return mixed, jnp.concatenate(stats, axis=0)
+
+
+def pull_back(scores, values_in, pulled, stats, keys_turned):
+    attention = [
+        jnp.exp(s - jnp.concatenate([stats[2 * i : 2 * i + 1], stats[2 * i + 1 : 2 * i + 2]], axis=1))
+        for i, s in enumerate(scores)
+    ]
+    low = [a.astype(jnp.bfloat16) for a in attention]
+    pushed = [dot_nt(v, g) for v, g in zip(values_in, pulled)]
+    inner = [jnp.sum(a * p, axis=0, keepdims=True) for a, p in zip(attention, pushed)]
+    grads = [
+        (a * (p - i)).astype(jnp.bfloat16) for a, p, i in zip(attention, pushed, inner)
+    ]
+    turned = [
+        diagonal(dot_nn(kt, g) * 0.125).astype(jnp.bfloat16) for kt, g in zip(keys_turned, grads)
+    ]
+    return low, grads, turned
+
+
 def query_places(block):
     return block * QB + lax.broadcasted_iota(jnp.int32, (1, QB), 1)
 
@@ -54,23 +85,15 @@
             rows = pl.ds(pl.multiple_of(block * QB, QB), QB)
             place = query_places(block)
             member = (place >= low) & (place < high)
-            for pair in range(pairs):
-                lanes = slice(pair * LANES, (pair + 1) * LANES)
-                stacked = head_stack(q_ref[rows, lanes], 0.125)
-                scores = dot_nt(k_ref[image, :, lanes], stacked)
-                peak = jnp.max(scores, axis=0, keepdims=True)
-                raised = jnp.exp(scores - peak)
-                total = jnp.sum(raised, axis=0, keepdims=True)
-                attention = (raised * (1.0 / total)).astype(jnp.bfloat16)
-                mixed = diagonal(dot_nn(vt_ref[pair], attention)).astype(jnp.bfloat16)
-                lse = peak + jnp.log(total)
-                o_ref[lanes, rows] = jnp.where(member, mixed, o_ref[lanes, rows])
-                l_ref[0, 2 * pair : 2 * pair + 1, rows] = jnp.where(
-                    member, lse[:, :QB], l_ref[0, 2 * pair : 2 * pair + 1, rows]
-                )
-                l_ref[0, 2 * pair + 1 : 2 * pair + 2, rows] = jnp.where(
-                    member, lse[:, QB:], l_ref[0, 2 * pair + 1 : 2 * pair + 2, rows]
-                )
+            spans = [slice(pair * LANES, (pair + 1) * LANES) for pair in range(pairs)]
+            scores = [
+                dot_nt(k_ref[image, :, lanes], head_stack(q_ref[rows, lanes], 0.125))
+                for lanes in spans
+            ]
+            mixed, stats = attend(scores, [vt_ref[pair] for pair in range(pairs)])
+            for lanes, block_out in zip(spans, mixed):
+                o_ref[lanes, rows] = jnp.where(member, block_out, o_ref[lanes, rows])
+            l_ref[0, :, rows] = jnp.where(member, stats, l_ref[0, :, rows])
             return carry
 
         lax.fori_loop(low // QB, (high - 1) // QB + 1, body, 0)
@@ -98,26 +121,22 @@
             rows = pl.ds(pl.multiple_of(block * QB, QB), QB)
             place = query_places(block)
             member = (place >= low) & (place < high)
+            spans = [slice(pair * LANES, (pair + 1) * LANES) for pair in range(pairs)]
+            stacked = [head_stack(q_ref[rows, lanes], 0.125) for lanes in spans]
+            pulled = [head_stack(g_ref[rows, lanes]) for lanes in spans]
+            stats = jnp.where(member, l_ref[0, :, rows], 1e30)
+            keys_in = [k_ref[image, :, lanes] for lanes in spans]
+            values_in = [v_ref[image, :, lanes] for lanes in spans]
+            soft, grads, turned = pull_back(
+                [dot_nt(k, q) for k, q in zip(keys_in, stacked)], values_in, pulled, stats,
+                [kt_ref[pair] for pair in range(pairs)],
+            )
+            for pair, lanes in enumerate(spans):
+                dq_ref[lanes, rows] = jnp.where(member, turned[pair], dq_ref[lanes, rows])
             for pair in range(pairs):
-                lanes = slice(pair * LANES, (pair + 1) * LANES)
-                stacked = head_stack(q_ref[rows, lanes], 0.125)
-                pulled = head_stack(g_ref[rows, lanes])
-                lse = jnp.concatenate(
-                    [
-                        jnp.where(member, l_ref[0, 2 * pair : 2 * pair + 1, rows], 1e30),
-                        jnp.where(member, l_ref[0, 2 * pair + 1 : 2 * pair + 2, rows], 1e30),
-                    ],
-                    axis=1,
-                )
-                scores = dot_nt(k_ref[image, :, lanes], stacked)
-                attention = jnp.exp(scores - lse)
-                pushed = dot_nt(v_ref[image, :, lanes], pulled)
-                dva_ref[pair] += dot_nn(attention.astype(jnp.bfloat16), pulled)
-                inner = jnp.sum(attention * pushed, axis=0, keepdims=True)
-                grad = (attention * (pushed - inner)).astype(jnp.bfloat16)
-                dka_ref[pair] += dot_nn(grad, stacked)
-                turned = diagonal(dot_nn(kt_ref[pair], grad) * 0.125).astype(jnp.bfloat16)
-                dq_ref[lanes, rows] = jnp.where(member, turned, dq_ref[lanes, rows])
+                dva_ref[pair] += dot_nn(soft[pair], pulled[pair])
+            for pair in range(pairs):
+                dka_ref[pair] += dot_nn(grads[pair], stacked[pair])
             return carry
 
         lax.fori_loop(low // QB, (high - 1) // QB + 1, body, 0)
@@ -158,19 +177,17 @@
             def _():
                 keys = pl.ds(pl.multiple_of(first * QB, QB), chunks * QB)
                 allowed = self_allowed(starts, query_places(block), first, chunks)
-                for pair in range(pairs):
-                    lanes = slice(pair * LANES, (pair + 1) * LANES)
-                    stacked = head_stack(q_ref[rows, lanes], 0.125)
-                    scores = jnp.where(allowed, dot_nt(k_ref[keys, lanes], stacked), -1e30)
-                    peak = jnp.max(scores, axis=0, keepdims=True)
-                    raised = jnp.exp(scores - peak)
-                    total = jnp.sum(raised, axis=0, keepdims=True)
-                    attention = (raised * (1.0 / total)).astype(jnp.bfloat16)
-                    mixed = diagonal(dot_nn(vt_ref[pair, :, keys], attention))
-                    lse = peak + jnp.log(total)
-                    o_ref[lanes, rows] = mixed.astype(jnp.bfloat16)
-                    l_ref[0, 2 * pair : 2 * pair + 1, rows] = lse[:, :QB]
-                    l_ref[0, 2 * pair + 1 : 2 * pair + 2, rows] = lse[:, QB:]
+                spans = [slice(pair * LANES, (pair + 1) * LANES) for pair in range(pairs)]
+                scores = [
+                    jnp.where(
+                        allowed, dot_nt(k_ref[keys, lanes], head_stack(q_ref[rows, lanes], 0.125)), -1e30
+                    )
+                    for lanes in spans
+                ]
+                mixed, stats = attend(scores, [vt_ref[pair, :, keys] for pair in range(pairs)])
+                for lanes, block_out in zip(spans, mixed):
+                    o_ref[lanes, rows] = block_out
+                l_ref[0, :, rows] = stats
 
         return carry
 
@@ -196,23 +213,23 @@
             def _():
                 keys = pl.ds(pl.multiple_of(first * QB, QB), chunks * QB)
                 allowed = self_allowed(starts, query_places(block), first, chunks)
+                spans = [slice(pair * LANES, (pair + 1) * LANES) for pair in range(pairs)]
+                stacked = [head_stack(q_ref[rows, lanes], 0.125) for lanes in spans]
+                pulled = [head_stack(g_ref[rows, lanes]) for lanes in spans]
+                scores = [
+                    jnp.where(allowed, dot_nt(k_ref[keys, lanes], q), -1e30)
+                    for lanes, q in zip(spans, stacked)
+                ]
+                soft, grads, turned = pull_back(
+                    scores, [v_ref[keys, lanes] for lanes in spans], pulled, l_ref[0, :, rows],
+                    [kt_ref[pair, :, keys] for pair in range(pairs)],
+                )
+                for pair, lanes in enumerate(spans):
+                    dq_ref[lanes, rows] = turned[pair]
                 for pair in range(pairs):
-                    lanes = slice(pair * LANES, (pair + 1) * LANES)
-                    stacked = head_stack(q_ref[rows, lanes], 0.125)
-                    pulled = head_stack(g_ref[rows, lanes])
-                    lse = jnp.concatenate(
-                        [l_ref[0, 2 * pair : 2 * pair + 1, rows], l_ref[0, 2 * pair + 1 : 2 * pair + 2, rows]],
-                        axis=1,
-                    )
-                    scores = jnp.where(allowed, dot_nt(k_ref[keys, lanes], stacked), -1e30)
-                    attention = jnp.exp(scores - lse)
-                    pushed = dot_nt(v_ref[keys, lanes], pulled)
-                    dva_ref[pair, keys, :] += dot_nn(attention.astype(jnp.bfloat16), pulled)
-                    inner = jnp.sum(attention * pushed, axis=0, keepdims=True)
-                    grad = (attention * (pushed - inner)).astype(jnp.bfloat16)
-                    dka_ref[pair, keys, :] += dot_nn(grad, stacked)
-                    turned = diagonal(dot_nn(kt_ref[pair, :, keys], grad) * 0.125)
-                    dq_ref[lanes, rows] = turned.astype(jnp.bfloat16)
+                    dva_ref[pair, keys, :] += dot_nn(soft[pair], pulled[pair])
+                for pair in range(pairs):
+                    dka_ref[pair, keys, :] += dot_nn(grads[pair], stacked[pair])
 
         return carry
 
@@ -241,7 +258,7 @@
     }
 
 
-def cross_forward(starts, pages, queries, keys_all, values_all, pairs=2):
+def cross_forward(starts, pages, queries, keys_all, values_all, pairs=4):
     length, width = queries.shape
     count, tokens, _ = keys_all.shape
     steps = width // (pairs * LANES)
@@ -264,7 +281,7 @@
     )(starts, pages, queries, keys_all, values_all)
 
 
-def cross_backward(starts, pages, queries, keys_all, values_all, grads, stats, pairs=2):
+def cross_backward(starts, pages, queries, keys_all, values_all, grads, stats, pairs=4):
     length, width = queries.shape
     count, tokens, _ = keys_all.shape
     steps = width // (pairs * LANES)
@@ -293,7 +310,7 @@
     )(starts, pages, queries, keys_all, values_all, grads, stats)
 
 
-def self_forward(starts, queries, keys_all, values_all, most, pairs=2):
+def self_forward(starts, queries, keys_all, values_all, most, pairs=4):
     length, width = queries.shape
     steps = width // (pairs * LANES)
     s = specs(pairs, 1)
@@ -316,7 +333,7 @@
     )(starts, queries, keys_all, values_all)
 
 
-def self_backward(starts, queries, keys_all, values_all, grads, stats, most, pairs=2):
+def self_backward(starts, queries, keys_all, values_all, grads, stats, most, pairs=4):
     length, width = queries.shape
     steps = width // (pairs * LANES)
     s = specs(pairs, 1)
@@ -357,6 +374,10 @@
     ).astype(out)
 
 
+def row_major(values):
+    return with_layout_constraint(values, Layout(major_to_minor=(0, 1)))
+
+
 def normalise(values):
     average = jnp.mean(values, axis=-1, keepdims=True)
     centered = values - average
@@ -396,32 +417,37 @@
 
 
 class Partial:
-    def __init__(self, value, sizes):
+    def __init__(self, value, sizes, blocks=1):
         dp_size, inner = sizes
-        keys, places = [], {}
+        keys, places = ["block"], {}
         for axis, size in (("dp", dp_size), ("fsdp", inner)):
             bit = size // 2
             while bit:
                 keys.append((axis, bit))
                 places[(axis, bit)] = (lax.axis_index(axis) // bit) % 2
                 bit //= 2
-        own = value.shape[0] // (dp_size * inner)
+        own = value.shape[0] // (blocks * dp_size * inner)
         self.sizes = {"dp": dp_size, "fsdp": inner}
         self.keys, self.places = keys, places
-        self.value = value.reshape((2,) * len(keys) + (own, value.shape[1]))
+        bits = (2,) * (len(keys) - 1)
+        self.terms = [value.reshape((blocks,) + bits + (own, value.shape[1]))]
+
+    def total(self, terms):
+        wide = [term.astype(jnp.float32) for term in terms]
+        return functools.reduce(jnp.add, wide)
 
     def send(self, key):
         axis = self.keys.index(key)
         self.keys.remove(key)
-        out = pick(self.value, 1 - self.places[key], axis).astype(jnp.bfloat16)
-        self.value = pick(self.value, self.places[key], axis).astype(jnp.float32)
-        return swap(out, key[0], self.sizes[key[0]], key[1])
+        out = self.total([pick(term, 1 - self.places[key], axis) for term in self.terms])
+        self.terms = [pick(term, self.places[key], axis) for term in self.terms]
+        return swap(out.astype(jnp.bfloat16), key[0], self.sizes[key[0]], key[1])
 
     def take(self, received):
-        self.value = self.value + received.astype(jnp.float32)
+        self.terms.append(received)
 
     def rest(self):
-        return self.value.astype(jnp.bfloat16)
+        return self.total(self.terms).astype(jnp.bfloat16)
 
 
 CORE = ("dp", 1)
@@ -433,12 +459,14 @@
     rests = []
     for part in parts:
         rest = part.rest()
-        own, columns = rest.shape[-2:]
-        rests.append(rest.reshape(inner, own, columns))
+        blocks, (own, columns) = rest.shape[0], rest.shape[-2:]
+        rest = rest.reshape(blocks, inner, own, columns).transpose(1, 0, 2, 3)
+        rests.append(rest.reshape(inner, blocks * own, columns))
     packed = rests[0] if len(rests) == 1 else jnp.concatenate(rests, axis=1)
     summed = lax.psum_scatter(
         packed.reshape(-1, columns), "fsdp", scatter_dimension=0, tiled=True
     ).astype(jnp.float32)
+    own = summed.shape[0] // len(parts)
     return [summed[i * own : (i + 1) * own] for i in range(len(parts))]
 
 
@@ -465,11 +493,23 @@
     offset = (lax.axis_index("dp") * inner + lax.axis_index("fsdp")) * mine
     spread = lax.dynamic_update_slice(jnp.zeros((6, width), jnp.float32), norms, (0, offset))
     norms = butterfly_sum(spread, axes)
-    w_sqkv = gather(self_query, self_key, self_value)
-    w_rest = gather(self_out, cross_query, cross_key, cross_value, cross_out)
-    w_in = lax.all_gather(turned(mlp_in), AXES, axis=0, tiled=True)
-    w_out = lax.all_gather(turned(mlp_out), AXES, axis=0, tiled=True)
-    w_so, w_cq, w_ck, w_cv, w_co = [w_rest[i] for i in range(5)]
+    near = gather(
+        self_query, self_key, self_value, self_out, cross_query, cross_key, cross_value, cross_out
+    )
+    w_sqkv, w_kv = near[:3], near[5:7]
+    w_so, w_cq, w_ck, w_cv, w_co = [near[i] for i in range(3, 8)]
+    own, devices = mlp_out.shape[1], dp_size * inner
+    blocks = mlp_out.shape[0] // width
+    step = width // devices
+    in_rows = turned(mlp_in).reshape(blocks, step, width)
+    out_rows = turned(mlp_out).reshape(own, devices, blocks, step).transpose(2, 0, 1, 3)
+    far = jnp.concatenate([in_rows, out_rows.reshape(blocks, own, width)])
+    far = lax.all_gather(far, AXES, axis=1, tiled=True)
+    (far,) = fence(far.reshape(2, blocks * width, width))
+    w_in = far[0]
+    w_out = jnp.concatenate(
+        [far[1, i * width : (i + 1) * width] for i in range(blocks)], axis=1
+    )
 
     starts = jnp.sum(
         segment_ids[0][None, :] < jnp.arange(page_map.shape[1] + 1, dtype=jnp.int32)[:, None],
@@ -482,13 +522,13 @@
     a1 = (normalise(rows)[0] * norms[0] + norms[1]).astype(low)
     sq, sk, sv = [contract(a1, w_sqkv[i], (1,), (1,), low) for i in range(3)]
     so, s_stats = self_forward(starts, sq, sk, sv, most)
-    x1 = rows + contract(so, w_so, (0,), (1,))
+    x1 = row_major(rows + contract(so, w_so, (0,), (1,)))
     a2 = (normalise(x1)[0] * norms[2] + norms[3]).astype(low)
     cq = contract(a2, w_cq, (1,), (1,), low)
     ck = contract(images, w_ck, (2,), (1,), low)
     cv = contract(images, w_cv, (2,), (1,), low)
     co, c_stats = cross_forward(starts, pages, cq, ck, cv)
-    x2 = x1 + contract(co, w_co, (0,), (1,))
+    x2 = row_major(x1 + contract(co, w_co, (0,), (1,)))
     a3 = (normalise(x2)[0] * norms[4] + norms[5]).astype(low)
     u = contract(a3, w_in, (1,), (1,))
     phi = 0.5 * (1.0 + lax.erf(u * ROOT_HALF))
@@ -507,7 +547,7 @@
     flying = p_out.send(ACROSS)
     g_in = contract(du, a3, (0,), (0,), low)
     du, g_in = fence(du, g_in)
-    p_in = Partial(g_in, sizes)
+    p_in = Partial(g_in, sizes, blocks)
     flying_in = p_in.send(CORE)
     d3 = contract(du, w_in, (1,), (0,))
     back, gg3, gs3 = norm_back(x2, norms[4], d3)
@@ -575,7 +615,7 @@
         both = jnp.concatenate([dck, dcv], axis=2).transpose(1, 0, 2)
         tokens, count, _ = both.shape
         flat = contract(
-            both.reshape(tokens * count, 2 * width), w_rest[2:4].reshape(2 * width, width), (1,), (0,)
+            both.reshape(tokens * count, 2 * width), w_kv.reshape(2 * width, width), (1,), (0,)
         )
         return flat.reshape(tokens, count, width).transpose(1, 0, 2)
 
@@ -596,10 +636,10 @@
             fenced = fence(*(flights + list(waits)))
         for p, f in zip(parts, fenced):
             p.take(f)
-        parts = [p for p in parts if len(p.keys)]
+        parts = [p for p in parts if len(p.keys) > 1]
         flights = [p.send(o[stage]) for p, o in zip(p_self, orders)]
-        if len(p_so.keys):
-            flights.append(p_so.send(p_so.keys[-1] if len(p_so.keys) == 1 else keys[stage + 2]))
+        if len(p_so.keys) > 1:
+            flights.append(p_so.send(keys[stage + 2]))
         if stage < 3:
             done = job(*needs)
             waits = jax.tree.leaves(done)[:1]
@@ -608,9 +648,11 @@
         p.take(f)
     grad_in, gg1, gs1 = results[0]
     block_out, grad_images = results[1], results[2]
-    g_self = [p.value for p in p_self + [p_so]]
+    g_self = [p.total(p.terms)[0] for p in p_self + [p_so]]
     norm_grads = butterfly_sum(jnp.stack([gg1, gs1, gg2, gs2, gg3, gs3]), axes)
     norm_grads = lax.dynamic_slice(norm_grads, (0, offset), (6, mine))
+    g_mlp_out = g_mlp_out.reshape(own, blocks, devices, step).transpose(0, 2, 1, 3)
+    g_mlp_out = g_mlp_out.reshape(own, -1)
     weight_grads = [g.T for g in g_self + g_cross + [g_mlp_in, g_mlp_out]]
     return (
         block_out[None], grad_in[None], grad_images, *[norm_grads[i] for i in range(6)],

time: 821 us -> 720 us (0.88)
  Pallas kernels: 176 us -> 134 us
  local copies, waits for them, and re-layouts: 85.8 us -> 61.6 us
  waiting for transfers between devices: 160 us -> 142 us
  starting transfers between devices: 56.9 us -> 43.7 us
    convert_element_type x6 -> x28, other arithmetic: 14.6 us -> 55.1 us  [the longest x22 39.8 us: send(): return swap(out.astype(jnp.bfloat16), key[0], self.sizes[key[0]], key[1])]
    all_gather x2 -> x1, waiting for transfers between devices: 38.8 us -> 11.2 us  [layer(): far = lax.all_gather(far, AXES, axis=1, tiled=True)]
    add x22 -> x0, other arithmetic: 24.2 us -> none  [take(): self.value = self.value + received.astype(jnp.float32)]
    pallas_call x1, Pallas kernels: 55.7 us -> 31.9 us  [cross_forward(): pl.pallas_call(functools.partial(cross_forward_kernel, pairs), out_shape=...]
    pallas_call x1, Pallas kernels: 32.2 us -> 19.2 us  [self_forward(): pl.pallas_call(functools.partial(self_forward_kernel, pairs, most), out_s...]
    ppermute x42, starting transfers between devices: 56.2 us -> 43.3 us  [swap(): return lax.ppermute(value, axis, [(i, i ^ bit) for i in range(size)])]
    convert_element_type x22 -> x2, local copies, waits for them, and re-layouts: 12.7 us -> 1.6 us  [the longest x1 1.58 us: rest(): return self.total(self.terms).astype(jnp.bfloat16)]
    dot_general x2 -> x0, local copies, waits for them, and re-layouts: 10.7 us -> none  [contract(): lax.dot_general(a, b, ((left, right), ((), ())), preferred_element_type=j...]
  transfers between devices with their start and end apart: 49 -> 47, of which waited for: 16 -> 11; matrix products, arithmetic and copies ran while one was open for 45% -> 42% of each run, Pallas kernels for 22% -> 19%
where the time goes in v3:
time: 720 us; the launch traced here: 710 us
  matrix products  222 us (31%)
  waiting for transfers between devices  142 us (20%)
  Pallas kernels  134 us (19%)
  other arithmetic  91 us (13%)
  local copies, waits for them, and re-layouts  61.6 us (9%)
  starting transfers between devices  43.7 us (6%)
  between operations  15.8 us (2%)
    dot_general x29, matrix products, contract(): lax.dot_general(a, b, ((left, right), ((), ())), preferred_element_type=j...  222 us
    all_gather x1, waiting for transfers between devices, gather(): return lax.all_gather(stacked, AXES, axis=1, tiled=True)  88.1 us
    pallas_call x1, Pallas kernels, cross_backward(): pl.pallas_call(functools.partial(cross_backward_kernel, pairs), out_shape...  54.3 us
    ppermute x42, starting transfers between devices, swap(): return lax.ppermute(value, axis, [(i, i ^ bit) for i in range(size)])  43.3 us
    ppermute x42, waiting for transfers between devices, swap(): return lax.ppermute(value, axis, [(i, i ^ bit) for i in range(size)])  43 us
    convert_element_type x22, other arithmetic, send(): return swap(out.astype(jnp.bfloat16), key[0], self.sizes[key[0]], key[1])  39.8 us
    unnamed x175, local copies, waits for them, and re-layouts  32.5 us
    pallas_call x1, Pallas kernels, cross_forward(): pl.pallas_call(functools.partial(cross_forward_kernel, pairs), out_shape=...  31.9 us
  transfers between devices with their start and end apart: 47, of which 11 were waited for; matrix products, arithmetic and copies ran while one was open for 42% of the time, Pallas kernels for 19%

profile of v3, /device:TPU:0, one launch (start us, length us, event | category | flops | bytes accessed | tf_op | source)
XLA Modules:
  0.0 710.4 jit_solution(1890384284334596278)
XLA Ops:
  44.8 88.1 %all-gather.3.cloned.1.call-done = bf16[8,1024,1024]{2,1,0:T(8,128)(2,1)} async-done(((bf16[8,32,1024]{2,1,0:T(8,128)(2,1)}), bf16[8,1024,1024]{2,1,0:T(8,128)(2,1)}) %all-gather.3.cloned.1.call-update) | async-done | bytes 16777232 | tf_op jit(solution)/shard_map/all_gather | solution.py:488
  132.9 5.4 convolution_convert_fusion.11.v_ref
  147.5 19.2 %self_forward.1 = (bf16[1024,1024]{1,0:T(8,128)(2,1)}, f32[2,8,1024]{2,1,0:T(8,128)}) custom-call(s32[5]{0:T(128)} %convert_reduce_fusion.1.starts, bf16[1024,1024]{1,0:T(8,128)(2,1)} %convolution_convert_fusion.13.q_ref, bf16[1024,1024]{1,0:T(8,128)(2,1)} %convolution_convert_fusion.12.k_ref, bf16[1024,1024]{1,0:T(8,128)(2,1)} %convolution_convert_fusion.11.v_ref), custom_call_target="tpu_custom_call" | custom-call | flops 5368709120 | bytes 10485760 | tf_op jit(solution)/shard_map/self_forward/pallas_call | solution.py:318
  173.6 6.2 convolution_convert_fusion.10.q_ref
  181.6 7.6 %convert_bitcast_fusion.1.v_ref = bf16[4,588,1024]{2,1,0:T(8,128)(2,1)} fusion(bf16[4,588,1024]{2,0,1:T(4,128)(2,1)S(1)} %bitcast.706, bf16[8,1024,1024]{2,1,0:T(8,128)(2,1)S(1)} %bitcast.623), kind=kOutput, calls=%fused_computation.30 | convolution fusion | flops 4934909952 | bytes 11730944 | tf_op jit(solution)/shard_map/dot_general | solution.py:372
  189.2 7.9 %convert_bitcast_fusion.2.k_ref = bf16[4,588,1024]{2,1,0:T(8,128)(2,1)} fusion(bf16[4,588,1024]{2,0,1:T(4,128)(2,1)S(1)} %bitcast.706, bf16[8,1024,1024]{2,1,0:T(8,128)(2,1)S(1)} %bitcast.623), kind=kOutput, calls=%fused_computation.31 | convolution fusion | flops 4934909952 | bytes 11730944 | tf_op jit(solution)/shard_map/dot_general | solution.py:372
  197.1 31.9 %cross_forward.1 = (bf16[1024,1024]{1,0:T(8,128)(2,1)}, f32[2,8,1024]{2,1,0:T(8,128)}) custom-call(s32[5]{0:T(128)} %convert_reduce_fusion.1.starts, s32[4]{0:T(128)} %bitcast.709, bf16[1024,1024]{1,0:T(8,128)(2,1)} %convolution_convert_fusion.10.q_ref, bf16[4,588,1024]{2,1,0:T(8,128)(2,1)} %convert_bitcast_fusion.2.k_ref, ...), custom_call_target="tpu_custom_call" | custom-call | flops 13564379136 | bytes 20971520 | tf_op jit(solution)/shard_map/cross_forward/pallas_call | solution.py:266
  229.0 6.0 fusion.110
  237.7 11.2 %all-gather.5.cloned.1.call-done = bf16[8,1024,1024]{2,1,0:T(8,128)(2,1)} async-done(((bf16[8,32,1024]{2,1,0:T(8,128)(2,1)}), bf16[8,1024,1024]{2,1,0:T(8,128)(2,1)}) %all-gather.5.cloned.1.call-update) | async-done | bytes 16777232 | tf_op jit(solution)/shard_map/all_gather | solution.py:507
  249.0 18.7 %multiply_convert_fusion.1 = (bf16[1024,4096]{1,0:T(8,128)(2,1)}, f32[1024,4096]{1,0:T(8,128)}) fusion(bf16[2,4096,1024]{2,1,0:T(8,128)(2,1)} %bitcast.617, f32[1024,1024]{1,0:T(8,128)} %copy-done.4, f32[1024]{0:T(1024)S(1)} %bitcast.702, f32[1024]{0:T(1024)S(1)} %bitcast.686, f32[1024]{0:T(1024)S(1)} %add_rsqrt_fusion, f32[1024]{0:T(1024)S(1)} %broadcast_multiply_fusion.6), kind=kOutput, calls=%fused_computation.7 | convolution fusion | flops 8616148992 | bytes 37765120 | tf_op jit(solution)/shard_map/dot_general | solution.py:372
  267.7 13.1 %convolution_convert_fusion.1 = bf16[4096,1024]{0,1:T(8,128)(2,1)S(1)} fusion(bf16[1024,4096]{1,0:T(8,128)(2,1)} %get-tuple-element.137, bf16[1,1024,1024]{2,1,0:T(8,128)(2,1)} %param.41), kind=kOutput, calls=%fused_computation.16 | convolution fusion | flops 8594128896 | bytes 18874368 | tf_op jit(solution)/shard_map/dot_general | solution.py:372
  289.0 20.7 %multiply_convert_fusion = bf16[1024,4096]{1,0:T(8,128)(2,1)} fusion(bf16[1024,1024]{1,0:T(8,128)(2,1)} %bitcast.669, f32[1024,4096]{1,0:T(8,128)} %get-tuple-element.274, bf16[1024,1024]{1,0:T(8,128)(2,1)} %get-tuple-element.250, bf16[1024,1024]{1,0:T(8,128)(2,1)} %get-tuple-element.251, bf16[1024,1024]{1,0:T(8,128)(2,1)} %get-tuple-element.252, ...), kind=kOutput, calls=%fused_computation.6 | convolution fusion | flops 8673820672 | bytes 35651584 | tf_op jit(solution)/shard_map/dot_general | solution.py:372
  309.7 12.2 %convolution_convert_fusion = bf16[4096,1024]{1,0:T(8,128)(2,1)S(1)} fusion(bf16[1024,4096]{1,0:T(8,128)(2,1)} %multiply_convert_fusion, f32[1024,1024]{1,0:T(8,128)S(1)} %copy-done.5, f32[1024]{0:T(1024)S(1)} %bitcast.703, f32[1024]{0:T(1024)S(1)} %bitcast.687, f32[1024]{0:T(1024)S(1)} %add_rsqrt_fusion, f32[1024]{0:T(1024)S(1)} %broadcast_multiply_fusion.6), kind=kOutput, calls=%fused_computation.15 | convolution fusion | flops 8599371776 | bytes 20987904 | tf_op jit(solution)/shard_map/dot_general | solution.py:372
  331.1 15.6 %multiply_reduce_fusion = (f32[1024]{0:T(1024)}, f32[1024]{0:T(1024)S(1)}, f32[1024]{0:T(1024)S(1)}, f32[1024]{0:T(1024)}, f32[1024,1024]{1,0:T(8,128)S(1)}) fusion(f32[1024,1024]{1,0:T(8,128)S(1)} %copy-done.6, f32[1024]{0:T(1024)S(1)} %add_rsqrt_fusion, f32[1024]{0:T(1024)S(1)} %broadcast_multiply_fusion.6, f32[1024]{0:T(1024)S(1)} %bitcast.688, ...), kind=kOutput, calls=%fused_computation.57 | convolution fusion | flops 8599367680 | bytes 25194496 | tf_op jit(solution)/shard_map/dot_general | solution.py:372
  350.3 27.3 %collective-permute-done.6 = bf16[1,2,2,2,32,4096]{5,4,3,2,1,0:T(8,128)(2,1)S(1)} collective-permute-done((bf16[1,2,2,2,32,4096]{5,4,3,2,1,0:T(8,128)(2,1)S(1)}, bf16[1,2,2,2,32,4096]{5,4,3,2,1,0:T(8,128)(2,1)S(1)}, u32[]{:S(2)}, u32[]{:S(2)}) %collective-permute-start.6) | collective-permute-done | bytes 2097184 | tf_op jit(solution)/shard_map/ppermute | solution.py:399
  388.3 5.9 convolution_convert_fusion.7
  399.5 54.3 %cross_backward.1 = (bf16[1024,1024]{1,0:T(8,128)(2,1)}, bf16[4,588,1024]{2,1,0:T(8,128)(2,1)}, bf16[4,588,1024]{2,1,0:T(8,128)(2,1)}) custom-call(s32[5]{0:T(128)} %convert_reduce_fusion.1.starts, s32[4]{0:T(128)} %bitcast.710, bf16[1024,1024]{1,0:T(8,128)(2,1)} %convolution_convert_fusion.10.q_ref, bf16[4,588,1024]{2,1,0:T(8,128)(2,1)} %convert_bitcast_fusion.2.k_ref, ...), custom_call_target="tpu_custom_call" | custom-call | flops 33910947840 | bytes 31457280 | tf_op jit(solution)/shard_map/cross_backward/pallas_call | solution.py:290
  463.6 6.2 bitcast_convert_fusion
  469.9 6.3 bitcast_convert_fusion.1
  481.9 7.3 %multiply_reduce_fusion.1 = (f32[1024]{0:T(1024)S(1)}, f32[1024]{0:T(1024)S(1)}, f32[1024]{0:T(1024)S(1)}, f32[1024]{0:T(1024)S(1)}, f32[1024,1024]{1,0:T(8,128)S(1)}) fusion(f32[1024,1024]{1,0:T(8,128)} %copy-done.7, f32[1024]{0:T(1024)S(1)} %copy-done.41, f32[1024]{0:T(1024)S(1)} %copy-done.37, f32[1024]{0:T(1024)S(1)} %bitcast.682, ...), kind=kOutput, calls=%fused_computation.58 | convolution fusion | flops 2156916736 | bytes 12611584 | tf_op jit(solution)/shard_map/dot_general | solution.py:372
  512.1 28.7 %self_backward.1 = (bf16[1024,1024]{1,0:T(8,128)(2,1)}, bf16[1024,1024]{1,0:T(8,128)(2,1)}, bf16[1024,1024]{1,0:T(8,128)(2,1)}) custom-call(s32[5]{0:T(128)} %convert_reduce_fusion.1.starts, bf16[1024,1024]{1,0:T(8,128)(2,1)} %convolution_convert_fusion.13.q_ref, bf16[1024,1024]{1,0:T(8,128)(2,1)} %convolution_convert_fusion.12.k_ref, ...), custom_call_target="tpu_custom_call" | custom-call | flops 13421772800 | bytes 16777216 | tf_op jit(solution)/shard_map/self_backward/pallas_call | solution.py:341
  636.3 15.3 %add_convert_fusion = bf16[1024,1024]{1,0:T(8,128)(2,1)} fusion(f32[1024,1024]{1,0:T(8,128)} %copy-done.4, bf16[1024,4096]{1,0:T(8,128)(2,1)} %get-tuple-element.137, bf16[1024,1024]{1,0:T(8,128)(2,1)} %get-tuple-element.250, bf16[1024,1024]{1,0:T(8,128)(2,1)} %get-tuple-element.251, bf16[1024,1024]{1,0:T(8,128)(2,1)} %get-tuple-element.252, ...), kind=kOutput, calls=%fused_computation.59 | convolution fusion | flops 8625586176 | bytes 23068672 | tf_op jit(solution)/shard_map/dot_general | solution.py:372
  658.8 15.5 %fusion.36 = f32[4,588,1024]{2,1,0:T(8,128)} fusion(bf16[2048,1024,1]{1,0,2:T(8,128)(2,1)S(1)} %bitcast.628, bf16[4,588,1024]{2,1,0:T(8,128)(2,1)} %get-tuple-element.143, bf16[4,588,1024]{2,1,0:T(8,128)(2,1)} %get-tuple-element.142), kind=kOutput, calls=%fused_computation.75 | convolution fusion | flops 9884270592 | bytes 23461888 | tf_op jit(solution)/shard_map/dot_general | solution.py:372
  674.2 13.8 %copy.160 = f32[4,588,1024]{2,0,1:T(4,128)} copy(f32[4,588,1024]{2,1,0:T(8,128)} %fusion.36) | data formatting | bytes 19267584
  (400 shorter events, 250.4 us)
Async XLA Ops:
  7.2 125.7 %all-gather.3.cloned.1.call-start = ((), (), s32[]{:S(2)}) async-start(), calls=%async_computation.3 | async-start | bytes 17301504 | tf_op jit(solution)/shard_map/all_gather | solution.py:488
  15.4 233.6 %all-gather.5.cloned.1.call-start = ((), (), s32[]{:S(2)}) async-start(), calls=%async_computation.4 | async-start | bytes 17301504 | tf_op jit(solution)/shard_map/all_gather | solution.py:507
  22.9 518.0 %reduce-scatter.8.cloned.1.call-start = ((), (), s32[]{:S(2)}) async-start(), calls=%async_computation.7 | async-start | bytes 2359296 | tf_op jit(solution)/shard_map/reduce_scatter | solution.py:466
  285.3 24.3 %collective-permute-start.5 = (bf16[1,2,2,2,2,32,4096]{6,5,4,3,2,1,0:T(8,128)(2,1)}, bf16[1,2,2,2,2,32,4096]{6,5,4,3,2,1,0:T(8,128)(2,1)}, u32[]{:S(2)}, u32[]{:S(2)}) collective-permute-start(bf16[1,2,2,2,2,32,4096]{6,5,4,3,2,1,0:T(8,128)(2,1)} %dynamic-slice_bitcast_fusion), channel_id=1, source_target_pairs={{0,8},{8,0},{16,24},{24,16},{1,9},{9,1},{17,25},{25,17},{2,10},{10... | collective-permute-start | bytes 12582920 | tf_op jit(solution)/shard_map/ppermute | solution.py:399
  326.3 51.3 %collective-permute-start.7 = (bf16[4,2,2,2,2,32,1024]{6,5,4,3,2,0,1:T(8,128)(2,1)}, bf16[4,2,2,2,2,32,1024]{6,5,4,3,2,0,1:T(8,128)(2,1)}, u32[]{:S(2)}, u32[]{:S(2)}) collective-permute-start(bf16[4,2,2,2,2,32,1024]{6,5,4,3,2,0,1:T(8,128)(2,1)} %copy_bitcast_fusion), channel_id=1, source_target_pairs={{0,8},{8,0},{16,24},{24,16},{1,9},{9,1},{17,25},{25,17},{2,10},{10... | collective-permute-start | bytes 12582920 | tf_op jit(solution)/shard_map/ppermute | solution.py:399
  329.7 47.9 %collective-permute-start.6 = (bf16[1,2,2,2,32,4096]{5,4,3,2,1,0:T(8,128)(2,1)S(1)}, bf16[1,2,2,2,32,4096]{5,4,3,2,1,0:T(8,128)(2,1)S(1)}, u32[]{:S(2)}, u32[]{:S(2)}) collective-permute-start(bf16[1,2,2,2,32,4096]{5,4,3,2,1,0:T(8,128)(2,1)S(1)} %fusion.35), channel_id=1, source_target_pairs={{0,16},{8,24},{16,0},{24,8},{1,17},{9,25},{17,1},{25,9},{2,18},{10... | collective-permute-start | bytes 6291464 | tf_op jit(solution)/shard_map/ppermute | solution.py:399
  382.2 242.1 %reduce-scatter.6.cloned.1.call-start = ((), (), s32[]{:S(2)}) async-start(), calls=%async_computation.6 | async-start | bytes 2359296 | tf_op jit(solution)/shard_map/reduce_scatter | solution.py:466
  387.0 66.8 %collective-permute-start.8 = (bf16[4,2,2,2,32,1024]{5,4,3,2,1,0:T(8,128)(2,1)}, bf16[4,2,2,2,32,1024]{5,4,3,2,1,0:T(8,128)(2,1)S(1)}, u32[]{:S(2)}, u32[]{:S(2)}) collective-permute-start(bf16[4,2,2,2,32,1024]{5,4,3,2,1,0:T(8,128)(2,1)} %fusion.34), channel_id=1, source_target_pairs={{0,16},{8,24},{16,0},{24,8},{1,17},{9,25},{17,1},{25,9},{2,18},{10... | collective-permute-start | bytes 6291464 | tf_op jit(solution)/shard_map/ppermute | solution.py:399
  481.7 220.0 %reduce-scatter.4.cloned.1.call-start = ((), (), s32[]{:S(2)}) async-start(), calls=%async_computation.5 | async-start | bytes 2359296 | tf_op jit(solution)/shard_map/reduce_scatter | solution.py:466
  495.1 54.8 %collective-permute-start.17 = (bf16[1,2,2,2,32,1024]{5,4,3,2,1,0:T(8,128)(2,1)}, bf16[1,2,2,2,32,1024]{5,4,3,2,1,0:T(8,128)(2,1)}, u32[]{:S(2)}, u32[]{:S(2)}) collective-permute-start(bf16[1,2,2,2,32,1024]{5,4,3,2,1,0:T(8,128)(2,1)} %fusion.70), channel_id=1, source_target_pairs={{0,16},{8,24},{16,0},{24,8},{1,17},{9,25},{17,1},{25,9},{2,18},{10... | collective-permute-start | bytes 1572872 | tf_op jit(solution)/shard_map/ppermute | solution.py:399
  497.5 52.5 %collective-permute-start.16 = (bf16[1,2,2,2,32,1024]{5,4,3,2,1,0:T(8,128)(2,1)}, bf16[1,2,2,2,32,1024]{5,4,3,2,1,0:T(8,128)(2,1)}, u32[]{:S(2)}, u32[]{:S(2)}) collective-permute-start(bf16[1,2,2,2,32,1024]{5,4,3,2,1,0:T(8,128)(2,1)} %fusion.71), channel_id=1, source_target_pairs={{0,16},{8,24},{16,0},{24,8},{1,17},{9,25},{17,1},{25,9},{2,18},{10... | collective-permute-start | bytes 1572872 | tf_op jit(solution)/shard_map/ppermute | solution.py:399
  501.6 48.4 %collective-permute-start.15 = (bf16[1,2,2,2,32,1024]{5,4,3,2,1,0:T(8,128)(2,1)}, bf16[1,2,2,2,32,1024]{5,4,3,2,1,0:T(8,128)(2,1)}, u32[]{:S(2)}, u32[]{:S(2)}) collective-permute-start(bf16[1,2,2,2,32,1024]{5,4,3,2,1,0:T(8,128)(2,1)} %fusion.72), channel_id=1, source_target_pairs={{0,16},{8,24},{16,0},{24,8},{1,17},{9,25},{17,1},{25,9},{2,18},{10... | collective-permute-start | bytes 1572872 | tf_op jit(solution)/shard_map/ppermute | solution.py:399
  503.9 46.0 %collective-permute-start.14 = (bf16[1,2,2,2,32,1024]{5,4,3,2,1,0:T(8,128)(2,1)}, bf16[1,2,2,2,32,1024]{5,4,3,2,1,0:T(8,128)(2,1)}, u32[]{:S(2)}, u32[]{:S(2)}) collective-permute-start(bf16[1,2,2,2,32,1024]{5,4,3,2,1,0:T(8,128)(2,1)} %fusion.73), channel_id=1, source_target_pairs={{0,16},{8,24},{16,0},{24,8},{1,17},{9,25},{17,1},{25,9},{2,18},{10... | collective-permute-start | bytes 1572872 | tf_op jit(solution)/shard_map/ppermute | solution.py:399
  508.3 41.6 %collective-permute-start.13 = (bf16[1,2,2,2,2,32,1024]{6,5,4,3,2,1,0:T(8,128)(2,1)S(1)}, bf16[1,2,2,2,2,32,1024]{6,5,4,3,2,1,0:T(8,128)(2,1)}, u32[]{:S(2)}, u32[]{:S(2)}) collective-permute-start(bf16[1,2,2,2,2,32,1024]{6,5,4,3,2,1,0:T(8,128)(2,1)S(1)} %dynamic-slice_bitcast_fusion.4), channel_id=1, source_target_pairs={{0,8},{8,0},{16,24},{24,16},{1,9},{9,1},{17,25},{25,17},{2,10},{10... | collective-permute-start | bytes 3145736 | tf_op jit(solution)/shard_map/ppermute | solution.py:399
  551.4 21.2 %collective-permute-start.18 = (bf16[1,2,2,2,32,1024]{5,4,3,2,1,0:T(8,128)(2,1)S(1)}, bf16[1,2,2,2,32,1024]{5,4,3,2,1,0:T(8,128)(2,1)S(1)}, u32[]{:S(2)}, u32[]{:S(2)}) collective-permute-start(bf16[1,2,2,2,32,1024]{5,4,3,2,1,0:T(8,128)(2,1)S(1)} %fusion.69), channel_id=1, source_target_pairs={{0,16},{8,24},{16,0},{24,8},{1,17},{9,25},{17,1},{25,9},{2,18},{10... | collective-permute-start | bytes 1572872 | tf_op jit(solution)/shard_map/ppermute | solution.py:399
  596.7 29.7 %collective-permute-start.26 = (bf16[1,2,32,1024]{3,2,1,0:T(8,128)(2,1)}, bf16[1,2,32,1024]{3,2,1,0:T(8,128)(2,1)}, u32[]{:S(2)}, u32[]{:S(2)}) collective-permute-start(bf16[1,2,32,1024]{3,2,1,0:T(8,128)(2,1)} %fusion.81), channel_id=1, source_target_pairs={{0,2},{1,3},{2,0},{3,1},{4,6},{5,7},{6,4},{7,5},{8,10},{9,11},{10,... | collective-permute-start | bytes 393224 | tf_op jit(solution)/shard_map/ppermute | solution.py:399
  601.4 25.0 %collective-permute-start.25 = (bf16[1,2,2,2,32,1024]{5,4,3,2,1,0:T(8,128)(2,1)}, bf16[1,2,2,2,32,1024]{5,4,3,2,1,0:T(8,128)(2,1)}, u32[]{:S(2)}, u32[]{:S(2)}) collective-permute-start(bf16[1,2,2,2,32,1024]{5,4,3,2,1,0:T(8,128)(2,1)} %fusion.66), channel_id=1, source_target_pairs={{0,2},{1,3},{2,0},{3,1},{4,6},{5,7},{6,4},{7,5},{8,10},{9,11},{10,... | collective-permute-start | bytes 1572872 | tf_op jit(solution)/shard_map/ppermute | solution.py:399
  606.5 19.8 %collective-permute-start.24 = (bf16[1,2,2,2,32,1024]{5,4,3,2,1,0:T(8,128)(2,1)}, bf16[1,2,2,2,32,1024]{5,4,3,2,1,0:T(8,128)(2,1)}, u32[]{:S(2)}, u32[]{:S(2)}) collective-permute-start(bf16[1,2,2,2,32,1024]{5,4,3,2,1,0:T(8,128)(2,1)} %fusion.67), channel_id=1, source_target_pairs={{0,1},{1,0},{2,3},{3,2},{4,5},{5,4},{6,7},{7,6},{8,9},{9,8},{10,11... | collective-permute-start | bytes 1572872 | tf_op jit(solution)/shard_map/ppermute | solution.py:399
  627.4 24.2 %collective-permute-start.30 = (bf16[1,32,1024]{2,1,0:T(8,128)(2,1)S(1)}, bf16[1,32,1024]{2,1,0:T(8,128)(2,1)S(1)}, u32[]{:S(2)}, u32[]{:S(2)}) collective-permute-start(bf16[1,32,1024]{2,1,0:T(8,128)(2,1)S(1)} %fusion.93), channel_id=1, source_target_pairs={{0,4},{1,5},{2,6},{3,7},{4,0},{5,1},{6,2},{7,3},{8,12},{9,13},{10,... | collective-permute-start | bytes 196616 | tf_op jit(solution)/shard_map/ppermute | solution.py:399
  628.8 22.9 %collective-permute-start.29 = (bf16[1,2,2,32,1024]{4,3,2,1,0:T(8,128)(2,1)S(1)}, bf16[1,2,2,32,1024]{4,3,2,1,0:T(8,128)(2,1)}, u32[]{:S(2)}, u32[]{:S(2)}) collective-permute-start(bf16[1,2,2,32,1024]{4,3,2,1,0:T(8,128)(2,1)S(1)} %fusion.74), channel_id=1, source_target_pairs={{0,4},{1,5},{2,6},{3,7},{4,0},{5,1},{6,2},{7,3},{8,12},{9,13},{10,... | collective-permute-start | bytes 786440 | tf_op jit(solution)/shard_map/ppermute | solution.py:399
  632.9 18.9 %collective-permute-start.28 = (bf16[1,2,2,32,1024]{4,3,2,1,0:T(8,128)(2,1)S(1)}, bf16[1,2,2,32,1024]{4,3,2,1,0:T(8,128)(2,1)}, u32[]{:S(2)}, u32[]{:S(2)}) collective-permute-start(bf16[1,2,2,32,1024]{4,3,2,1,0:T(8,128)(2,1)S(1)} %fusion.75), channel_id=1, source_target_pairs={{0,2},{1,3},{2,0},{3,1},{4,6},{5,7},{6,4},{7,5},{8,10},{9,11},{10,... | collective-permute-start | bytes 786440 | tf_op jit(solution)/shard_map/ppermute | solution.py:399
  652.9 36.8 %collective-permute-start.38 = (bf16[1,2,32,1024]{3,2,1,0:T(8,128)(2,1)S(1)}, bf16[1,2,32,1024]{3,2,1,0:T(8,128)(2,1)S(1)}, u32[]{:S(2)}, u32[]{:S(2)}) collective-permute-start(bf16[1,2,32,1024]{3,2,1,0:T(8,128)(2,1)S(1)} %fusion.78), channel_id=1, source_target_pairs={{0,16},{8,24},{16,0},{24,8},{1,17},{9,25},{17,1},{25,9},{2,18},{10... | collective-permute-start | bytes 393224 | tf_op jit(solution)/shard_map/ppermute | solution.py:399
  655.6 34.1 %collective-permute-start.37 = (bf16[1,2,32,1024]{3,2,1,0:T(8,128)(2,1)S(1)}, bf16[1,2,32,1024]{3,2,1,0:T(8,128)(2,1)S(1)}, u32[]{:S(2)}, u32[]{:S(2)}) collective-permute-start(bf16[1,2,32,1024]{3,2,1,0:T(8,128)(2,1)S(1)} %fusion.79), channel_id=1, source_target_pairs={{0,4},{1,5},{2,6},{3,7},{4,0},{5,1},{6,2},{7,3},{8,12},{9,13},{10,... | collective-permute-start | bytes 393224 | tf_op jit(solution)/shard_map/ppermute | solution.py:399
  656.8 32.9 %collective-permute-start.36 = (bf16[1,2,32,1024]{3,2,1,0:T(8,128)(2,1)S(1)}, bf16[1,2,32,1024]{3,2,1,0:T(8,128)(2,1)S(1)}, u32[]{:S(2)}, u32[]{:S(2)}) collective-permute-start(bf16[1,2,32,1024]{3,2,1,0:T(8,128)(2,1)S(1)} %fusion.80), channel_id=1, source_target_pairs={{0,2},{1,3},{2,0},{3,1},{4,6},{5,7},{6,4},{7,5},{8,10},{9,11},{10,... | collective-permute-start | bytes 393224 | tf_op jit(solution)/shard_map/ppermute | solution.py:399
  (110 other events, 1560.3 us)
Sparse Core Ops, SparseCore 0:
  15.5 117.3 all-gather.2
  136.5 112.4 all-gather.4
  382.4 66.7 reduce-scatter.7
  481.8 66.8 reduce-scatter.5
  568.2 80.8 reduce-scatter.3

commit v4 on v3

--- a/solution.py
+++ b/solution.py
@@ -417,20 +417,19 @@
 
 
 class Partial:
-    def __init__(self, value, sizes, blocks=1):
+    def __init__(self, value, sizes):
         dp_size, inner = sizes
-        keys, places = ["block"], {}
+        keys, places = [], {}
         for axis, size in (("dp", dp_size), ("fsdp", inner)):
             bit = size // 2
             while bit:
                 keys.append((axis, bit))
                 places[(axis, bit)] = (lax.axis_index(axis) // bit) % 2
                 bit //= 2
-        own = value.shape[0] // (blocks * dp_size * inner)
+        own = value.shape[0] // (dp_size * inner)
         self.sizes = {"dp": dp_size, "fsdp": inner}
         self.keys, self.places = keys, places
-        bits = (2,) * (len(keys) - 1)
-        self.terms = [value.reshape((blocks,) + bits + (own, value.shape[1]))]
+        self.terms = [value.reshape((2,) * len(keys) + (own, value.shape[1]))]
 
     def total(self, terms):
         wide = [term.astype(jnp.float32) for term in terms]
@@ -450,6 +449,37 @@
         return self.total(self.terms).astype(jnp.bfloat16)
 
 
+class Spread:
+    def __init__(self, value, sizes):
+        dp_size, inner = sizes
+        self.sizes = {"dp": dp_size, "fsdp": inner}
+        self.ranks = {}
+        for axis, size in (("dp", dp_size), ("fsdp", inner)):
+            bit = size // 2
+            while bit:
+                self.ranks[(axis, bit)] = len(self.ranks)
+                bit //= 2
+        self.held, self.value = [], value
+
+    def send(self, key):
+        self.key = key
+        return swap(self.value, key[0], self.sizes[key[0]], key[1])
+
+    def take(self, received):
+        axis, bit = self.key
+        upper = (lax.axis_index(axis) // bit) % 2 == 1
+        self.held.append(self.ranks[self.key])
+        self.held.sort()
+        place = self.held.index(self.ranks[self.key])
+        pair = (self.value, received)
+        both = jnp.where(upper, jnp.stack(pair[::-1], place), jnp.stack(pair, place))
+        order = tuple(range(both.ndim))
+        (self.value,) = fence(with_layout_constraint(both, Layout(major_to_minor=order)))
+
+    def rows(self):
+        return self.value.reshape(-1, self.value.shape[-1])
+
+
 CORE = ("dp", 1)
 ACROSS = ("dp", 2)
 
@@ -459,14 +489,12 @@
     rests = []
     for part in parts:
         rest = part.rest()
-        blocks, (own, columns) = rest.shape[0], rest.shape[-2:]
-        rest = rest.reshape(blocks, inner, own, columns).transpose(1, 0, 2, 3)
-        rests.append(rest.reshape(inner, blocks * own, columns))
+        own, columns = rest.shape[-2:]
+        rests.append(rest.reshape(inner, own, columns))
     packed = rests[0] if len(rests) == 1 else jnp.concatenate(rests, axis=1)
     summed = lax.psum_scatter(
         packed.reshape(-1, columns), "fsdp", scatter_dimension=0, tiled=True
     ).astype(jnp.float32)
-    own = summed.shape[0] // len(parts)
     return [summed[i * own : (i + 1) * own] for i in range(len(parts))]
 
 
@@ -493,23 +521,24 @@
     offset = (lax.axis_index("dp") * inner + lax.axis_index("fsdp")) * mine
     spread = lax.dynamic_update_slice(jnp.zeros((6, width), jnp.float32), norms, (0, offset))
     norms = butterfly_sum(spread, axes)
-    near = gather(
-        self_query, self_key, self_value, self_out, cross_query, cross_key, cross_value, cross_out
-    )
-    w_sqkv, w_kv = near[:3], near[5:7]
-    w_so, w_cq, w_ck, w_cv, w_co = [near[i] for i in range(3, 8)]
-    own, devices = mlp_out.shape[1], dp_size * inner
-    blocks = mlp_out.shape[0] // width
-    step = width // devices
-    in_rows = turned(mlp_in).reshape(blocks, step, width)
-    out_rows = turned(mlp_out).reshape(own, devices, blocks, step).transpose(2, 0, 1, 3)
-    far = jnp.concatenate([in_rows, out_rows.reshape(blocks, own, width)])
-    far = lax.all_gather(far, AXES, axis=1, tiled=True)
-    (far,) = fence(far.reshape(2, blocks * width, width))
-    w_in = far[0]
-    w_out = jnp.concatenate(
-        [far[1, i * width : (i + 1) * width] for i in range(blocks)], axis=1
-    )
+    near = gather(self_out, cross_query, cross_key, cross_value, cross_out)
+    w_so, w_cq, w_ck, w_cv, w_co = [near[i] for i in range(5)]
+    w_kv = near[2:4]
+    w_in = lax.all_gather(row_major(turned(mlp_in)), AXES, axis=0, tiled=True)
+    keys = [("fsdp", 1 << i) for i in reversed(range(inner.bit_length() - 1))] + [ACROSS]
+    orders = [keys[:1] + keys[1 + i :] + keys[1 : 1 + i] for i in range(3)]
+    whole = [Spread(turned(m), sizes) for m in (self_query, self_key, self_value)]
+    spread_out = Spread(turned(mlp_out), sizes)
+    for stage in range(len(keys) + 1):
+        flights = [w.send(o[stage] if stage < len(keys) else CORE) for w, o in zip(whole, orders)]
+        if stage + 1 < len(keys):
+            flights.append(spread_out.send(keys[stage]))
+        if stage + 1 == len(keys):
+            flying_w = spread_out.send(ACROSS)
+        flights = fence(*flights)
+        for w, f in zip(whole + [spread_out], flights):
+            w.take(f)
+    w_sqkv = [w.rows() for w in whole]
 
     starts = jnp.sum(
         segment_ids[0][None, :] < jnp.arange(page_map.shape[1] + 1, dtype=jnp.int32)[:, None],
@@ -527,7 +556,13 @@
     cq = contract(a2, w_cq, (1,), (1,), low)
     ck = contract(images, w_ck, (2,), (1,), low)
     cv = contract(images, w_cv, (2,), (1,), low)
+    cq, ck, cv, flying_w = fence(cq, ck, cv, flying_w)
+    spread_out.take(flying_w)
+    flying_w = spread_out.send(CORE)
     co, c_stats = cross_forward(starts, pages, cq, ck, cv)
+    co, c_stats, flying_w = fence(co, c_stats, flying_w)
+    spread_out.take(flying_w)
+    w_out = spread_out.rows()
     x2 = row_major(x1 + contract(co, w_co, (0,), (1,)))
     a3 = (normalise(x2)[0] * norms[4] + norms[5]).astype(low)
     u = contract(a3, w_in, (1,), (1,))
@@ -547,20 +582,20 @@
     flying = p_out.send(ACROSS)
     g_in = contract(du, a3, (0,), (0,), low)
     du, g_in = fence(du, g_in)
-    p_in = Partial(g_in, sizes, blocks)
+    p_in = Partial(g_in, sizes)
     flying_in = p_in.send(CORE)
     d3 = contract(du, w_in, (1,), (0,))
     back, gg3, gs3 = norm_back(x2, norms[4], d3)
     e2 = e + back
     e2b = e2.astype(low)
-    e2, e2b, flying, flying_in = fence(e2, e2b, flying, flying_in)
-    p_out.take(flying)
-    (g_mlp_out,) = scatter([p_out], sizes)
+    e2, e2b, flying_in = fence(e2, e2b, flying_in)
     p_in.take(flying_in)
     flying_in = p_in.send(ACROSS)
     d_co = contract(e2b, w_co, (1,), (0,), low)
     dcq, dck, dcv = cross_backward(starts, pages, cq, ck, cv, d_co, c_stats)
-    dcq, dck, dcv, flying_in = fence(dcq, dck, dcv, flying_in)
+    dcq, dck, dcv, flying, flying_in = fence(dcq, dck, dcv, flying, flying_in)
+    p_out.take(flying)
+    (g_mlp_out,) = scatter([p_out], sizes)
     p_in.take(flying_in)
     (g_mlp_in,) = scatter([p_in], sizes)
     g_co = contract(e2b, co, (0,), (1,), low)
@@ -636,10 +671,10 @@
             fenced = fence(*(flights + list(waits)))
         for p, f in zip(parts, fenced):
             p.take(f)
-        parts = [p for p in parts if len(p.keys) > 1]
+        parts = [p for p in parts if len(p.keys)]
         flights = [p.send(o[stage]) for p, o in zip(p_self, orders)]
-        if len(p_so.keys) > 1:
-            flights.append(p_so.send(keys[stage + 2]))
+        if len(p_so.keys):
+            flights.append(p_so.send(p_so.keys[-1] if len(p_so.keys) == 1 else keys[stage + 2]))
         if stage < 3:
             done = job(*needs)
             waits = jax.tree.leaves(done)[:1]
@@ -648,11 +683,9 @@
         p.take(f)
     grad_in, gg1, gs1 = results[0]
     block_out, grad_images = results[1], results[2]
-    g_self = [p.total(p.terms)[0] for p in p_self + [p_so]]
+    g_self = [p.total(p.terms) for p in p_self + [p_so]]
     norm_grads = butterfly_sum(jnp.stack([gg1, gs1, gg2, gs2, gg3, gs3]), axes)
     norm_grads = lax.dynamic_slice(norm_grads, (0, offset), (6, mine))
-    g_mlp_out = g_mlp_out.reshape(own, blocks, devices, step).transpose(0, 2, 1, 3)
-    g_mlp_out = g_mlp_out.reshape(own, -1)
     weight_grads = [g.T for g in g_self + g_cross + [g_mlp_in, g_mlp_out]]
     return (
         block_out[None], grad_in[None], grad_images, *[norm_grads[i] for i in range(6)],

time: 720 us -> 736 us (1.022)
  other arithmetic: 91 us -> 144 us
  starting transfers between devices: 43.7 us -> 72.5 us
  waiting for transfers between devices: 142 us -> 116 us
  local copies, waits for them, and re-layouts: 61.6 us -> 36.3 us
    all_gather x1, waiting for transfers between devices: 88.1 us -> 0.01 us  [gather(): return lax.all_gather(stacked, AXES, axis=1, tiled=True)]
    ppermute x42 -> x62, waiting for transfers between devices: 43 us -> 116 us  [swap(): return lax.ppermute(value, axis, [(i, i ^ bit) for i in range(size)])]
    select_n x0 -> x19, other arithmetic: none -> 48.4 us  [take(): jnp.where(upper, jnp.stack(pair[::-1], place), jnp.stack(pair, place))]
    ppermute x42 -> x62, starting transfers between devices: 43.3 us -> 71.5 us  [swap(): return lax.ppermute(value, axis, [(i, i ^ bit) for i in range(size)])]
    all_gather x1, waiting for transfers between devices: 11.2 us -> 0.02 us  [layer(): w_in = lax.all_gather(row_major(turned(mlp_in)), AXES, axis=0, tiled=True)]
    transpose x4 -> x1, local copies, waits for them, and re-layouts: 9.89 us -> 0.8 us  [layer(): weight_grads = [g.T for g in g_self + g_cross + [g_mlp_in, g_mlp_out]]]
    unnamed x175 -> x167, local copies, waits for them, and re-layouts: 32.5 us -> 27.3 us
  transfers between devices with their start and end apart: 47 -> 67, of which waited for: 11 -> 15; matrix products, arithmetic and copies ran while one was open for 42% -> 45% of each run, Pallas kernels for 19% -> 18%
where the time goes in v4:
time: 736 us; the launch traced here: 732 us
  matrix products  215 us (29%)
  other arithmetic  144 us (20%)
  Pallas kernels  131 us (18%)
  waiting for transfers between devices  116 us (16%)
  starting transfers between devices  72.5 us (10%)
  local copies, waits for them, and re-layouts  36.3 us (5%)
  between operations  15.7 us (2%)
    dot_general x29, matrix products, contract(): lax.dot_general(a, b, ((left, right), ((), ())), preferred_element_type=j...  215 us
    ppermute x62, waiting for transfers between devices, swap(): return lax.ppermute(value, axis, [(i, i ^ bit) for i in range(size)])  116 us
    ppermute x62, starting transfers between devices, swap(): return lax.ppermute(value, axis, [(i, i ^ bit) for i in range(size)])  71.5 us
    pallas_call x1, Pallas kernels, cross_backward(): pl.pallas_call(functools.partial(cross_backward_kernel, pairs), out_shape...  53.6 us
    select_n x19, other arithmetic, take(): jnp.where(upper, jnp.stack(pair[::-1], place), jnp.stack(pair, place))  48.4 us
    convert_element_type x22, other arithmetic, send(): return swap(out.astype(jnp.bfloat16), key[0], self.sizes[key[0]], key[1])  41 us
    pallas_call x1, Pallas kernels, cross_forward(): pl.pallas_call(functools.partial(cross_forward_kernel, pairs), out_shape=...  31.5 us
    pallas_call x1, Pallas kernels, self_backward(): pl.pallas_call(functools.partial(self_backward_kernel, pairs, most), out_...  27.8 us
  transfers between devices with their start and end apart: 67, of which 15 were waited for; matrix products, arithmetic and copies ran while one was open for 45% of the time, Pallas kernels for 18%

profile of v4, /device:TPU:0, one launch (start us, length us, event | category | flops | bytes accessed | tf_op | source)
XLA Modules:
  0.0 732.0 jit_solution(11867029883324730030)
XLA Ops:
  24.5 18.8 %collective-permute-done.5 = bf16[32,1024]{1,0:T(8,128)(2,1)S(1)} collective-permute-done((bf16[32,1024]{1,0:T(8,128)(2,1)S(1)}, bf16[32,1024]{1,0:T(8,128)(2,1)S(1)}, u32[]{:S(2)}, u32[]{:S(2)}) %collective-permute-start.5) | collective-permute-done | bytes 65568 | tf_op jit(solution)/shard_map/ppermute | solution.py:399
  58.4 16.9 %collective-permute-done.9 = bf16[2,32,1024]{2,1,0:T(8,128)(2,1)} collective-permute-done((bf16[2,32,1024]{2,1,0:T(8,128)(2,1)S(1)}, bf16[2,32,1024]{2,1,0:T(8,128)(2,1)}, u32[]{:S(2)}, u32[]{:S(2)}) %collective-permute-start.9) | collective-permute-done | bytes 131104 | tf_op jit(solution)/shard_map/ppermute | solution.py:399
  90.1 9.1 %collective-permute-done.15 = bf16[2,2,32,1024]{3,2,1,0:T(8,128)(2,1)} collective-permute-done((bf16[2,2,32,1024]{3,2,1,0:T(8,128)(2,1)S(1)}, bf16[2,2,32,1024]{3,2,1,0:T(8,128)(2,1)}, u32[]{:S(2)}, u32[]{:S(2)}) %collective-permute-start.15) | collective-permute-done | bytes 262176 | tf_op jit(solution)/shard_map/ppermute | solution.py:399
  99.2 24.9 %collective-permute-done.13 = bf16[2,2,32,1024]{3,2,1,0:T(8,128)(2,1)} collective-permute-done((bf16[2,2,32,1024]{3,2,1,0:T(8,128)(2,1)}, bf16[2,2,32,1024]{3,2,1,0:T(8,128)(2,1)}, u32[]{:S(2)}, u32[]{:S(2)}) %collective-permute-start.13) | collective-permute-done | bytes 262176 | tf_op jit(solution)/shard_map/ppermute | solution.py:399
  156.3 8.4 %collective-permute-start.4 = (f32[6,1024]{1,0:T(8,128)S(1)}, f32[6,1024]{1,0:T(8,128)S(1)}, u32[]{:S(2)}, u32[]{:S(2)}) collective-permute-start(f32[6,1024]{1,0:T(8,128)S(1)} %add.1207), channel_id=1, source_target_pairs={{0,4},{1,5},{2,6},{3,7},{4,0},{5,1},{6,2},{7,3},{8,12},{9,13},{10,... | collective-permute-start | bytes 73736 | tf_op jit(solution)/shard_map/ppermute | solution.py:399
  191.0 18.5 %self_forward.1 = (bf16[1024,1024]{1,0:T(8,128)(2,1)}, f32[2,8,1024]{2,1,0:T(8,128)}) custom-call(s32[5]{0:T(128)} %convert_reduce_fusion.1.starts, bf16[1024,1024]{1,0:T(8,128)(2,1)} %convolution_convert_fusion.13.q_ref, bf16[1024,1024]{1,0:T(8,128)(2,1)} %convolution_convert_fusion.12.k_ref, bf16[1024,1024]{1,0:T(8,128)(2,1)} %convolution_convert_fusion.11.v_ref), custom_call_target="tpu_custom_call" | custom-call | flops 5368709120 | bytes 10485760 | tf_op jit(solution)/shard_map/self_forward/pallas_call | solution.py:318
  220.4 7.6 %convert_bitcast_fusion.1.v_ref = bf16[4,588,1024]{2,1,0:T(8,128)(2,1)} fusion(bf16[4,588,1024]{2,0,1:T(4,128)(2,1)S(1)} %bitcast.724, bf16[5,1024,1024]{2,1,0:T(8,128)(2,1)S(1)} %bitcast.626), kind=kOutput, calls=%fused_computation.27 | convolution fusion | flops 4934909952 | bytes 11730944 | tf_op jit(solution)/shard_map/dot_general | solution.py:372
  228.0 8.0 %convert_bitcast_fusion.2.k_ref = bf16[4,588,1024]{2,1,0:T(8,128)(2,1)} fusion(bf16[4,588,1024]{2,0,1:T(4,128)(2,1)S(1)} %bitcast.724, bf16[5,1024,1024]{2,1,0:T(8,128)(2,1)S(1)} %bitcast.626), kind=kOutput, calls=%fused_computation.28 | convolution fusion | flops 4934909952 | bytes 11730944 | tf_op jit(solution)/shard_map/dot_general | solution.py:372
  242.0 31.5 %cross_forward.1 = (bf16[1024,1024]{1,0:T(8,128)(2,1)}, f32[2,8,1024]{2,1,0:T(8,128)}) custom-call(s32[5]{0:T(128)} %convert_reduce_fusion.1.starts, s32[4]{0:T(128)} %bitcast.725, bf16[1024,1024]{1,0:T(8,128)(2,1)} %convolution_convert_fusion.10.q_ref, bf16[4,588,1024]{2,1,0:T(8,128)(2,1)} %convert_bitcast_fusion.2.k_ref, ...), custom_call_target="tpu_custom_call" | custom-call | flops 13564379136 | bytes 20971520 | tf_op jit(solution)/shard_map/cross_forward/pallas_call | solution.py:266
  282.1 18.9 %multiply_convert_fusion.1 = (bf16[1024,4096]{1,0:T(8,128)(2,1)}, f32[1024,4096]{1,0:T(8,128)}) fusion(bf16[4096,1024]{1,0:T(8,128)(2,1)} %all-gather.5.cloned.1.call-done, f32[1024,1024]{1,0:T(8,128)} %copy-done.4, f32[1024]{0:T(1024)S(1)} %bitcast.720, f32[1024]{0:T(1024)S(1)} %bitcast.704, f32[1024]{0:T(1024)S(1)} %add_rsqrt_fusion, ...), kind=kOutput, calls=%fused_computation.7 | convolution fusion | flops 8616148992 | bytes 37765120 | tf_op jit(solution)/shard_map/dot_general | solution.py:372
  301.0 11.3 %convolution_convert_fusion.1 = bf16[4096,1024]{0,1:T(8,128)(2,1)S(1)} fusion(bf16[1024,4096]{1,0:T(8,128)(2,1)} %get-tuple-element.187, bf16[1,1024,1024]{2,1,0:T(8,128)(2,1)S(1)} %copy-done.29), kind=kOutput, calls=%fused_computation.15 | convolution fusion | flops 8594128896 | bytes 18874368 | tf_op jit(solution)/shard_map/dot_general | solution.py:372
  315.6 8.3 %maximum_select_fusion = bf16[2,2,2,2,2,32,4096]{6,5,4,3,2,1,0:T(8,128)(2,1)S(1)} fusion(bf16[2,1,2,2,2,32,4096]{6,5,4,3,2,1,0:T(8,128)(2,1)} %bitcast.88, bf16[2,1,2,2,2,32,4096]{6,5,4,3,2,1,0:T(8,128)(2,1)} %bitcast.87, pred[]{:T(512)S(6)} %eq.83), kind=kLoop, calls=%fused_computation.13 | loop fusion | flops 12582912 | bytes 16777216 | tf_op jit(solution)/shard_map/jit(_where)/select_n | solution.py:475
  324.0 19.6 %multiply_convert_fusion = bf16[1024,4096]{1,0:T(8,128)(2,1)} fusion(bf16[1024,1024]{1,0:T(8,128)(2,1)S(1)} %bitcast.679, bf16[1024,4096]{1,0:T(8,128)(2,1)S(1)} %bitcast.612, f32[1024,4096]{1,0:T(8,128)} %get-tuple-element.328), kind=kOutput, calls=%fused_computation.6 | convolution fusion | flops 8640266240 | bytes 35651584 | tf_op jit(solution)/shard_map/dot_general | solution.py:372
  343.6 12.6 %convolution_convert_fusion = bf16[4096,1024]{1,0:T(8,128)(2,1)S(1)} fusion(bf16[1024,4096]{1,0:T(8,128)(2,1)} %multiply_convert_fusion, f32[1024,1024]{1,0:T(8,128)S(1)} %copy-done.5, f32[1024]{0:T(1024)S(1)} %bitcast.721, f32[1024]{0:T(1024)S(1)} %bitcast.705, f32[1024]{0:T(1024)S(1)} %add_rsqrt_fusion, f32[1024]{0:T(1024)S(1)} %broadcast_multiply_fusion.6), kind=kOutput, calls=%fused_computation.14 | convolution fusion | flops 8599371776 | bytes 20987904 | tf_op jit(solution)/shard_map/dot_general | solution.py:372
  365.7 15.2 %multiply_reduce_fusion = (f32[1024]{0:T(1024)}, f32[1024]{0:T(1024)S(1)}, f32[1024]{0:T(1024)S(1)}, f32[1024]{0:T(1024)}, f32[1024,1024]{1,0:T(8,128)S(1)}) fusion(f32[1024,1024]{1,0:T(8,128)S(1)} %copy-done.6, f32[1024]{0:T(1024)S(1)} %add_rsqrt_fusion, f32[1024]{0:T(1024)S(1)} %broadcast_multiply_fusion.6, f32[1024]{0:T(1024)S(1)} %bitcast.706, ...), kind=kOutput, calls=%fused_computation.54 | convolution fusion | flops 8599367680 | bytes 25194496 | tf_op jit(solution)/shard_map/dot_general | solution.py:372
  398.4 53.6 %cross_backward.1 = (bf16[1024,1024]{1,0:T(8,128)(2,1)}, bf16[4,588,1024]{2,1,0:T(8,128)(2,1)}, bf16[4,588,1024]{2,1,0:T(8,128)(2,1)}) custom-call(s32[5]{0:T(128)} %convert_reduce_fusion.1.starts, s32[4]{0:T(128)} %bitcast.726, bf16[1024,1024]{1,0:T(8,128)(2,1)} %convolution_convert_fusion.10.q_ref, bf16[4,588,1024]{2,1,0:T(8,128)(2,1)} %convert_bitcast_fusion.2.k_ref, ...), custom_call_target="tpu_custom_call" | custom-call | flops 33910947840 | bytes 31457280 | tf_op jit(solution)/shard_map/cross_backward/pallas_call | solution.py:290
  469.7 10.6 %bitcast_convert_fusion = bf16[1024,1024]{1,0:T(8,128)(2,1)S(1)} fusion(bf16[4,588,1024]{2,1,0:T(8,128)(2,1)} %get-tuple-element.193, bf16[4,588,1024]{2,0,1:T(4,128)(2,1)} %param.22), kind=kOutput, calls=%fused_computation.52 | convolution fusion | flops 4933550080 | bytes 11730944 | tf_op jit(solution)/shard_map/dot_general | solution.py:372
  480.3 10.5 %bitcast_convert_fusion.1 = bf16[1024,1024]{1,0:T(8,128)(2,1)S(1)} fusion(bf16[4,588,1024]{2,1,0:T(8,128)(2,1)} %get-tuple-element.192, bf16[4,588,1024]{2,0,1:T(4,128)(2,1)} %param.22), kind=kOutput, calls=%fused_computation.53 | convolution fusion | flops 4933550080 | bytes 11730944 | tf_op jit(solution)/shard_map/dot_general | solution.py:372
  500.6 7.3 %multiply_reduce_fusion.1 = (f32[1024]{0:T(1024)S(1)}, f32[1024]{0:T(1024)S(1)}, f32[1024]{0:T(1024)S(1)}, f32[1024]{0:T(1024)S(1)}, f32[1024,1024]{1,0:T(8,128)S(1)}) fusion(f32[1024,1024]{1,0:T(8,128)} %copy-done.8, f32[1024]{0:T(1024)S(1)} %copy-done.52, f32[1024]{0:T(1024)S(1)} %copy-done.48, f32[1024]{0:T(1024)S(1)} %bitcast.700, ...), kind=kOutput, calls=%fused_computation.55 | convolution fusion | flops 2156916736 | bytes 12611584 | tf_op jit(solution)/shard_map/dot_general | solution.py:372
  530.6 27.8 %self_backward.1 = (bf16[1024,1024]{1,0:T(8,128)(2,1)}, bf16[1024,1024]{1,0:T(8,128)(2,1)}, bf16[1024,1024]{1,0:T(8,128)(2,1)}) custom-call(s32[5]{0:T(128)} %convert_reduce_fusion.1.starts, bf16[1024,1024]{1,0:T(8,128)(2,1)} %convolution_convert_fusion.13.q_ref, bf16[1024,1024]{1,0:T(8,128)(2,1)} %convolution_convert_fusion.12.k_ref, ...), custom_call_target="tpu_custom_call" | custom-call | flops 13421772800 | bytes 16777216 | tf_op jit(solution)/shard_map/self_backward/pallas_call | solution.py:341
  619.6 14.8 %collective-permute-done.54 = f32[6,1024]{1,0:T(8,128)S(1)} collective-permute-done((f32[6,1024]{1,0:T(8,128)S(1)}, f32[6,1024]{1,0:T(8,128)S(1)}, u32[]{:S(2)}, u32[]{:S(2)}) %collective-permute-start.54) | collective-permute-done | bytes 24608 | tf_op jit(solution)/shard_map/ppermute | solution.py:399
  659.7 15.2 %add_convert_fusion = bf16[1024,1024]{1,0:T(8,128)(2,1)} fusion(f32[1024,1024]{1,0:T(8,128)S(1)} %copy-done.7, bf16[1024,4096]{1,0:T(8,128)(2,1)} %get-tuple-element.187, bf16[1024,4096]{1,0:T(8,128)(2,1)} %bitcast.613), kind=kOutput, calls=%fused_computation.56 | convolution fusion | flops 8592031744 | bytes 23068672 | tf_op jit(solution)/shard_map/dot_general | solution.py:372
  682.0 14.2 %fusion.34 = f32[4,588,1024]{2,1,0:T(8,128)} fusion(bf16[2048,1024,1]{1,0,2:T(8,128)(2,1)S(1)} %bitcast.631, bf16[4,588,1024]{2,1,0:T(8,128)(2,1)} %get-tuple-element.193, bf16[4,588,1024]{2,1,0:T(8,128)(2,1)S(1)} %bitcast.729), kind=kOutput, calls=%fused_computation.73 | convolution fusion | flops 9884270592 | bytes 23461888 | tf_op jit(solution)/shard_map/dot_general | solution.py:372
  696.2 13.8 %copy.143 = f32[4,588,1024]{2,0,1:T(4,128)} copy(f32[4,588,1024]{2,1,0:T(8,128)} %fusion.34) | data formatting | bytes 19267584
  (440 shorter events, 318.9 us)
Async XLA Ops:
  7.2 202.3 %all-gather.3.cloned.1.call-start = ((), (), s32[]{:S(2)}) async-start(), calls=%async_computation.3 | async-start | bytes 10813440 | tf_op jit(solution)/shard_map/all_gather | solution.py:516
  12.6 269.5 %all-gather.5.cloned.1.call-start = ((), (), s32[]{:S(2)}) async-start(), calls=%async_computation.4 | async-start | bytes 8650752 | tf_op jit(solution)/shard_map/all_gather | solution.py:527
  13.9 31.4 %collective-permute-start.8 = (bf16[32,4096]{1,0:T(8,128)(2,1)S(1)}, bf16[32,4096]{1,0:T(8,128)(2,1)S(1)}, u32[]{:S(2)}, u32[]{:S(2)}) collective-permute-start(bf16[32,4096]{1,0:T(8,128)(2,1)S(1)} %get-tuple-element.304), channel_id=1, source_target_pairs={{0,4},{1,5},{2,6},{3,7},{4,0},{5,1},{6,2},{7,3},{8,12},{9,13},{10,... | collective-permute-start | bytes 786440 | tf_op jit(solution)/shard_map/ppermute | solution.py:399
  77.8 46.3 %collective-permute-start.16 = (bf16[2,2,32,4096]{3,2,1,0:T(8,128)(2,1)S(1)}, bf16[2,2,32,4096]{3,2,1,0:T(8,128)(2,1)}, u32[]{:S(2)}, u32[]{:S(2)}) collective-permute-start(bf16[2,2,32,4096]{3,2,1,0:T(8,128)(2,1)S(1)} %maximum_select_fusion.6), channel_id=1, source_target_pairs={{0,1},{1,0},{2,3},{3,2},{4,5},{5,4},{6,7},{7,6},{8,9},{9,8},{10,11... | collective-permute-start | bytes 3145736 | tf_op jit(solution)/shard_map/ppermute | solution.py:399
  86.1 37.9 %collective-permute-start.13 = (bf16[2,2,32,1024]{3,2,1,0:T(8,128)(2,1)}, bf16[2,2,32,1024]{3,2,1,0:T(8,128)(2,1)}, u32[]{:S(2)}, u32[]{:S(2)}) collective-permute-start(bf16[2,2,32,1024]{3,2,1,0:T(8,128)(2,1)} %maximum_select_fusion.14), channel_id=1, source_target_pairs={{0,1},{1,0},{2,3},{3,2},{4,5},{5,4},{6,7},{7,6},{8,9},{9,8},{10,11... | collective-permute-start | bytes 786440 | tf_op jit(solution)/shard_map/ppermute | solution.py:399
  87.5 46.3 %collective-permute-start = (f32[6,1024]{1,0:T(8,128)S(1)}, f32[6,1024]{1,0:T(8,128)S(1)}, u32[]{:S(2)}, u32[]{:S(2)}) collective-permute-start(f32[6,1024]{1,0:T(8,128)S(1)} %dynamic_update_slice.5), channel_id=1, source_target_pairs={{0,8},{8,0},{16,24},{24,16},{1,9},{9,1},{17,25},{25,17},{2,10},{10... | collective-permute-start | bytes 73736 | tf_op jit(solution)/shard_map/ppermute | solution.py:399
  89.5 556.5 %reduce-scatter.8.cloned.1.call-start = ((), (), s32[]{:S(2)}) async-start(), calls=%async_computation.6 | async-start | bytes 2359296 | tf_op jit(solution)/shard_map/reduce_scatter | solution.py:495
  170.1 65.8 %collective-permute-start.23 = (bf16[2,2,2,32,4096]{4,3,2,1,0:T(8,128)(2,1)}, bf16[2,2,2,32,4096]{4,3,2,1,0:T(8,128)(2,1)}, u32[]{:S(2)}, u32[]{:S(2)}) collective-permute-start(bf16[2,2,2,32,4096]{4,3,2,1,0:T(8,128)(2,1)} %maximum_select_fusion.5), channel_id=1, source_target_pairs={{0,16},{8,24},{16,0},{24,8},{1,17},{9,25},{17,1},{25,9},{2,18},{10... | collective-permute-start | bytes 6291464 | tf_op jit(solution)/shard_map/ppermute | solution.py:399
  242.0 31.5 %collective-permute-start.24 = (bf16[2,2,2,2,32,4096]{5,4,3,2,1,0:T(8,128)(2,1)}, bf16[2,2,2,2,32,4096]{5,4,3,2,1,0:T(8,128)(2,1)}, u32[]{:S(2)}, u32[]{:S(2)}) collective-permute-start(bf16[2,2,2,2,32,4096]{5,4,3,2,1,0:T(8,128)(2,1)} %maximum_select_fusion.1), channel_id=1, source_target_pairs={{0,8},{8,0},{16,24},{24,16},{1,9},{9,1},{17,25},{25,17},{2,10},{10... | collective-permute-start | bytes 12582920 | tf_op jit(solution)/shard_map/ppermute | solution.py:399
  365.7 86.2 %collective-permute-start.27 = (bf16[2,2,2,32,4096]{4,3,2,1,0:T(8,128)(2,1)}, bf16[2,2,2,32,4096]{4,3,2,1,0:T(8,128)(2,1)}, u32[]{:S(2)}, u32[]{:S(2)}) collective-permute-start(bf16[2,2,2,32,4096]{4,3,2,1,0:T(8,128)(2,1)} %fusion.33), channel_id=1, source_target_pairs={{0,16},{8,24},{16,0},{24,8},{1,17},{9,25},{17,1},{25,9},{2,18},{10... | collective-permute-start | bytes 6291464 | tf_op jit(solution)/shard_map/ppermute | solution.py:399
  388.9 69.5 %collective-permute-start.28 = (bf16[2,2,2,128,1024]{4,3,2,1,0:T(8,128)(2,1)}, bf16[2,2,2,128,1024]{4,3,2,1,0:T(8,128)(2,1)S(1)}, u32[]{:S(2)}, u32[]{:S(2)}) collective-permute-start(bf16[2,2,2,128,1024]{4,3,2,1,0:T(8,128)(2,1)} %fusion.32), channel_id=1, source_target_pairs={{0,16},{8,24},{16,0},{24,8},{1,17},{9,25},{17,1},{25,9},{2,18},{10... | collective-permute-start | bytes 6291464 | tf_op jit(solution)/shard_map/ppermute | solution.py:399
  463.8 183.9 %reduce-scatter.10.cloned.1.call-start = ((), (), s32[]{:S(2)}) async-start(), calls=%async_computation.7 | async-start | bytes 2359296
  500.3 223.0 %reduce-scatter.6.cloned.1.call-start = ((), (), s32[]{:S(2)}) async-start(), calls=%async_computation.5 | async-start | bytes 2359296 | tf_op jit(solution)/shard_map/reduce_scatter | solution.py:495
  513.6 44.8 %collective-permute-start.37 = (bf16[2,2,2,32,1024]{4,3,2,1,0:T(8,128)(2,1)}, bf16[2,2,2,32,1024]{4,3,2,1,0:T(8,128)(2,1)}, u32[]{:S(2)}, u32[]{:S(2)}) collective-permute-start(bf16[2,2,2,32,1024]{4,3,2,1,0:T(8,128)(2,1)} %fusion.65), channel_id=1, source_target_pairs={{0,16},{8,24},{16,0},{24,8},{1,17},{9,25},{17,1},{25,9},{2,18},{10... | collective-permute-start | bytes 1572872 | tf_op jit(solution)/shard_map/ppermute | solution.py:399
  515.9 42.5 %collective-permute-start.36 = (bf16[2,2,2,32,1024]{4,3,2,1,0:T(8,128)(2,1)}, bf16[2,2,2,32,1024]{4,3,2,1,0:T(8,128)(2,1)}, u32[]{:S(2)}, u32[]{:S(2)}) collective-permute-start(bf16[2,2,2,32,1024]{4,3,2,1,0:T(8,128)(2,1)} %fusion.66), channel_id=1, source_target_pairs={{0,16},{8,24},{16,0},{24,8},{1,17},{9,25},{17,1},{25,9},{2,18},{10... | collective-permute-start | bytes 1572872 | tf_op jit(solution)/shard_map/ppermute | solution.py:399
  520.0 38.4 %collective-permute-start.35 = (bf16[2,2,2,32,1024]{4,3,2,1,0:T(8,128)(2,1)}, bf16[2,2,2,32,1024]{4,3,2,1,0:T(8,128)(2,1)}, u32[]{:S(2)}, u32[]{:S(2)}) collective-permute-start(bf16[2,2,2,32,1024]{4,3,2,1,0:T(8,128)(2,1)} %fusion.67), channel_id=1, source_target_pairs={{0,16},{8,24},{16,0},{24,8},{1,17},{9,25},{17,1},{25,9},{2,18},{10... | collective-permute-start | bytes 1572872 | tf_op jit(solution)/shard_map/ppermute | solution.py:399
  522.4 39.2 %collective-permute-start.34 = (bf16[2,2,2,32,1024]{4,3,2,1,0:T(8,128)(2,1)}, bf16[2,2,2,32,1024]{4,3,2,1,0:T(8,128)(2,1)}, u32[]{:S(2)}, u32[]{:S(2)}) collective-permute-start(bf16[2,2,2,32,1024]{4,3,2,1,0:T(8,128)(2,1)} %fusion.68), channel_id=1, source_target_pairs={{0,16},{8,24},{16,0},{24,8},{1,17},{9,25},{17,1},{25,9},{2,18},{10... | collective-permute-start | bytes 1572872 | tf_op jit(solution)/shard_map/ppermute | solution.py:399
  526.8 34.8 %collective-permute-start.33 = (bf16[2,2,2,2,32,1024]{5,4,3,2,1,0:T(8,128)(2,1)S(1)}, bf16[2,2,2,2,32,1024]{5,4,3,2,1,0:T(8,128)(2,1)}, u32[]{:S(2)}, u32[]{:S(2)}) collective-permute-start(bf16[2,2,2,2,32,1024]{5,4,3,2,1,0:T(8,128)(2,1)S(1)} %dynamic-slice_bitcast_fusion.5), channel_id=1, source_target_pairs={{0,8},{8,0},{16,24},{24,16},{1,9},{9,1},{17,25},{25,17},{2,10},{10... | collective-permute-start | bytes 3145736 | tf_op jit(solution)/shard_map/ppermute | solution.py:399
  605.3 44.5 %collective-permute-start.46 = (bf16[2,32,1024]{2,1,0:T(8,128)(2,1)}, bf16[2,32,1024]{2,1,0:T(8,128)(2,1)}, u32[]{:S(2)}, u32[]{:S(2)}) collective-permute-start(bf16[2,32,1024]{2,1,0:T(8,128)(2,1)} %fusion.76), channel_id=1, source_target_pairs={{0,2},{1,3},{2,0},{3,1},{4,6},{5,7},{6,4},{7,5},{8,10},{9,11},{10,... | collective-permute-start | bytes 393224 | tf_op jit(solution)/shard_map/ppermute | solution.py:399
  610.4 39.3 %collective-permute-start.45 = (bf16[2,2,2,32,1024]{4,3,2,1,0:T(8,128)(2,1)}, bf16[2,2,2,32,1024]{4,3,2,1,0:T(8,128)(2,1)}, u32[]{:S(2)}, u32[]{:S(2)}) collective-permute-start(bf16[2,2,2,32,1024]{4,3,2,1,0:T(8,128)(2,1)} %fusion.61), channel_id=1, source_target_pairs={{0,2},{1,3},{2,0},{3,1},{4,6},{5,7},{6,4},{7,5},{8,10},{9,11},{10,... | collective-permute-start | bytes 1572872 | tf_op jit(solution)/shard_map/ppermute | solution.py:399
  614.7 35.0 %collective-permute-start.44 = (bf16[2,2,2,32,1024]{4,3,2,1,0:T(8,128)(2,1)}, bf16[2,2,2,32,1024]{4,3,2,1,0:T(8,128)(2,1)}, u32[]{:S(2)}, u32[]{:S(2)}) collective-permute-start(bf16[2,2,2,32,1024]{4,3,2,1,0:T(8,128)(2,1)} %fusion.62), channel_id=1, source_target_pairs={{0,1},{1,0},{2,3},{3,2},{4,5},{5,4},{6,7},{7,6},{8,9},{9,8},{10,11... | collective-permute-start | bytes 1572872 | tf_op jit(solution)/shard_map/ppermute | solution.py:399
  676.0 35.6 %collective-permute-start.58 = (bf16[2,32,1024]{2,1,0:T(8,128)(2,1)S(1)}, bf16[2,32,1024]{2,1,0:T(8,128)(2,1)S(1)}, u32[]{:S(2)}, u32[]{:S(2)}) collective-permute-start(bf16[2,32,1024]{2,1,0:T(8,128)(2,1)S(1)} %fusion.73), channel_id=1, source_target_pairs={{0,16},{8,24},{16,0},{24,8},{1,17},{9,25},{17,1},{25,9},{2,18},{10... | collective-permute-start | bytes 393224 | tf_op jit(solution)/shard_map/ppermute | solution.py:399
  678.0 33.7 %collective-permute-start.57 = (bf16[2,32,1024]{2,1,0:T(8,128)(2,1)S(1)}, bf16[2,32,1024]{2,1,0:T(8,128)(2,1)S(1)}, u32[]{:S(2)}, u32[]{:S(2)}) collective-permute-start(bf16[2,32,1024]{2,1,0:T(8,128)(2,1)S(1)} %fusion.74), channel_id=1, source_target_pairs={{0,4},{1,5},{2,6},{3,7},{4,0},{5,1},{6,2},{7,3},{8,12},{9,13},{10,... | collective-permute-start | bytes 393224 | tf_op jit(solution)/shard_map/ppermute | solution.py:399
  680.0 31.7 %collective-permute-start.56 = (bf16[2,32,1024]{2,1,0:T(8,128)(2,1)S(1)}, bf16[2,32,1024]{2,1,0:T(8,128)(2,1)S(1)}, u32[]{:S(2)}, u32[]{:S(2)}) collective-permute-start(bf16[2,32,1024]{2,1,0:T(8,128)(2,1)S(1)} %fusion.75), channel_id=1, source_target_pairs={{0,2},{1,3},{2,0},{3,1},{4,6},{5,7},{6,4},{7,5},{8,10},{9,11},{10,... | collective-permute-start | bytes 393224 | tf_op jit(solution)/shard_map/ppermute | solution.py:399
  (126 other events, 1781.7 us)
Sparse Core Ops, SparseCore 0:
  12.7 123.2 all-gather.2
  138.9 95.0 all-gather.4
  464.0 70.0 reduce-scatter.7
  537.4 67.3 reduce-scatter.9
  608.2 75.7 reduce-scatter.5

commit v5 on v3

--- a/solution.py
+++ b/solution.py
@@ -437,11 +437,17 @@
         return functools.reduce(jnp.add, wide)
 
     def send(self, key):
+        return self.fly(self.cut(key), key)
+
+    def fly(self, load, key):
+        return swap(load, key[0], self.sizes[key[0]], key[1])
+
+    def cut(self, key):
         axis = self.keys.index(key)
         self.keys.remove(key)
         out = self.total([pick(term, 1 - self.places[key], axis) for term in self.terms])
         self.terms = [pick(term, self.places[key], axis) for term in self.terms]
-        return swap(out.astype(jnp.bfloat16), key[0], self.sizes[key[0]], key[1])
+        return out.astype(jnp.bfloat16)
 
     def take(self, received):
         self.terms.append(received)
@@ -553,14 +559,14 @@
     back, gg3, gs3 = norm_back(x2, norms[4], d3)
     e2 = e + back
     e2b = e2.astype(low)
-    e2, e2b, flying, flying_in = fence(e2, e2b, flying, flying_in)
-    p_out.take(flying)
-    (g_mlp_out,) = scatter([p_out], sizes)
+    e2, e2b, flying_in = fence(e2, e2b, flying_in)
     p_in.take(flying_in)
     flying_in = p_in.send(ACROSS)
     d_co = contract(e2b, w_co, (1,), (0,), low)
     dcq, dck, dcv = cross_backward(starts, pages, cq, ck, cv, d_co, c_stats)
-    dcq, dck, dcv, flying_in = fence(dcq, dck, dcv, flying_in)
+    dcq, dck, dcv, flying, flying_in = fence(dcq, dck, dcv, flying, flying_in)
+    p_out.take(flying)
+    (g_mlp_out,) = scatter([p_out], sizes)
     p_in.take(flying_in)
     (g_mlp_in,) = scatter([p_in], sizes)
     g_co = contract(e2b, co, (0,), (1,), low)
@@ -579,28 +585,21 @@
         p.take(f)
     flying = [p.send(ACROSS) for p in p_cross]
     g_so = contract(e1b, so, (0,), (1,), low)
-    p_so = Partial(g_so, sizes)
-    flying_so = p_so.send(CORE)
     d_so = contract(e1b, w_so, (1,), (0,), low)
     dsq, dsk, dsv = self_backward(starts, sq, sk, sv, d_so, s_stats, most)
-    dsq, dsk, dsv, flying_so, *flying = fence(dsq, dsk, dsv, flying_so, *flying)
+    dsq, dsk, dsv, g_so, *flying = fence(dsq, dsk, dsv, g_so, *flying)
     for p, f in zip(p_cross, flying):
         p.take(f)
     g_cross = scatter(p_cross, sizes)
-    orders = []
-    keys = [ACROSS] + [("fsdp", 1 << i) for i in range(inner.bit_length() - 1)]
-    for shift in range(3):
-        orders.append(keys[shift:] + keys[:shift])
-    p_so.take(flying_so)
-    flying_so = p_so.send(keys[0])
     g_sq = contract(dsq, a1, (1,), (0,), low)
     g_sk = contract(dsk, a1, (0,), (0,), low)
     g_sv = contract(dsv, a1, (0,), (0,), low)
-    dsq, dsk, dsv, g_sq, g_sk, g_sv, flying_so = fence(dsq, dsk, dsv, g_sq, g_sk, g_sv, flying_so)
-    p_so.take(flying_so)
-    p_self = [Partial(g, sizes) for g in (g_sq, g_sk, g_sv)]
-    flying = [p.send(CORE) for p in p_self]
-    flying_so = p_so.send(keys[1])
+    pairs = (jnp.concatenate([g_sq, g_sk]), jnp.concatenate([g_sv, g_so]))
+    dsq, dsk, dsv, *pairs = fence(dsq, dsk, dsv, *pairs)
+    groups = [Partial(pair, sizes, 2) for pair in pairs]
+    keys = [("fsdp", 1 << i) for i in range(inner.bit_length() - 1)]
+    orders = [[ACROSS] + keys, keys[:-1] + [ACROSS] + keys[-1:]]
+    flights = [g.send(CORE) for g in groups]
     d1 = (
         contract(dsq, w_sqkv[0], (0,), (0,))
         + contract(dsk, w_sqkv[1], (1,), (0,))
@@ -617,38 +616,30 @@
         flat = contract(
             both.reshape(tokens * count, 2 * width), w_kv.reshape(2 * width, width), (1,), (0,)
         )
-        return flat.reshape(tokens, count, width).transpose(1, 0, 2)
+        return flat.reshape(tokens, count, width)
 
     def finish(hidden):
         return (x2 + contract(hidden, w_out, (1,), (1,))).astype(low)
 
-    fillers = [(norm_one, (d1,)), (finish, (hidden,)), (image_grads, (dck, dcv))]
-    results = []
-    waits = (d1,)
-    parts = p_self + [p_so]
-    flights = flying + [flying_so]
-    for stage in range(len(keys)):
-        if stage < 3:
-            job, needs = fillers[stage]
-            fenced = fence(*(flights + list(waits) + list(needs)))
-            needs = fenced[-len(needs) :]
-        else:
-            fenced = fence(*(flights + list(waits)))
-        for p, f in zip(parts, fenced):
-            p.take(f)
-        parts = [p for p in parts if len(p.keys) > 1]
-        flights = [p.send(o[stage]) for p, o in zip(p_self, orders)]
-        if len(p_so.keys) > 1:
-            flights.append(p_so.send(keys[stage + 2]))
-        if stage < 3:
-            done = job(*needs)
-            waits = jax.tree.leaves(done)[:1]
-            results.append(done)
-    for p, f in zip(parts, flights):
-        p.take(f)
-    grad_in, gg1, gs1 = results[0]
-    block_out, grad_images = results[1], results[2]
-    g_self = [p.total(p.terms)[0] for p in p_self + [p_so]]
+    grad_in, gg1, gs1 = norm_one(d1)
+    grad_in, hidden, dck, dcv, *flights = fence(grad_in, hidden, dck, dcv, *flights)
+    for stage in range(len(keys) + 1):
+        for g, f in zip(groups, flights):
+            g.take(f)
+        loads = [g.cut(o[stage]) for g, o in zip(groups, orders)]
+        if stage == 0:
+            hidden, *loads = fence(hidden, *loads)
+        if stage == 1:
+            dck, dcv, *loads = fence(dck, dcv, *loads)
+        flights = [g.fly(load, o[stage]) for g, load, o in zip(groups, loads, orders)]
+        if stage == 0:
+            block_out, *flights = fence(finish(hidden), *flights)
+        if stage == 1:
+            grad_images, *flights = fence(image_grads(dck, dcv), *flights)
+            grad_images = grad_images.transpose(1, 0, 2)
+    for g, f in zip(groups, flights):
+        g.take(f)
+    g_self = [g.total(g.terms)[i] for g in groups for i in range(2)]
     norm_grads = butterfly_sum(jnp.stack([gg1, gs1, gg2, gs2, gg3, gs3]), axes)
     norm_grads = lax.dynamic_slice(norm_grads, (0, offset), (6, mine))
     g_mlp_out = g_mlp_out.reshape(own, blocks, devices, step).transpose(0, 2, 1, 3)

time: 720 us -> 705 us (0.979)
  other arithmetic: 91 us -> 78.9 us
  starting transfers between devices: 43.7 us -> 34.7 us
    ppermute x42 -> x32, starting transfers between devices: 43.3 us -> 34 us  [swap(): return lax.ppermute(value, axis, [(i, i ^ bit) for i in range(size)])]
    convert_element_type x22 -> x14, other arithmetic: 39.8 us -> 32.4 us  [cut(): return out.astype(jnp.bfloat16)]
    unnamed x175 -> x161, local copies, waits for them, and re-layouts: 32.5 us -> 31.4 us
    ppermute x42 -> x32, waiting for transfers between devices: 43 us -> 42.4 us  [swap(): return lax.ppermute(value, axis, [(i, i ^ bit) for i in range(size)])]
  transfers between devices with their start and end apart: 47 -> 37, of which waited for: 11 -> 16; matrix products, arithmetic and copies ran while one was open for 42% -> 42% of each run, Pallas kernels for 19% -> 19%
where the time goes in v5:
time: 705 us; the launch traced here: 696 us
  matrix products  226 us (32%)
  waiting for transfers between devices  142 us (20%)
  Pallas kernels  133 us (19%)
  other arithmetic  78.9 us (11%)
  local copies, waits for them, and re-layouts  67.1 us (10%)
  starting transfers between devices  34.7 us (5%)
  between operations  15.4 us (2%)
    dot_general x29, matrix products, contract(): lax.dot_general(a, b, ((left, right), ((), ())), preferred_element_type=j...  226 us
    all_gather x1, waiting for transfers between devices, gather(): return lax.all_gather(stacked, AXES, axis=1, tiled=True)  88.1 us
    pallas_call x1, Pallas kernels, cross_backward(): pl.pallas_call(functools.partial(cross_backward_kernel, pairs), out_shape...  53.6 us
    ppermute x32, waiting for transfers between devices, swap(): return lax.ppermute(value, axis, [(i, i ^ bit) for i in range(size)])  42.4 us
    ppermute x32, starting transfers between devices, swap(): return lax.ppermute(value, axis, [(i, i ^ bit) for i in range(size)])  34 us
    convert_element_type x14, other arithmetic, cut(): return out.astype(jnp.bfloat16)  32.4 us
    pallas_call x1, Pallas kernels, cross_forward(): pl.pallas_call(functools.partial(cross_forward_kernel, pairs), out_shape=...  32.1 us
    unnamed x161, local copies, waits for them, and re-layouts  31.4 us
  transfers between devices with their start and end apart: 37, of which 16 were waited for; matrix products, arithmetic and copies ran while one was open for 42% of the time, Pallas kernels for 19%

profile of v5, /device:TPU:0, one launch (start us, length us, event | category | flops | bytes accessed | tf_op | source)
XLA Modules:
  0.0 696.3 jit_solution(16756665814906304834)
XLA Ops:
  44.8 88.1 %all-gather.3.cloned.1.call-done = bf16[8,1024,1024]{2,1,0:T(8,128)(2,1)} async-done(((bf16[8,32,1024]{2,1,0:T(8,128)(2,1)}), bf16[8,1024,1024]{2,1,0:T(8,128)(2,1)}) %all-gather.3.cloned.1.call-update) | async-done | bytes 16777232 | tf_op jit(solution)/shard_map/all_gather | solution.py:494
  147.6 19.1 %self_forward.1 = (bf16[1024,1024]{1,0:T(8,128)(2,1)}, f32[2,8,1024]{2,1,0:T(8,128)}) custom-call(s32[5]{0:T(128)} %convert_reduce_fusion.1.starts, bf16[1024,1024]{1,0:T(8,128)(2,1)} %convolution_convert_fusion.13.q_ref, bf16[1024,1024]{1,0:T(8,128)(2,1)} %convolution_convert_fusion.12.k_ref, bf16[1024,1024]{1,0:T(8,128)(2,1)} %convolution_convert_fusion.11.v_ref), custom_call_target="tpu_custom_call" | custom-call | flops 5368709120 | bytes 10485760 | tf_op jit(solution)/shard_map/self_forward/pallas_call | solution.py:318
  173.5 6.2 convolution_convert_fusion.10.q_ref
  181.6 7.6 %convert_bitcast_fusion.2.k_ref = bf16[4,588,1024]{2,1,0:T(8,128)(2,1)} fusion(bf16[4,588,1024]{2,0,1:T(4,128)(2,1)S(1)} %bitcast.590, bf16[8,1024,1024]{2,1,0:T(8,128)(2,1)S(1)} %bitcast.529), kind=kOutput, calls=%fused_computation.31 | convolution fusion | flops 4934909952 | bytes 11730944 | tf_op jit(solution)/shard_map/dot_general | solution.py:372
  189.2 7.9 %convert_bitcast_fusion.1.v_ref = bf16[4,588,1024]{2,1,0:T(8,128)(2,1)} fusion(bf16[4,588,1024]{2,0,1:T(4,128)(2,1)S(1)} %bitcast.590, bf16[8,1024,1024]{2,1,0:T(8,128)(2,1)S(1)} %bitcast.529), kind=kOutput, calls=%fused_computation.30 | convolution fusion | flops 4934909952 | bytes 11730944 | tf_op jit(solution)/shard_map/dot_general | solution.py:372
  197.1 32.1 %cross_forward.1 = (bf16[1024,1024]{1,0:T(8,128)(2,1)}, f32[2,8,1024]{2,1,0:T(8,128)}) custom-call(s32[5]{0:T(128)} %convert_reduce_fusion.1.starts, s32[4]{0:T(128)} %bitcast.591, bf16[1024,1024]{1,0:T(8,128)(2,1)} %convolution_convert_fusion.10.q_ref, bf16[4,588,1024]{2,1,0:T(8,128)(2,1)} %convert_bitcast_fusion.2.k_ref, ...), custom_call_target="tpu_custom_call" | custom-call | flops 13564379136 | bytes 20971520 | tf_op jit(solution)/shard_map/cross_forward/pallas_call | solution.py:266
  229.2 6.0 fusion.94
  237.9 11.0 %all-gather.5.cloned.1.call-done = bf16[8,1024,1024]{2,1,0:T(8,128)(2,1)} async-done(((bf16[8,32,1024]{2,1,0:T(8,128)(2,1)}), bf16[8,1024,1024]{2,1,0:T(8,128)(2,1)}) %all-gather.5.cloned.1.call-update) | async-done | bytes 16777232 | tf_op jit(solution)/shard_map/all_gather | solution.py:513
  248.9 18.7 %multiply_convert_fusion.1 = (bf16[1024,4096]{1,0:T(8,128)(2,1)}, f32[1024,4096]{1,0:T(8,128)}) fusion(bf16[2,4096,1024]{2,1,0:T(8,128)(2,1)} %bitcast.523, f32[1024,1024]{1,0:T(8,128)} %copy-done.4, f32[1024]{0:T(1024)S(1)} %bitcast.586, f32[1024]{0:T(1024)S(1)} %bitcast.568, f32[1024]{0:T(1024)S(1)} %add_rsqrt_fusion, f32[1024]{0:T(1024)S(1)} %broadcast_multiply_fusion.6), kind=kOutput, calls=%fused_computation.7 | convolution fusion | flops 8616148992 | bytes 37765120 | tf_op jit(solution)/shard_map/dot_general | solution.py:372
  267.7 13.1 %convolution_convert_fusion.1 = bf16[4096,1024]{0,1:T(8,128)(2,1)S(1)} fusion(bf16[1024,4096]{1,0:T(8,128)(2,1)} %get-tuple-element.131, bf16[1,1024,1024]{2,1,0:T(8,128)(2,1)} %param.41), kind=kOutput, calls=%fused_computation.16 | convolution fusion | flops 8594128896 | bytes 18874368 | tf_op jit(solution)/shard_map/dot_general | solution.py:372
  289.0 20.7 %multiply_convert_fusion = bf16[1024,4096]{1,0:T(8,128)(2,1)} fusion(bf16[1024,1024]{1,0:T(8,128)(2,1)} %bitcast.553, f32[1024,4096]{1,0:T(8,128)} %get-tuple-element.274, bf16[1024,1024]{1,0:T(8,128)(2,1)} %get-tuple-element.246, bf16[1024,1024]{1,0:T(8,128)(2,1)} %get-tuple-element.247, bf16[1024,1024]{1,0:T(8,128)(2,1)} %get-tuple-element.248, ...), kind=kOutput, calls=%fused_computation.6 | convolution fusion | flops 8673820672 | bytes 35651584 | tf_op jit(solution)/shard_map/dot_general | solution.py:372
  309.7 12.2 %convolution_convert_fusion = bf16[4096,1024]{1,0:T(8,128)(2,1)S(1)} fusion(bf16[1024,4096]{1,0:T(8,128)(2,1)} %multiply_convert_fusion, f32[1024,1024]{1,0:T(8,128)S(1)} %copy-done.5, f32[1024]{0:T(1024)S(1)} %bitcast.587, f32[1024]{0:T(1024)S(1)} %bitcast.569, f32[1024]{0:T(1024)S(1)} %add_rsqrt_fusion, f32[1024]{0:T(1024)S(1)} %broadcast_multiply_fusion.6), kind=kOutput, calls=%fused_computation.15 | convolution fusion | flops 8599371776 | bytes 20987904 | tf_op jit(solution)/shard_map/dot_general | solution.py:372
  332.6 15.0 %multiply_reduce_fusion = (f32[1024]{0:T(1024)S(1)}, f32[1024]{0:T(1024)S(1)}, f32[1024]{0:T(1024)S(1)}, f32[1024]{0:T(1024)S(1)}, f32[1024,1024]{1,0:T(8,128)S(1)}) fusion(f32[1024,1024]{1,0:T(8,128)S(1)} %copy-done.6, f32[1024]{0:T(1024)S(1)} %add_rsqrt_fusion, f32[1024]{0:T(1024)S(1)} %broadcast_multiply_fusion.6, f32[1024]{0:T(1024)S(1)} %bitcast.570, ...), kind=kOutput, calls=%fused_computation.59 | convolution fusion | flops 8599367680 | bytes 25194496 | tf_op jit(solution)/shard_map/dot_general | solution.py:372
  350.6 6.1 fusion.34
  364.6 53.6 %cross_backward.1 = (bf16[1024,1024]{1,0:T(8,128)(2,1)}, bf16[4,588,1024]{2,1,0:T(8,128)(2,1)}, bf16[4,588,1024]{2,1,0:T(8,128)(2,1)}) custom-call(s32[5]{0:T(128)} %convert_reduce_fusion.1.starts, s32[4]{0:T(128)} %bitcast.592, bf16[1024,1024]{1,0:T(8,128)(2,1)} %convolution_convert_fusion.10.q_ref, bf16[4,588,1024]{2,1,0:T(8,128)(2,1)} %convert_bitcast_fusion.2.k_ref, ...), custom_call_target="tpu_custom_call" | custom-call | flops 33910947840 | bytes 31457280 | tf_op jit(solution)/shard_map/cross_backward/pallas_call | solution.py:290
  418.2 5.9 collective-permute-done.8
  436.0 10.4 %bitcast_convert_fusion.1 = bf16[1024,1024]{1,0:T(8,128)(2,1)S(1)} fusion(bf16[4,588,1024]{2,1,0:T(8,128)(2,1)} %get-tuple-element.140, bf16[4,588,1024]{2,0,1:T(4,128)(2,1)} %param.22), kind=kOutput, calls=%fused_computation.57 | convolution fusion | flops 4933550080 | bytes 11730944 | tf_op jit(solution)/shard_map/dot_general | solution.py:372
  446.5 10.6 %bitcast_convert_fusion = bf16[1024,1024]{1,0:T(8,128)(2,1)S(1)} fusion(bf16[4,588,1024]{2,1,0:T(8,128)(2,1)} %get-tuple-element.141, bf16[4,588,1024]{2,0,1:T(4,128)(2,1)} %param.22), kind=kOutput, calls=%fused_computation.56 | convolution fusion | flops 4933550080 | bytes 11730944 | tf_op jit(solution)/shard_map/dot_general | solution.py:372
  466.3 7.4 %multiply_reduce_fusion.1 = (f32[1024]{0:T(1024)S(1)}, f32[1024]{0:T(1024)S(1)}, f32[1024]{0:T(1024)S(1)}, f32[1024]{0:T(1024)S(1)}, f32[1024,1024]{1,0:T(8,128)S(1)}) fusion(f32[1024,1024]{1,0:T(8,128)} %copy-done.8, f32[1024]{0:T(1024)S(1)} %copy-done.38, f32[1024]{0:T(1024)S(1)} %copy-done.30, f32[1024]{0:T(1024)S(1)} %bitcast.566, ...), kind=kOutput, calls=%fused_computation.60 | convolution fusion | flops 2156916736 | bytes 12611584 | tf_op jit(solution)/shard_map/dot_general | solution.py:372
  493.5 28.2 %self_backward.1 = (bf16[1024,1024]{1,0:T(8,128)(2,1)}, bf16[1024,1024]{1,0:T(8,128)(2,1)}, bf16[1024,1024]{1,0:T(8,128)(2,1)}) custom-call(s32[5]{0:T(128)} %convert_reduce_fusion.1.starts, bf16[1024,1024]{1,0:T(8,128)(2,1)} %convolution_convert_fusion.13.q_ref, bf16[1024,1024]{1,0:T(8,128)(2,1)} %convolution_convert_fusion.12.k_ref, ...), custom_call_target="tpu_custom_call" | custom-call | flops 13421772800 | bytes 16777216 | tf_op jit(solution)/shard_map/self_backward/pallas_call | solution.py:341
  590.8 14.8 %add_convert_fusion = bf16[1024,1024]{1,0:T(8,128)(2,1)} fusion(f32[1024,1024]{1,0:T(8,128)S(1)} %copy-done.7, bf16[1024,4096]{1,0:T(8,128)(2,1)} %get-tuple-element.131, bf16[1024,1024]{1,0:T(8,128)(2,1)} %get-tuple-element.246, bf16[1024,1024]{1,0:T(8,128)(2,1)} %get-tuple-element.247, bf16[1024,1024]{1,0:T(8,128)(2,1)} %get-tuple-element.248, ...), kind=kOutput, calls=%fused_computation.61 | convolution fusion | flops 8625586176 | bytes 23068672 | tf_op jit(solution)/shard_map/dot_general | solution.py:372
  609.9 10.6 %collective-permute-done.20 = bf16[2,2,2,2,32,1024]{5,4,0,3,2,1:T(8,128)(2,1)S(1)} collective-permute-done((bf16[2,2,2,2,32,1024]{5,4,0,3,2,1:T(8,128)(2,1)}, bf16[2,2,2,2,32,1024]{5,4,0,3,2,1:T(8,128)(2,1)S(1)}, u32[]{:S(2)}, u32[]{:S(2)}) %collective-permute-start.20) | collective-permute-done | bytes 1048608 | tf_op jit(solution)/shard_map/ppermute | solution.py:399
  625.3 15.4 %fusion.5 = f32[588,4,1024]{2,0,1:T(8,128)} fusion(bf16[2048,1024,1]{1,0,2:T(8,128)(2,1)S(1)} %bitcast.536, bf16[4,588,1024]{2,1,0:T(8,128)(2,1)} %get-tuple-element.141, bf16[4,588,1024]{2,1,0:T(8,128)(2,1)} %get-tuple-element.140), kind=kOutput, calls=%fused_computation.10 | convolution fusion | flops 9884270592 | bytes 23461888 | tf_op jit(solution)/shard_map/dot_general | solution.py:372
  663.6 13.8 %copy.156 = f32[4,588,1024]{2,0,1:T(4,128)} copy(f32[4,588,1024]{2,1,0:T(8,128)} %bitcast.510) | data formatting | bytes 19267584
  (357 shorter events, 246.5 us)
Async XLA Ops:
  7.2 125.7 %all-gather.3.cloned.1.call-start = ((), (), s32[]{:S(2)}) async-start(), calls=%async_computation.3 | async-start | bytes 17301504 | tf_op jit(solution)/shard_map/all_gather | solution.py:494
  15.4 233.6 %all-gather.5.cloned.1.call-start = ((), (), s32[]{:S(2)}) async-start(), calls=%async_computation.4 | async-start | bytes 17301504 | tf_op jit(solution)/shard_map/all_gather | solution.py:513
  22.9 629.7 %reduce-scatter.6.cloned.1.call-start = ((), (), s32[]{:S(2)}) async-start(), calls=%async_computation.6 | async-start | bytes 2359296 | tf_op jit(solution)/shard_map/reduce_scatter | solution.py:472
  285.3 24.4 %collective-permute-start.5 = (bf16[1,2,2,2,2,32,4096]{6,5,4,3,2,1,0:T(8,128)(2,1)}, bf16[1,2,2,2,2,32,4096]{6,5,4,3,2,1,0:T(8,128)(2,1)}, u32[]{:S(2)}, u32[]{:S(2)}) collective-permute-start(bf16[1,2,2,2,2,32,4096]{6,5,4,3,2,1,0:T(8,128)(2,1)} %dynamic-slice_bitcast_fusion), channel_id=1, source_target_pairs={{0,8},{8,0},{16,24},{24,16},{1,9},{9,1},{17,25},{25,17},{2,10},{10... | collective-permute-start | bytes 12582920 | tf_op jit(solution)/shard_map/ppermute | solution.py:399
  326.4 24.3 %collective-permute-start.6 = (bf16[4,2,2,2,2,32,1024]{6,5,4,3,2,0,1:T(8,128)(2,1)}, bf16[4,2,2,2,2,32,1024]{6,5,4,3,2,0,1:T(8,128)(2,1)}, u32[]{:S(2)}, u32[]{:S(2)}) collective-permute-start(bf16[4,2,2,2,2,32,1024]{6,5,4,3,2,0,1:T(8,128)(2,1)} %copy_bitcast_fusion), channel_id=1, source_target_pairs={{0,8},{8,0},{16,24},{24,16},{1,9},{9,1},{17,25},{25,17},{2,10},{10... | collective-permute-start | bytes 12582920 | tf_op jit(solution)/shard_map/ppermute | solution.py:399
  331.1 87.1 %collective-permute-start.7 = (bf16[1,2,2,2,32,4096]{5,4,3,2,1,0:T(8,128)(2,1)}, bf16[1,2,2,2,32,4096]{5,4,3,2,1,0:T(8,128)(2,1)S(1)}, u32[]{:S(2)}, u32[]{:S(2)}) collective-permute-start(bf16[1,2,2,2,32,4096]{5,4,3,2,1,0:T(8,128)(2,1)} %fusion.35), channel_id=1, source_target_pairs={{0,16},{8,24},{16,0},{24,8},{1,17},{9,25},{17,1},{25,9},{2,18},{10... | collective-permute-start | bytes 6291464 | tf_op jit(solution)/shard_map/ppermute | solution.py:399
  356.7 67.5 %collective-permute-start.8 = (bf16[4,2,2,2,32,1024]{5,4,3,2,1,0:T(8,128)(2,1)}, bf16[4,2,2,2,32,1024]{5,4,3,2,1,0:T(8,128)(2,1)}, u32[]{:S(2)}, u32[]{:S(2)}) collective-permute-start(bf16[4,2,2,2,32,1024]{5,4,3,2,1,0:T(8,128)(2,1)} %fusion.34), channel_id=1, source_target_pairs={{0,16},{8,24},{16,0},{24,8},{1,17},{9,25},{17,1},{25,9},{2,18},{10... | collective-permute-start | bytes 6291464 | tf_op jit(solution)/shard_map/ppermute | solution.py:399
  430.1 224.4 %reduce-scatter.8.cloned.1.call-start = ((), (), s32[]{:S(2)}) async-start(), calls=%async_computation.7 | async-start | bytes 2359296 | tf_op jit(solution)/shard_map/reduce_scatter | solution.py:472
  457.2 19.8 %collective-permute-start.9 = (bf16[1,2,2,2,2,32,1024]{6,5,4,3,2,1,0:T(8,128)(2,1)S(1)}, bf16[1,2,2,2,2,32,1024]{6,5,4,3,2,1,0:T(8,128)(2,1)}, u32[]{:S(2)}, u32[]{:S(2)}) collective-permute-start(bf16[1,2,2,2,2,32,1024]{6,5,4,3,2,1,0:T(8,128)(2,1)S(1)} %dynamic-slice_bitcast_fusion.4), channel_id=1, source_target_pairs={{0,8},{8,0},{16,24},{24,16},{1,9},{9,1},{17,25},{25,17},{2,10},{10... | collective-permute-start | bytes 3145736 | tf_op jit(solution)/shard_map/ppermute | solution.py:399
  458.3 18.6 %collective-permute-start.10 = (bf16[1,2,2,2,2,32,1024]{6,5,4,3,2,1,0:T(8,128)(2,1)}, bf16[1,2,2,2,2,32,1024]{6,5,4,3,2,1,0:T(8,128)(2,1)}, u32[]{:S(2)}, u32[]{:S(2)}) collective-permute-start(bf16[1,2,2,2,2,32,1024]{6,5,4,3,2,1,0:T(8,128)(2,1)} %dynamic-slice_bitcast_fusion.3), channel_id=1, source_target_pairs={{0,8},{8,0},{16,24},{24,16},{1,9},{9,1},{17,25},{25,17},{2,10},{10... | collective-permute-start | bytes 3145736 | tf_op jit(solution)/shard_map/ppermute | solution.py:399
  459.9 17.0 %collective-permute-start.11 = (bf16[1,2,2,2,2,32,1024]{6,5,4,3,2,1,0:T(8,128)(2,1)}, bf16[1,2,2,2,2,32,1024]{6,5,4,3,2,1,0:T(8,128)(2,1)}, u32[]{:S(2)}, u32[]{:S(2)}) collective-permute-start(bf16[1,2,2,2,2,32,1024]{6,5,4,3,2,1,0:T(8,128)(2,1)} %dynamic-slice_bitcast_fusion.2), channel_id=1, source_target_pairs={{0,8},{8,0},{16,24},{24,16},{1,9},{9,1},{17,25},{25,17},{2,10},{10... | collective-permute-start | bytes 3145736 | tf_op jit(solution)/shard_map/ppermute | solution.py:399
  466.2 221.5 %reduce-scatter.4.cloned.1.call-start = ((), (), s32[]{:S(2)}) async-start(), calls=%async_computation.5 | async-start | bytes 2359296 | tf_op jit(solution)/shard_map/reduce_scatter | solution.py:472
  479.9 46.7 %collective-permute-start.13 = (bf16[1,2,2,2,32,1024]{5,4,3,2,1,0:T(8,128)(2,1)S(1)}, bf16[1,2,2,2,32,1024]{5,4,3,2,1,0:T(8,128)(2,1)}, u32[]{:S(2)}, u32[]{:S(2)}) collective-permute-start(bf16[1,2,2,2,32,1024]{5,4,3,2,1,0:T(8,128)(2,1)S(1)} %fusion.71), channel_id=1, source_target_pairs={{0,16},{8,24},{16,0},{24,8},{1,17},{9,25},{17,1},{25,9},{2,18},{10... | collective-permute-start | bytes 1572872 | tf_op jit(solution)/shard_map/ppermute | solution.py:399
  482.9 43.7 %collective-permute-start.14 = (bf16[1,2,2,2,32,1024]{5,4,3,2,1,0:T(8,128)(2,1)S(1)}, bf16[1,2,2,2,32,1024]{5,4,3,2,1,0:T(8,128)(2,1)}, u32[]{:S(2)}, u32[]{:S(2)}) collective-permute-start(bf16[1,2,2,2,32,1024]{5,4,3,2,1,0:T(8,128)(2,1)S(1)} %fusion.70), channel_id=1, source_target_pairs={{0,16},{8,24},{16,0},{24,8},{1,17},{9,25},{17,1},{25,9},{2,18},{10... | collective-permute-start | bytes 1572872 | tf_op jit(solution)/shard_map/ppermute | solution.py:399
  485.6 41.0 %collective-permute-start.15 = (bf16[1,2,2,2,32,1024]{5,4,3,2,1,0:T(8,128)(2,1)}, bf16[1,2,2,2,32,1024]{5,4,3,2,1,0:T(8,128)(2,1)}, u32[]{:S(2)}, u32[]{:S(2)}) collective-permute-start(bf16[1,2,2,2,32,1024]{5,4,3,2,1,0:T(8,128)(2,1)} %fusion.69), channel_id=1, source_target_pairs={{0,16},{8,24},{16,0},{24,8},{1,17},{9,25},{17,1},{25,9},{2,18},{10... | collective-permute-start | bytes 1572872 | tf_op jit(solution)/shard_map/ppermute | solution.py:399
  489.4 38.1 %collective-permute-start.16 = (bf16[1,2,2,2,32,1024]{5,4,3,2,1,0:T(8,128)(2,1)}, bf16[1,2,2,2,32,1024]{5,4,3,2,1,0:T(8,128)(2,1)}, u32[]{:S(2)}, u32[]{:S(2)}) collective-permute-start(bf16[1,2,2,2,32,1024]{5,4,3,2,1,0:T(8,128)(2,1)} %fusion.68), channel_id=1, source_target_pairs={{0,16},{8,24},{16,0},{24,8},{1,17},{9,25},{17,1},{25,9},{2,18},{10... | collective-permute-start | bytes 1572872 | tf_op jit(solution)/shard_map/ppermute | solution.py:399
  539.9 42.6 %collective-permute-start.17 = (bf16[2,2,2,2,2,32,1024]{6,5,0,2,4,3,1:T(8,128)(2,1)}, bf16[2,2,2,2,2,32,1024]{6,5,0,2,4,3,1:T(8,128)(2,1)}, u32[]{:S(2)}, u32[]{:S(2)}) collective-permute-start(bf16[2,2,2,2,2,32,1024]{6,5,0,2,4,3,1:T(8,128)(2,1)} %copy_bitcast_fusion.2), channel_id=1, source_target_pairs={{0,8},{8,0},{16,24},{24,16},{1,9},{9,1},{17,25},{25,17},{2,10},{10... | collective-permute-start | bytes 6291464 | tf_op jit(solution)/shard_map/ppermute | solution.py:399
  542.3 40.2 %collective-permute-start.18 = (bf16[2,2,2,2,2,32,1024]{6,5,0,2,4,3,1:T(8,128)(2,1)}, bf16[2,2,2,2,2,32,1024]{6,5,0,2,4,3,1:T(8,128)(2,1)}, u32[]{:S(2)}, u32[]{:S(2)}) collective-permute-start(bf16[2,2,2,2,2,32,1024]{6,5,0,2,4,3,1:T(8,128)(2,1)} %copy_bitcast_fusion.1), channel_id=1, source_target_pairs={{0,8},{8,0},{16,24},{24,16},{1,9},{9,1},{17,25},{25,17},{2,10},{10... | collective-permute-start | bytes 6291464 | tf_op jit(solution)/shard_map/ppermute | solution.py:399
  587.7 22.2 %collective-permute-start.19 = (bf16[2,2,2,2,32,1024]{5,4,0,3,2,1:T(8,128)(2,1)}, bf16[2,2,2,2,32,1024]{5,4,0,3,2,1:T(8,128)(2,1)}, u32[]{:S(2)}, u32[]{:S(2)}) collective-permute-start(bf16[2,2,2,2,32,1024]{5,4,0,3,2,1:T(8,128)(2,1)} %copy.140), channel_id=1, source_target_pairs={{0,16},{8,24},{16,0},{24,8},{1,17},{9,25},{17,1},{25,9},{2,18},{10... | collective-permute-start | bytes 3145736 | tf_op jit(solution)/shard_map/ppermute | solution.py:399
  590.1 30.4 %collective-permute-start.20 = (bf16[2,2,2,2,32,1024]{5,4,0,3,2,1:T(8,128)(2,1)}, bf16[2,2,2,2,32,1024]{5,4,0,3,2,1:T(8,128)(2,1)S(1)}, u32[]{:S(2)}, u32[]{:S(2)}) collective-permute-start(bf16[2,2,2,2,32,1024]{5,4,0,3,2,1:T(8,128)(2,1)} %copy.141), channel_id=1, source_target_pairs={{0,1},{1,0},{2,3},{3,2},{4,5},{5,4},{6,7},{7,6},{8,9},{9,8},{10,11... | collective-permute-start | bytes 3145736 | tf_op jit(solution)/shard_map/ppermute | solution.py:399
  623.7 17.1 %collective-permute-start.21 = (bf16[2,2,2,32,1024]{4,3,0,2,1:T(8,128)(2,1)S(1)}, bf16[2,2,2,32,1024]{4,3,0,2,1:T(8,128)(2,1)S(1)}, u32[]{:S(2)}, u32[]{:S(2)}) collective-permute-start(bf16[2,2,2,32,1024]{4,3,0,2,1:T(8,128)(2,1)S(1)} %copy.146), channel_id=1, source_target_pairs={{0,1},{1,0},{2,3},{3,2},{4,5},{5,4},{6,7},{7,6},{8,9},{9,8},{10,11... | collective-permute-start | bytes 1572872 | tf_op jit(solution)/shard_map/ppermute | solution.py:399
  624.7 16.1 %collective-permute-start.22 = (bf16[2,2,2,32,1024]{4,3,0,2,1:T(8,128)(2,1)S(1)}, bf16[2,2,2,32,1024]{4,3,0,2,1:T(8,128)(2,1)S(1)}, u32[]{:S(2)}, u32[]{:S(2)}) collective-permute-start(bf16[2,2,2,32,1024]{4,3,0,2,1:T(8,128)(2,1)S(1)} %fusion.66), channel_id=1, source_target_pairs={{0,2},{1,3},{2,0},{3,1},{4,6},{5,7},{6,4},{7,5},{8,10},{9,11},{10,... | collective-permute-start | bytes 1572872 | tf_op jit(solution)/shard_map/ppermute | solution.py:399
  645.6 31.8 %collective-permute-start.30 = (bf16[2,2,32,1024]{3,2,0,1:T(8,128)(2,1)S(1)}, bf16[2,2,32,1024]{3,2,0,1:T(8,128)(2,1)}, u32[]{:S(2)}, u32[]{:S(2)}) collective-permute-start(bf16[2,2,32,1024]{3,2,0,1:T(8,128)(2,1)S(1)} %fusion.72), channel_id=1, source_target_pairs={{0,16},{8,24},{16,0},{24,8},{1,17},{9,25},{17,1},{25,9},{2,18},{10... | collective-permute-start | bytes 786440 | tf_op jit(solution)/shard_map/ppermute | solution.py:399
  650.8 29.0 %collective-permute-start.29 = (bf16[2,32,1024]{2,1,0:T(8,128)(2,1)}, bf16[2,32,1024]{2,1,0:T(8,128)(2,1)S(1)}, u32[]{:S(2)}, u32[]{:S(2)}) collective-permute-start(bf16[2,32,1024]{2,1,0:T(8,128)(2,1)} %fusion.76), channel_id=1, source_target_pairs={{0,4},{1,5},{2,6},{3,7},{4,0},{5,1},{6,2},{7,3},{8,12},{9,13},{10,... | collective-permute-start | bytes 393224 | tf_op jit(solution)/shard_map/ppermute | solution.py:399
  (93 other events, 1405.6 us)
Sparse Core Ops, SparseCore 0:
  15.5 117.3 all-gather.2
  136.5 112.3 all-gather.4
  430.2 66.6 reduce-scatter.5
  500.4 67.5 reduce-scatter.7
  574.5 70.4 reduce-scatter.3

commit v6 on v5

--- a/solution.py
+++ b/solution.py
@@ -476,6 +476,30 @@
     return [summed[i * own : (i + 1) * own] for i in range(len(parts))]
 
 
+def side_by_side_kernel(own, blocks, rows_ref, out_ref):
+    width = rows_ref.shape[1]
+    for device in range(out_ref.shape[0] // own):
+        for block in range(blocks):
+            first = (device * blocks + block) * own
+            out_ref[device * own : (device + 1) * own, block * width : (block + 1) * width] = (
+                rows_ref[first : first + own, :]
+            )
+
+
+def side_by_side(far, own, blocks, devices=4):
+    _, rows, width = far.shape
+    step = devices * own
+    return pl.pallas_call(
+        functools.partial(side_by_side_kernel, own, blocks),
+        out_shape=jax.ShapeDtypeStruct((rows // blocks, blocks * width), far.dtype),
+        grid=(rows // (blocks * step),),
+        in_specs=[pl.BlockSpec((None, blocks * step, width), lambda i: (1, i, 0))],
+        out_specs=pl.BlockSpec((step, blocks * width), lambda i: (i, 0)),
+        cost_estimate=cost(0, 4 * rows * width, 0),
+        name="side_by_side",
+    )(far)
+
+
 def layer(
     sizes, block_in, images, segment_ids, page_map, ln1_gain, ln1_shift, ln2_gain, ln2_shift,
     ln3_gain, ln3_shift, self_query, self_key, self_value, self_out, cross_query, cross_key,
@@ -504,18 +528,13 @@
     )
     w_sqkv, w_kv = near[:3], near[5:7]
     w_so, w_cq, w_ck, w_cv, w_co = [near[i] for i in range(3, 8)]
-    own, devices = mlp_out.shape[1], dp_size * inner
+    own = mlp_out.shape[1]
     blocks = mlp_out.shape[0] // width
-    step = width // devices
-    in_rows = turned(mlp_in).reshape(blocks, step, width)
-    out_rows = turned(mlp_out).reshape(own, devices, blocks, step).transpose(2, 0, 1, 3)
-    far = jnp.concatenate([in_rows, out_rows.reshape(blocks, own, width)])
+    out_rows = turned(mlp_out).reshape(own, blocks, width).transpose(1, 0, 2)
+    far = jnp.stack([turned(mlp_in), out_rows.reshape(blocks * own, width)])
     far = lax.all_gather(far, AXES, axis=1, tiled=True)
-    (far,) = fence(far.reshape(2, blocks * width, width))
     w_in = far[0]
-    w_out = jnp.concatenate(
-        [far[1, i * width : (i + 1) * width] for i in range(blocks)], axis=1
-    )
+    w_out = side_by_side(far, own, blocks)
 
     starts = jnp.sum(
         segment_ids[0][None, :] < jnp.arange(page_map.shape[1] + 1, dtype=jnp.int32)[:, None],
@@ -553,7 +572,7 @@
     flying = p_out.send(ACROSS)
     g_in = contract(du, a3, (0,), (0,), low)
     du, g_in = fence(du, g_in)
-    p_in = Partial(g_in, sizes, blocks)
+    p_in = Partial(g_in, sizes)
     flying_in = p_in.send(CORE)
     d3 = contract(du, w_in, (1,), (0,))
     back, gg3, gs3 = norm_back(x2, norms[4], d3)
@@ -628,22 +647,20 @@
             g.take(f)
         loads = [g.cut(o[stage]) for g, o in zip(groups, orders)]
         if stage == 0:
+            dck, dcv, *loads = fence(dck, dcv, *loads)
+        if stage == 1:
             hidden, *loads = fence(hidden, *loads)
-        if stage == 1:
-            dck, dcv, *loads = fence(dck, dcv, *loads)
         flights = [g.fly(load, o[stage]) for g, load, o in zip(groups, loads, orders)]
         if stage == 0:
+            grad_images = image_grads(dck, dcv).transpose(1, 0, 2)
+            grad_images, *flights = fence(grad_images, *flights)
+        if stage == 1:
             block_out, *flights = fence(finish(hidden), *flights)
-        if stage == 1:
-            grad_images, *flights = fence(image_grads(dck, dcv), *flights)
-            grad_images = grad_images.transpose(1, 0, 2)
     for g, f in zip(groups, flights):
         g.take(f)
     g_self = [g.total(g.terms)[i] for g in groups for i in range(2)]
     norm_grads = butterfly_sum(jnp.stack([gg1, gs1, gg2, gs2, gg3, gs3]), axes)
     norm_grads = lax.dynamic_slice(norm_grads, (0, offset), (6, mine))
-    g_mlp_out = g_mlp_out.reshape(own, blocks, devices, step).transpose(0, 2, 1, 3)
-    g_mlp_out = g_mlp_out.reshape(own, -1)
     weight_grads = [g.T for g in g_self + g_cross + [g_mlp_in, g_mlp_out]]
     return (
         block_out[None], grad_in[None], grad_images, *[norm_grads[i] for i in range(6)],

time: 705 us -> 693 us (0.983)
  local copies, waits for them, and re-layouts: 67.1 us -> 47.1 us
  waiting for transfers between devices: 142 us -> 153 us
    transpose x6 -> x3, local copies, waits for them, and re-layouts: 11.3 us -> 2.23 us  [layer(): weight_grads = [g.T for g in g_self + g_cross + [g_mlp_in, g_mlp_out]]]
    pallas_call x0 -> x1, Pallas kernels: none -> 8.97 us  [side_by_side(): pl.pallas_call(functools.partial(side_by_side_kernel, own, blocks), out_s...]
    unnamed x161 -> x145, local copies, waits for them, and re-layouts: 31.4 us -> 31.6 us
  transfers between devices with their start and end apart: 37 -> 37, of which waited for: 16 -> 16; matrix products, arithmetic and copies ran while one was open for 42% -> 40% of each run, Pallas kernels for 19% -> 19%
where the time goes in v6:
time: 693 us; the launch traced here: 685 us
  matrix products  219 us (32%)
  waiting for transfers between devices  153 us (22%)
  Pallas kernels  134 us (19%)
  other arithmetic  82.5 us (12%)
  local copies, waits for them, and re-layouts  47.1 us (7%)
  starting transfers between devices  34.2 us (5%)
  between operations  15.3 us (2%)
    dot_general x29, matrix products, contract(): lax.dot_general(a, b, ((left, right), ((), ())), preferred_element_type=j...  219 us
    all_gather x1, waiting for transfers between devices, gather(): return lax.all_gather(stacked, AXES, axis=1, tiled=True)  91.6 us
    pallas_call x1, Pallas kernels, cross_backward(): pl.pallas_call(functools.partial(cross_backward_kernel, pairs), out_shape...  49.4 us
    ppermute x32, waiting for transfers between devices, swap(): return lax.ppermute(value, axis, [(i, i ^ bit) for i in range(size)])  47.4 us
    ppermute x32, starting transfers between devices, swap(): return lax.ppermute(value, axis, [(i, i ^ bit) for i in range(size)])  33.6 us
    convert_element_type x14, other arithmetic, cut(): return out.astype(jnp.bfloat16)  32.6 us
    unnamed x145, local copies, waits for them, and re-layouts  31.6 us
    pallas_call x1, Pallas kernels, cross_forward(): pl.pallas_call(functools.partial(cross_forward_kernel, pairs), out_shape=...  30.2 us
  transfers between devices with their start and end apart: 37, of which 16 were waited for; matrix products, arithmetic and copies ran while one was open for 40% of the time, Pallas kernels for 19%

profile of v6, /device:TPU:0, one launch (start us, length us, event | category | flops | bytes accessed | tf_op | source)
XLA Modules:
  0.0 685.2 jit_solution(16434736581147421502)
XLA Ops:
  42.1 91.6 %all-gather.3.cloned.1.call-done = bf16[8,1024,1024]{2,1,0:T(8,128)(2,1)} async-done(((bf16[8,32,1024]{2,1,0:T(8,128)(2,1)}), bf16[8,1024,1024]{2,1,0:T(8,128)(2,1)}) %all-gather.3.cloned.1.call-update) | async-done | bytes 16777232 | tf_op jit(solution)/shard_map/all_gather | solution.py:518
  148.3 18.3 %self_forward.1 = (bf16[1024,1024]{1,0:T(8,128)(2,1)}, f32[2,8,1024]{2,1,0:T(8,128)}) custom-call(s32[5]{0:T(128)} %convert_reduce_fusion.1.starts, bf16[1024,1024]{1,0:T(8,128)(2,1)} %convolution_convert_fusion.13.q_ref, bf16[1024,1024]{1,0:T(8,128)(2,1)} %convolution_convert_fusion.12.k_ref, bf16[1024,1024]{1,0:T(8,128)(2,1)} %convolution_convert_fusion.11.v_ref), custom_call_target="tpu_custom_call" | custom-call | flops 5368709120 | bytes 10485760 | tf_op jit(solution)/shard_map/self_forward/pallas_call | solution.py:318
  173.4 6.2 convolution_convert_fusion.10.q_ref
  181.5 7.6 %convert_bitcast_fusion.2.k_ref = bf16[4,588,1024]{2,1,0:T(8,128)(2,1)} fusion(bf16[4,588,1024]{2,0,1:T(4,128)(2,1)S(1)} %bitcast.579, bf16[8,1024,1024]{2,1,0:T(8,128)(2,1)S(1)} %bitcast.517), kind=kOutput, calls=%fused_computation.30 | convolution fusion | flops 4934909952 | bytes 11730944 | tf_op jit(solution)/shard_map/dot_general | solution.py:372
  189.1 7.8 %convert_bitcast_fusion.1.v_ref = bf16[4,588,1024]{2,1,0:T(8,128)(2,1)} fusion(bf16[4,588,1024]{2,0,1:T(4,128)(2,1)S(1)} %bitcast.579, bf16[8,1024,1024]{2,1,0:T(8,128)(2,1)S(1)} %bitcast.517), kind=kOutput, calls=%fused_computation.29 | convolution fusion | flops 4934909952 | bytes 11730944 | tf_op jit(solution)/shard_map/dot_general | solution.py:372
  196.9 30.2 %cross_forward.1 = (bf16[1024,1024]{1,0:T(8,128)(2,1)}, f32[2,8,1024]{2,1,0:T(8,128)}) custom-call(s32[5]{0:T(128)} %convert_reduce_fusion.1.starts, s32[4]{0:T(128)} %bitcast.580, bf16[1024,1024]{1,0:T(8,128)(2,1)} %convolution_convert_fusion.10.q_ref, bf16[4,588,1024]{2,1,0:T(8,128)(2,1)} %convert_bitcast_fusion.2.k_ref, ...), custom_call_target="tpu_custom_call" | custom-call | flops 13564379136 | bytes 20971520 | tf_op jit(solution)/shard_map/cross_forward/pallas_call | solution.py:266
  227.1 6.1 fusion.93
  235.8 14.1 %all-gather.5.cloned.1.call-done.rows_ref = bf16[2,4096,1024]{2,1,0:T(8,128)(2,1)} async-done(((bf16[2,128,1024]{2,1,0:T(8,128)(2,1)}), bf16[2,4096,1024]{2,1,0:T(8,128)(2,1)}) %all-gather.5.cloned.1.call-update) | async-done | bytes 16777232 | tf_op jit(solution)/shard_map/all_gather | solution.py:535
  249.9 18.8 %multiply_convert_fusion.1 = (bf16[1024,4096]{1,0:T(8,128)(2,1)}, f32[1024,4096]{1,0:T(8,128)}) fusion(bf16[2,4096,1024]{2,1,0:T(8,128)(2,1)} %all-gather.5.cloned.1.call-done.rows_ref, f32[1024,1024]{1,0:T(8,128)} %copy-done.4, f32[1024]{0:T(1024)S(1)} %bitcast.575, f32[1024]{0:T(1024)S(1)} %bitcast.557, f32[1024]{0:T(1024)S(1)} %add_rsqrt_fusion, ...), kind=kOutput, calls=%fused_computation.7 | convolution fusion | flops 8616148992 | bytes 37765120 | tf_op jit(solution)/shard_map/dot_general | solution.py:372
  268.7 11.3 %convolution_convert_fusion.1 = bf16[4096,1024]{0,1:T(8,128)(2,1)S(1)} fusion(bf16[1024,4096]{1,0:T(8,128)(2,1)} %get-tuple-element.139, bf16[1,1024,1024]{2,1,0:T(8,128)(2,1)S(1)} %copy-done.19), kind=kOutput, calls=%fused_computation.15 | convolution fusion | flops 8594128896 | bytes 18874368 | tf_op jit(solution)/shard_map/dot_general | solution.py:372
  284.8 9.0 %side_by_side.1 = bf16[1024,4096]{1,0:T(8,128)(2,1)} custom-call(bf16[2,4096,1024]{2,1,0:T(8,128)(2,1)} %all-gather.5.cloned.1.call-done.rows_ref), custom_call_target="tpu_custom_call" | custom-call | bytes 16777216 | tf_op jit(solution)/shard_map/side_by_side/pallas_call | solution.py:492
  293.8 17.8 %multiply_convert_fusion = bf16[1024,4096]{1,0:T(8,128)(2,1)} fusion(bf16[1024,1024]{1,0:T(8,128)(2,1)S(1)} %bitcast.541, bf16[1024,4096]{1,0:T(8,128)(2,1)} %side_by_side.1, f32[1024,4096]{1,0:T(8,128)} %get-tuple-element.251), kind=kOutput, calls=%fused_computation.6 | convolution fusion | flops 8640266240 | bytes 35651584 | tf_op jit(solution)/shard_map/dot_general | solution.py:372
  311.7 12.7 %convolution_convert_fusion = bf16[4096,1024]{1,0:T(8,128)(2,1)S(1)} fusion(bf16[1024,4096]{1,0:T(8,128)(2,1)} %multiply_convert_fusion, f32[1024,1024]{1,0:T(8,128)S(1)} %copy-done.5, f32[1024]{0:T(1024)S(1)} %bitcast.576, f32[1024]{0:T(1024)S(1)} %bitcast.558, f32[1024]{0:T(1024)S(1)} %add_rsqrt_fusion, f32[1024]{0:T(1024)S(1)} %broadcast_multiply_fusion.6), kind=kOutput, calls=%fused_computation.14 | convolution fusion | flops 8599371776 | bytes 20987904 | tf_op jit(solution)/shard_map/dot_general | solution.py:372
  335.0 14.8 %multiply_reduce_fusion = (f32[1024]{0:T(1024)S(1)}, f32[1024]{0:T(1024)S(1)}, f32[1024]{0:T(1024)S(1)}, f32[1024]{0:T(1024)S(1)}, f32[1024,1024]{1,0:T(8,128)S(1)}) fusion(f32[1024,1024]{1,0:T(8,128)S(1)} %copy-done.6, f32[1024]{0:T(1024)S(1)} %add_rsqrt_fusion, f32[1024]{0:T(1024)S(1)} %broadcast_multiply_fusion.6, f32[1024]{0:T(1024)S(1)} %bitcast.559, ...), kind=kOutput, calls=%fused_computation.57 | convolution fusion | flops 8599367680 | bytes 25194496 | tf_op jit(solution)/shard_map/dot_general | solution.py:372
  366.9 49.4 %cross_backward.1 = (bf16[1024,1024]{1,0:T(8,128)(2,1)}, bf16[4,588,1024]{2,1,0:T(8,128)(2,1)}, bf16[4,588,1024]{2,1,0:T(8,128)(2,1)}) custom-call(s32[5]{0:T(128)} %convert_reduce_fusion.1.starts, s32[4]{0:T(128)} %bitcast.581, bf16[1024,1024]{1,0:T(8,128)(2,1)} %convolution_convert_fusion.10.q_ref, bf16[4,588,1024]{2,1,0:T(8,128)(2,1)} %convert_bitcast_fusion.2.k_ref, ...), custom_call_target="tpu_custom_call" | custom-call | flops 33910947840 | bytes 31457280 | tf_op jit(solution)/shard_map/cross_backward/pallas_call | solution.py:290
  416.3 10.2 %collective-permute-done.8 = bf16[1,2,2,2,128,1024]{5,4,3,2,1,0:T(8,128)(2,1)S(1)} collective-permute-done((bf16[1,2,2,2,128,1024]{5,4,3,2,1,0:T(8,128)(2,1)}, bf16[1,2,2,2,128,1024]{5,4,3,2,1,0:T(8,128)(2,1)S(1)}, u32[]{:S(2)}, u32[]{:S(2)}) %collective-permute-start.8) | collective-permute-done | bytes 2097184 | tf_op jit(solution)/shard_map/ppermute | solution.py:399
  437.7 10.4 %bitcast_convert_fusion.1 = bf16[1024,1024]{1,0:T(8,128)(2,1)S(1)} fusion(bf16[4,588,1024]{2,1,0:T(8,128)(2,1)} %get-tuple-element.133, bf16[4,588,1024]{2,0,1:T(4,128)(2,1)} %param.22), kind=kOutput, calls=%fused_computation.56 | convolution fusion | flops 4933550080 | bytes 11730944 | tf_op jit(solution)/shard_map/dot_general | solution.py:372
  448.1 10.6 %bitcast_convert_fusion = bf16[1024,1024]{1,0:T(8,128)(2,1)S(1)} fusion(bf16[4,588,1024]{2,1,0:T(8,128)(2,1)} %get-tuple-element.134, bf16[4,588,1024]{2,0,1:T(4,128)(2,1)} %param.22), kind=kOutput, calls=%fused_computation.55 | convolution fusion | flops 4933550080 | bytes 11730944 | tf_op jit(solution)/shard_map/dot_general | solution.py:372
  468.5 7.4 %multiply_reduce_fusion.1 = (f32[1024]{0:T(1024)S(1)}, f32[1024]{0:T(1024)S(1)}, f32[1024]{0:T(1024)S(1)}, f32[1024]{0:T(1024)S(1)}, f32[1024,1024]{1,0:T(8,128)S(1)}) fusion(f32[1024,1024]{1,0:T(8,128)} %copy-done.8, f32[1024]{0:T(1024)S(1)} %copy-done.32, f32[1024]{0:T(1024)S(1)} %copy-done.24, f32[1024]{0:T(1024)S(1)} %bitcast.555, ...), kind=kOutput, calls=%fused_computation.58 | convolution fusion | flops 2156916736 | bytes 12611584 | tf_op jit(solution)/shard_map/dot_general | solution.py:372
  495.7 26.7 %self_backward.1 = (bf16[1024,1024]{1,0:T(8,128)(2,1)}, bf16[1024,1024]{1,0:T(8,128)(2,1)}, bf16[1024,1024]{1,0:T(8,128)(2,1)}) custom-call(s32[5]{0:T(128)} %convert_reduce_fusion.1.starts, bf16[1024,1024]{1,0:T(8,128)(2,1)} %convolution_convert_fusion.13.q_ref, bf16[1024,1024]{1,0:T(8,128)(2,1)} %convolution_convert_fusion.12.k_ref, ...), custom_call_target="tpu_custom_call" | custom-call | flops 13421772800 | bytes 16777216 | tf_op jit(solution)/shard_map/self_backward/pallas_call | solution.py:341
  591.6 15.6 %fusion.36 = f32[4,588,1024]{2,1,0:T(8,128)} fusion(bf16[2048,1024,1]{1,0,2:T(8,128)(2,1)S(1)} %bitcast.524, bf16[4,588,1024]{2,1,0:T(8,128)(2,1)} %get-tuple-element.134, bf16[4,588,1024]{2,1,0:T(8,128)(2,1)} %get-tuple-element.133), kind=kOutput, calls=%fused_computation.76 | convolution fusion | flops 9884270592 | bytes 23461888 | tf_op jit(solution)/shard_map/dot_general | solution.py:372
  611.8 8.1 %collective-permute-done.20 = bf16[2,2,2,2,32,1024]{5,4,0,3,2,1:T(8,128)(2,1)S(1)} collective-permute-done((bf16[2,2,2,2,32,1024]{5,4,0,3,2,1:T(8,128)(2,1)S(1)}, bf16[2,2,2,2,32,1024]{5,4,0,3,2,1:T(8,128)(2,1)S(1)}, u32[]{:S(2)}, u32[]{:S(2)}) %collective-permute-start.20) | collective-permute-done | bytes 1048608 | tf_op jit(solution)/shard_map/ppermute | solution.py:399
  624.4 12.6 %add_convert_fusion = bf16[1024,1024]{1,0:T(8,128)(2,1)} fusion(f32[1024,1024]{1,0:T(8,128)S(1)} %copy-done.7, bf16[1024,4096]{1,0:T(8,128)(2,1)} %get-tuple-element.139, bf16[1024,4096]{1,0:T(8,128)(2,1)S(1)} %bitcast.505), kind=kOutput, calls=%fused_computation.59 | convolution fusion | flops 8592031744 | bytes 23068672 | tf_op jit(solution)/shard_map/dot_general | solution.py:372
  652.6 13.8 %copy.117 = f32[4,588,1024]{2,0,1:T(4,128)} copy(f32[4,588,1024]{2,1,0:T(8,128)} %fusion.36) | data formatting | bytes 19267584
  (336 shorter events, 239.0 us)
Async XLA Ops:
  7.3 126.4 %all-gather.3.cloned.1.call-start = ((), (), s32[]{:S(2)}) async-start(), calls=%async_computation.3 | async-start | bytes 17301504 | tf_op jit(solution)/shard_map/all_gather | solution.py:518
  15.6 234.3 %all-gather.5.cloned.1.call-start = ((), (), s32[]{:S(2)}) async-start(), calls=%async_computation.4 | async-start | bytes 17301504 | tf_op jit(solution)/shard_map/all_gather | solution.py:535
  18.8 622.1 %reduce-scatter.8.cloned.1.call-start = ((), (), s32[]{:S(2)}) async-start(), calls=%async_computation.6 | async-start | bytes 2359296 | tf_op jit(solution)/shard_map/reduce_scatter | solution.py:472
  284.6 27.0 %collective-permute-start.5 = (bf16[1,2,2,2,2,32,4096]{6,5,4,3,2,1,0:T(8,128)(2,1)}, bf16[1,2,2,2,2,32,4096]{6,5,4,3,2,1,0:T(8,128)(2,1)}, u32[]{:S(2)}, u32[]{:S(2)}) collective-permute-start(bf16[1,2,2,2,2,32,4096]{6,5,4,3,2,1,0:T(8,128)(2,1)} %dynamic-slice_bitcast_fusion.1), channel_id=1, source_target_pairs={{0,8},{8,0},{16,24},{24,16},{1,9},{9,1},{17,25},{25,17},{2,10},{10... | collective-permute-start | bytes 12582920 | tf_op jit(solution)/shard_map/ppermute | solution.py:399
  328.8 24.3 %collective-permute-start.6 = (bf16[1,2,2,2,2,128,1024]{6,5,4,3,2,1,0:T(8,128)(2,1)}, bf16[1,2,2,2,2,128,1024]{6,5,4,3,2,1,0:T(8,128)(2,1)}, u32[]{:S(2)}, u32[]{:S(2)}) collective-permute-start(bf16[1,2,2,2,2,128,1024]{6,5,4,3,2,1,0:T(8,128)(2,1)} %dynamic-slice_bitcast_fusion), channel_id=1, source_target_pairs={{0,8},{8,0},{16,24},{24,16},{1,9},{9,1},{17,25},{25,17},{2,10},{10... | collective-permute-start | bytes 12582920 | tf_op jit(solution)/shard_map/ppermute | solution.py:399
  333.6 82.7 %collective-permute-start.7 = (bf16[1,2,2,2,32,4096]{5,4,3,2,1,0:T(8,128)(2,1)}, bf16[1,2,2,2,32,4096]{5,4,3,2,1,0:T(8,128)(2,1)}, u32[]{:S(2)}, u32[]{:S(2)}) collective-permute-start(bf16[1,2,2,2,32,4096]{5,4,3,2,1,0:T(8,128)(2,1)} %fusion.35), channel_id=1, source_target_pairs={{0,16},{8,24},{16,0},{24,8},{1,17},{9,25},{17,1},{25,9},{2,18},{10... | collective-permute-start | bytes 6291464 | tf_op jit(solution)/shard_map/ppermute | solution.py:399
  358.9 67.6 %collective-permute-start.8 = (bf16[1,2,2,2,128,1024]{5,4,3,2,1,0:T(8,128)(2,1)}, bf16[1,2,2,2,128,1024]{5,4,3,2,1,0:T(8,128)(2,1)S(1)}, u32[]{:S(2)}, u32[]{:S(2)}) collective-permute-start(bf16[1,2,2,2,128,1024]{5,4,3,2,1,0:T(8,128)(2,1)} %fusion.34), channel_id=1, source_target_pairs={{0,16},{8,24},{16,0},{24,8},{1,17},{9,25},{17,1},{25,9},{2,18},{10... | collective-permute-start | bytes 6291464 | tf_op jit(solution)/shard_map/ppermute | solution.py:399
  431.9 210.8 %reduce-scatter.10.cloned.1.call-start = ((), (), s32[]{:S(2)}) async-start(), calls=%async_computation.7 | async-start | bytes 2359296
  458.9 20.3 %collective-permute-start.9 = (bf16[1,2,2,2,2,32,1024]{6,5,4,3,2,1,0:T(8,128)(2,1)S(1)}, bf16[1,2,2,2,2,32,1024]{6,5,4,3,2,1,0:T(8,128)(2,1)}, u32[]{:S(2)}, u32[]{:S(2)}) collective-permute-start(bf16[1,2,2,2,2,32,1024]{6,5,4,3,2,1,0:T(8,128)(2,1)S(1)} %dynamic-slice_bitcast_fusion.5), channel_id=1, source_target_pairs={{0,8},{8,0},{16,24},{24,16},{1,9},{9,1},{17,25},{25,17},{2,10},{10... | collective-permute-start | bytes 3145736 | tf_op jit(solution)/shard_map/ppermute | solution.py:399
  460.1 19.1 %collective-permute-start.10 = (bf16[1,2,2,2,2,32,1024]{6,5,4,3,2,1,0:T(8,128)(2,1)}, bf16[1,2,2,2,2,32,1024]{6,5,4,3,2,1,0:T(8,128)(2,1)}, u32[]{:S(2)}, u32[]{:S(2)}) collective-permute-start(bf16[1,2,2,2,2,32,1024]{6,5,4,3,2,1,0:T(8,128)(2,1)} %dynamic-slice_bitcast_fusion.4), channel_id=1, source_target_pairs={{0,8},{8,0},{16,24},{24,16},{1,9},{9,1},{17,25},{25,17},{2,10},{10... | collective-permute-start | bytes 3145736 | tf_op jit(solution)/shard_map/ppermute | solution.py:399
  461.6 17.5 %collective-permute-start.11 = (bf16[1,2,2,2,2,32,1024]{6,5,4,3,2,1,0:T(8,128)(2,1)}, bf16[1,2,2,2,2,32,1024]{6,5,4,3,2,1,0:T(8,128)(2,1)}, u32[]{:S(2)}, u32[]{:S(2)}) collective-permute-start(bf16[1,2,2,2,2,32,1024]{6,5,4,3,2,1,0:T(8,128)(2,1)} %dynamic-slice_bitcast_fusion.3), channel_id=1, source_target_pairs={{0,8},{8,0},{16,24},{24,16},{1,9},{9,1},{17,25},{25,17},{2,10},{10... | collective-permute-start | bytes 3145736 | tf_op jit(solution)/shard_map/ppermute | solution.py:399
  462.8 16.4 %collective-permute-start.12 = (bf16[1,2,2,2,2,32,1024]{6,5,4,3,2,1,0:T(8,128)(2,1)}, bf16[1,2,2,2,2,32,1024]{6,5,4,3,2,1,0:T(8,128)(2,1)}, u32[]{:S(2)}, u32[]{:S(2)}) collective-permute-start(bf16[1,2,2,2,2,32,1024]{6,5,4,3,2,1,0:T(8,128)(2,1)} %dynamic-slice_bitcast_fusion.2), channel_id=1, source_target_pairs={{0,8},{8,0},{16,24},{24,16},{1,9},{9,1},{17,25},{25,17},{2,10},{10... | collective-permute-start | bytes 3145736 | tf_op jit(solution)/shard_map/ppermute | solution.py:399
  468.4 208.3 %reduce-scatter.6.cloned.1.call-start = ((), (), s32[]{:S(2)}) async-start(), calls=%async_computation.5 | async-start | bytes 2359296 | tf_op jit(solution)/shard_map/reduce_scatter | solution.py:472
  482.0 45.3 %collective-permute-start.13 = (bf16[1,2,2,2,32,1024]{5,4,3,2,1,0:T(8,128)(2,1)S(1)}, bf16[1,2,2,2,32,1024]{5,4,3,2,1,0:T(8,128)(2,1)}, u32[]{:S(2)}, u32[]{:S(2)}) collective-permute-start(bf16[1,2,2,2,32,1024]{5,4,3,2,1,0:T(8,128)(2,1)S(1)} %fusion.72), channel_id=1, source_target_pairs={{0,16},{8,24},{16,0},{24,8},{1,17},{9,25},{17,1},{25,9},{2,18},{10... | collective-permute-start | bytes 1572872 | tf_op jit(solution)/shard_map/ppermute | solution.py:399
  485.0 42.3 %collective-permute-start.14 = (bf16[1,2,2,2,32,1024]{5,4,3,2,1,0:T(8,128)(2,1)S(1)}, bf16[1,2,2,2,32,1024]{5,4,3,2,1,0:T(8,128)(2,1)}, u32[]{:S(2)}, u32[]{:S(2)}) collective-permute-start(bf16[1,2,2,2,32,1024]{5,4,3,2,1,0:T(8,128)(2,1)S(1)} %fusion.71), channel_id=1, source_target_pairs={{0,16},{8,24},{16,0},{24,8},{1,17},{9,25},{17,1},{25,9},{2,18},{10... | collective-permute-start | bytes 1572872 | tf_op jit(solution)/shard_map/ppermute | solution.py:399
  487.8 39.5 %collective-permute-start.15 = (bf16[1,2,2,2,32,1024]{5,4,3,2,1,0:T(8,128)(2,1)}, bf16[1,2,2,2,32,1024]{5,4,3,2,1,0:T(8,128)(2,1)}, u32[]{:S(2)}, u32[]{:S(2)}) collective-permute-start(bf16[1,2,2,2,32,1024]{5,4,3,2,1,0:T(8,128)(2,1)} %fusion.70), channel_id=1, source_target_pairs={{0,16},{8,24},{16,0},{24,8},{1,17},{9,25},{17,1},{25,9},{2,18},{10... | collective-permute-start | bytes 1572872 | tf_op jit(solution)/shard_map/ppermute | solution.py:399
  491.5 38.3 %collective-permute-start.16 = (bf16[1,2,2,2,32,1024]{5,4,3,2,1,0:T(8,128)(2,1)}, bf16[1,2,2,2,32,1024]{5,4,3,2,1,0:T(8,128)(2,1)}, u32[]{:S(2)}, u32[]{:S(2)}) collective-permute-start(bf16[1,2,2,2,32,1024]{5,4,3,2,1,0:T(8,128)(2,1)} %fusion.69), channel_id=1, source_target_pairs={{0,16},{8,24},{16,0},{24,8},{1,17},{9,25},{17,1},{25,9},{2,18},{10... | collective-permute-start | bytes 1572872 | tf_op jit(solution)/shard_map/ppermute | solution.py:399
  542.1 44.1 %collective-permute-start.17 = (bf16[2,2,2,2,2,32,1024]{6,5,0,2,4,3,1:T(8,128)(2,1)}, bf16[2,2,2,2,2,32,1024]{6,5,0,2,4,3,1:T(8,128)(2,1)}, u32[]{:S(2)}, u32[]{:S(2)}) collective-permute-start(bf16[2,2,2,2,2,32,1024]{6,5,0,2,4,3,1:T(8,128)(2,1)} %copy_bitcast_fusion.1), channel_id=1, source_target_pairs={{0,8},{8,0},{16,24},{24,16},{1,9},{9,1},{17,25},{25,17},{2,10},{10... | collective-permute-start | bytes 6291464 | tf_op jit(solution)/shard_map/ppermute | solution.py:399
  544.5 41.6 %collective-permute-start.18 = (bf16[2,2,2,2,2,32,1024]{6,5,0,2,4,3,1:T(8,128)(2,1)}, bf16[2,2,2,2,2,32,1024]{6,5,0,2,4,3,1:T(8,128)(2,1)}, u32[]{:S(2)}, u32[]{:S(2)}) collective-permute-start(bf16[2,2,2,2,2,32,1024]{6,5,0,2,4,3,1:T(8,128)(2,1)} %copy_bitcast_fusion), channel_id=1, source_target_pairs={{0,8},{8,0},{16,24},{24,16},{1,9},{9,1},{17,25},{25,17},{2,10},{10... | collective-permute-start | bytes 6291464 | tf_op jit(solution)/shard_map/ppermute | solution.py:399
  590.3 21.4 %collective-permute-start.19 = (bf16[2,2,2,2,32,1024]{5,4,0,3,2,1:T(8,128)(2,1)S(1)}, bf16[2,2,2,2,32,1024]{5,4,0,3,2,1:T(8,128)(2,1)S(1)}, u32[]{:S(2)}, u32[]{:S(2)}) collective-permute-start(bf16[2,2,2,2,32,1024]{5,4,0,3,2,1:T(8,128)(2,1)S(1)} %copy.103), channel_id=1, source_target_pairs={{0,16},{8,24},{16,0},{24,8},{1,17},{9,25},{17,1},{25,9},{2,18},{10... | collective-permute-start | bytes 3145736 | tf_op jit(solution)/shard_map/ppermute | solution.py:399
  590.9 29.0 %collective-permute-start.20 = (bf16[2,2,2,2,32,1024]{5,4,0,3,2,1:T(8,128)(2,1)S(1)}, bf16[2,2,2,2,32,1024]{5,4,0,3,2,1:T(8,128)(2,1)S(1)}, u32[]{:S(2)}, u32[]{:S(2)}) collective-permute-start(bf16[2,2,2,2,32,1024]{5,4,0,3,2,1:T(8,128)(2,1)S(1)} %copy.104), channel_id=1, source_target_pairs={{0,1},{1,0},{2,3},{3,2},{4,5},{5,4},{6,7},{7,6},{8,9},{9,8},{10,11... | collective-permute-start | bytes 3145736 | tf_op jit(solution)/shard_map/ppermute | solution.py:399
  622.9 14.0 %collective-permute-start.21 = (bf16[2,2,2,32,1024]{4,3,0,2,1:T(8,128)(2,1)S(1)}, bf16[2,2,2,32,1024]{4,3,0,2,1:T(8,128)(2,1)S(1)}, u32[]{:S(2)}, u32[]{:S(2)}) collective-permute-start(bf16[2,2,2,32,1024]{4,3,0,2,1:T(8,128)(2,1)S(1)} %copy.108), channel_id=1, source_target_pairs={{0,1},{1,0},{2,3},{3,2},{4,5},{5,4},{6,7},{7,6},{8,9},{9,8},{10,11... | collective-permute-start | bytes 1572872 | tf_op jit(solution)/shard_map/ppermute | solution.py:399
  645.7 20.7 %collective-permute-start.30 = (bf16[2,2,32,1024]{3,2,0,1:T(8,128)(2,1)}, bf16[2,2,32,1024]{3,2,0,1:T(8,128)(2,1)}, u32[]{:S(2)}, u32[]{:S(2)}) collective-permute-start(bf16[2,2,32,1024]{3,2,0,1:T(8,128)(2,1)} %fusion.73), channel_id=1, source_target_pairs={{0,16},{8,24},{16,0},{24,8},{1,17},{9,25},{17,1},{25,9},{2,18},{10... | collective-permute-start | bytes 786440 | tf_op jit(solution)/shard_map/ppermute | solution.py:399
  649.5 18.7 %collective-permute-start.29 = (bf16[2,32,1024]{2,1,0:T(8,128)(2,1)}, bf16[2,32,1024]{2,1,0:T(8,128)(2,1)S(1)}, u32[]{:S(2)}, u32[]{:S(2)}) collective-permute-start(bf16[2,32,1024]{2,1,0:T(8,128)(2,1)} %fusion.77), channel_id=1, source_target_pairs={{0,4},{1,5},{2,6},{3,7},{4,0},{5,1},{6,2},{7,3},{8,12},{9,13},{10,... | collective-permute-start | bytes 393224 | tf_op jit(solution)/shard_map/ppermute | solution.py:399
  (85 other events, 1411.4 us)
Sparse Core Ops, SparseCore 0:
  15.7 117.9 all-gather.2
  137.3 112.5 all-gather.4
  432.0 66.4 reduce-scatter.7
  501.9 67.7 reduce-scatter.9
  576.0 71.7 reduce-scatter.5

commit v7 on v6

--- a/solution.py
+++ b/solution.py
@@ -500,6 +500,22 @@
     )(far)
 
 
+def lower_stack_kernel(*refs):
+    for i, master in enumerate(refs[:-1]):
+        refs[-1][i] = master[...].astype(refs[-1].dtype)
+
+
+def lower_stack(masters):
+    rows, width = masters[0].shape
+    count = len(masters)
+    return pl.pallas_call(
+        lower_stack_kernel,
+        out_shape=jax.ShapeDtypeStruct((count, rows, width), jnp.bfloat16),
+        cost_estimate=cost(0, 6 * count * rows * width, 0),
+        name="lower_stack",
+    )(*masters)
+
+
 def layer(
     sizes, block_in, images, segment_ids, page_map, ln1_gain, ln1_shift, ln2_gain, ln2_shift,
     ln3_gain, ln3_shift, self_query, self_key, self_value, self_out, cross_query, cross_key,
@@ -514,8 +530,7 @@
         return master.astype(low).T
 
     def gather(*masters):
-        stacked = jnp.stack([turned(m) for m in masters])
-        return lax.all_gather(stacked, AXES, axis=1, tiled=True)
+        return lax.all_gather(lower_stack([m.T for m in masters]), AXES, axis=1, tiled=True)
 
     norms = jnp.stack([ln1_gain, ln1_shift, ln2_gain, ln2_shift, ln3_gain, ln3_shift])
     norms = norms.astype(low).astype(jnp.float32)

time: 693 us -> 688 us (level)
  other arithmetic: 82.5 us -> 74.9 us
    unnamed x145 -> x143, local copies, waits for them, and re-layouts: 31.6 us -> 30.8 us
where the time goes in v7:
time: 688 us; the launch traced here: 681 us
  matrix products  219 us (32%)
  waiting for transfers between devices  158 us (23%)
  Pallas kernels  134 us (19%)
  other arithmetic  74.9 us (11%)
  local copies, waits for them, and re-layouts  46.2 us (7%)
  starting transfers between devices  32.7 us (5%)
  between operations  15.3 us (2%)
    dot_general x29, matrix products, contract(): lax.dot_general(a, b, ((left, right), ((), ())), preferred_element_type=j...  219 us
    all_gather x1, waiting for transfers between devices, gather(): lax.all_gather(lower_stack([m.T for m in masters]), AXES, axis=1, tiled=T...  92.6 us
    ppermute x32, waiting for transfers between devices, swap(): return lax.ppermute(value, axis, [(i, i ^ bit) for i in range(size)])  50.9 us
    pallas_call x1, Pallas kernels, cross_backward(): pl.pallas_call(functools.partial(cross_backward_kernel, pairs), out_shape...  49.4 us
    convert_element_type x14, other arithmetic, cut(): return out.astype(jnp.bfloat16)  32.6 us
    ppermute x32, starting transfers between devices, swap(): return lax.ppermute(value, axis, [(i, i ^ bit) for i in range(size)])  32.1 us
    unnamed x143, local copies, waits for them, and re-layouts  30.8 us
    pallas_call x1, Pallas kernels, cross_forward(): pl.pallas_call(functools.partial(cross_forward_kernel, pairs), out_shape=...  30.7 us
  transfers between devices with their start and end apart: 37, of which 16 were waited for; matrix products, arithmetic and copies ran while one was open for 40% of the time, Pallas kernels for 19%

profile of v7, /device:TPU:0, one launch (start us, length us, event | category | flops | bytes accessed | tf_op | source)
XLA Modules:
  0.0 680.7 jit_solution(12061797722776847108)
XLA Ops:
  36.6 92.6 %all-gather.3.cloned.1.call-done = bf16[8,1024,1024]{2,1,0:T(8,128)(2,1)} async-done(((bf16[8,32,1024]{2,1,0:T(8,128)(2,1)}), bf16[8,1024,1024]{2,1,0:T(8,128)(2,1)}) %all-gather.3.cloned.1.call-update) | async-done | bytes 16777232 | tf_op jit(solution)/shard_map/all_gather | solution.py:533
  143.8 17.5 %self_forward.1 = (bf16[1024,1024]{1,0:T(8,128)(2,1)}, f32[2,8,1024]{2,1,0:T(8,128)}) custom-call(s32[5]{0:T(128)} %convert_reduce_fusion.1.starts, bf16[1024,1024]{1,0:T(8,128)(2,1)} %convolution_convert_fusion.13.q_ref, bf16[1024,1024]{1,0:T(8,128)(2,1)} %convolution_convert_fusion.12.k_ref, bf16[1024,1024]{1,0:T(8,128)(2,1)} %convolution_convert_fusion.11.v_ref), custom_call_target="tpu_custom_call" | custom-call | flops 5368709120 | bytes 10485760 | tf_op jit(solution)/shard_map/self_forward/pallas_call | solution.py:318
  168.2 6.2 convolution_convert_fusion.10.q_ref
  176.2 7.7 %convert_bitcast_fusion.2.k_ref = bf16[4,588,1024]{2,1,0:T(8,128)(2,1)} fusion(bf16[4,588,1024]{2,0,1:T(4,128)(2,1)S(1)} %bitcast.563, bf16[8,1024,1024]{2,1,0:T(8,128)(2,1)S(1)} %bitcast.493), kind=kOutput, calls=%fused_computation.30 | convolution fusion | flops 4934909952 | bytes 11730944 | tf_op jit(solution)/shard_map/dot_general | solution.py:372
  183.9 7.8 %convert_bitcast_fusion.1.v_ref = bf16[4,588,1024]{2,1,0:T(8,128)(2,1)} fusion(bf16[4,588,1024]{2,0,1:T(4,128)(2,1)S(1)} %bitcast.563, bf16[8,1024,1024]{2,1,0:T(8,128)(2,1)S(1)} %bitcast.493), kind=kOutput, calls=%fused_computation.29 | convolution fusion | flops 4934909952 | bytes 11730944 | tf_op jit(solution)/shard_map/dot_general | solution.py:372
  191.7 30.7 %cross_forward.1 = (bf16[1024,1024]{1,0:T(8,128)(2,1)}, f32[2,8,1024]{2,1,0:T(8,128)}) custom-call(s32[5]{0:T(128)} %convert_reduce_fusion.1.starts, s32[4]{0:T(128)} %bitcast.564, bf16[1024,1024]{1,0:T(8,128)(2,1)} %convolution_convert_fusion.10.q_ref, bf16[4,588,1024]{2,1,0:T(8,128)(2,1)} %convert_bitcast_fusion.2.k_ref, ...), custom_call_target="tpu_custom_call" | custom-call | flops 13564379136 | bytes 20971520 | tf_op jit(solution)/shard_map/cross_forward/pallas_call | solution.py:266
  222.4 6.0 fusion.93
  231.0 14.5 %all-gather.5.cloned.1.call-done.rows_ref = bf16[2,4096,1024]{2,1,0:T(8,128)(2,1)} async-done(((bf16[2,128,1024]{2,1,0:T(8,128)(2,1)}), bf16[2,4096,1024]{2,1,0:T(8,128)(2,1)}) %all-gather.5.cloned.1.call-update) | async-done | bytes 16777232 | tf_op jit(solution)/shard_map/all_gather | solution.py:550
  245.5 18.7 %multiply_convert_fusion.1 = (bf16[1024,4096]{1,0:T(8,128)(2,1)}, f32[1024,4096]{1,0:T(8,128)}) fusion(bf16[2,4096,1024]{2,1,0:T(8,128)(2,1)} %all-gather.5.cloned.1.call-done.rows_ref, f32[1024,1024]{1,0:T(8,128)} %copy-done.4, f32[1024]{0:T(1024)S(1)} %bitcast.559, f32[1024]{0:T(1024)S(1)} %bitcast.541, f32[1024]{0:T(1024)S(1)} %add_rsqrt_fusion, ...), kind=kOutput, calls=%fused_computation.7 | convolution fusion | flops 8616148992 | bytes 37765120 | tf_op jit(solution)/shard_map/dot_general | solution.py:372
  264.2 11.3 %convolution_convert_fusion.1 = bf16[4096,1024]{0,1:T(8,128)(2,1)S(1)} fusion(bf16[1024,4096]{1,0:T(8,128)(2,1)} %get-tuple-element.139, bf16[1,1024,1024]{2,1,0:T(8,128)(2,1)S(1)} %copy-done.19), kind=kOutput, calls=%fused_computation.15 | convolution fusion | flops 8594128896 | bytes 18874368 | tf_op jit(solution)/shard_map/dot_general | solution.py:372
  280.4 9.0 %side_by_side.1 = bf16[1024,4096]{1,0:T(8,128)(2,1)} custom-call(bf16[2,4096,1024]{2,1,0:T(8,128)(2,1)} %all-gather.5.cloned.1.call-done.rows_ref), custom_call_target="tpu_custom_call" | custom-call | bytes 16777216 | tf_op jit(solution)/shard_map/side_by_side/pallas_call | solution.py:492
  289.4 17.8 %multiply_convert_fusion = bf16[1024,4096]{1,0:T(8,128)(2,1)} fusion(bf16[1024,1024]{1,0:T(8,128)(2,1)S(1)} %bitcast.517, bf16[1024,4096]{1,0:T(8,128)(2,1)} %side_by_side.1, f32[1024,4096]{1,0:T(8,128)} %get-tuple-element.251), kind=kOutput, calls=%fused_computation.6 | convolution fusion | flops 8640266240 | bytes 35651584 | tf_op jit(solution)/shard_map/dot_general | solution.py:372
  307.2 12.7 %convolution_convert_fusion = bf16[4096,1024]{1,0:T(8,128)(2,1)S(1)} fusion(bf16[1024,4096]{1,0:T(8,128)(2,1)} %multiply_convert_fusion, f32[1024,1024]{1,0:T(8,128)S(1)} %copy-done.5, f32[1024]{0:T(1024)S(1)} %bitcast.560, f32[1024]{0:T(1024)S(1)} %bitcast.542, f32[1024]{0:T(1024)S(1)} %add_rsqrt_fusion, f32[1024]{0:T(1024)S(1)} %broadcast_multiply_fusion.6), kind=kOutput, calls=%fused_computation.14 | convolution fusion | flops 8599371776 | bytes 20987904 | tf_op jit(solution)/shard_map/dot_general | solution.py:372
  330.5 14.8 %multiply_reduce_fusion = (f32[1024]{0:T(1024)S(1)}, f32[1024]{0:T(1024)S(1)}, f32[1024]{0:T(1024)S(1)}, f32[1024]{0:T(1024)S(1)}, f32[1024,1024]{1,0:T(8,128)S(1)}) fusion(f32[1024,1024]{1,0:T(8,128)S(1)} %copy-done.6, f32[1024]{0:T(1024)S(1)} %add_rsqrt_fusion, f32[1024]{0:T(1024)S(1)} %broadcast_multiply_fusion.6, f32[1024]{0:T(1024)S(1)} %bitcast.543, ...), kind=kOutput, calls=%fused_computation.57 | convolution fusion | flops 8599367680 | bytes 25194496 | tf_op jit(solution)/shard_map/dot_general | solution.py:372
  362.5 49.4 %cross_backward.1 = (bf16[1024,1024]{1,0:T(8,128)(2,1)}, bf16[4,588,1024]{2,1,0:T(8,128)(2,1)}, bf16[4,588,1024]{2,1,0:T(8,128)(2,1)}) custom-call(s32[5]{0:T(128)} %convert_reduce_fusion.1.starts, s32[4]{0:T(128)} %bitcast.565, bf16[1024,1024]{1,0:T(8,128)(2,1)} %convolution_convert_fusion.10.q_ref, bf16[4,588,1024]{2,1,0:T(8,128)(2,1)} %convert_bitcast_fusion.2.k_ref, ...), custom_call_target="tpu_custom_call" | custom-call | flops 33910947840 | bytes 31457280 | tf_op jit(solution)/shard_map/cross_backward/pallas_call | solution.py:290
  411.8 10.2 %collective-permute-done.8 = bf16[1,2,2,2,128,1024]{5,4,3,2,1,0:T(8,128)(2,1)S(1)} collective-permute-done((bf16[1,2,2,2,128,1024]{5,4,3,2,1,0:T(8,128)(2,1)}, bf16[1,2,2,2,128,1024]{5,4,3,2,1,0:T(8,128)(2,1)S(1)}, u32[]{:S(2)}, u32[]{:S(2)}) %collective-permute-start.8) | collective-permute-done | bytes 2097184 | tf_op jit(solution)/shard_map/ppermute | solution.py:399
  433.2 10.4 %bitcast_convert_fusion.1 = bf16[1024,1024]{1,0:T(8,128)(2,1)S(1)} fusion(bf16[4,588,1024]{2,1,0:T(8,128)(2,1)} %get-tuple-element.133, bf16[4,588,1024]{2,0,1:T(4,128)(2,1)} %param.22), kind=kOutput, calls=%fused_computation.56 | convolution fusion | flops 4933550080 | bytes 11730944 | tf_op jit(solution)/shard_map/dot_general | solution.py:372
  443.7 10.6 %bitcast_convert_fusion = bf16[1024,1024]{1,0:T(8,128)(2,1)S(1)} fusion(bf16[4,588,1024]{2,1,0:T(8,128)(2,1)} %get-tuple-element.134, bf16[4,588,1024]{2,0,1:T(4,128)(2,1)} %param.22), kind=kOutput, calls=%fused_computation.55 | convolution fusion | flops 4933550080 | bytes 11730944 | tf_op jit(solution)/shard_map/dot_general | solution.py:372
  464.1 7.4 %multiply_reduce_fusion.1 = (f32[1024]{0:T(1024)S(1)}, f32[1024]{0:T(1024)S(1)}, f32[1024]{0:T(1024)S(1)}, f32[1024]{0:T(1024)S(1)}, f32[1024,1024]{1,0:T(8,128)S(1)}) fusion(f32[1024,1024]{1,0:T(8,128)} %copy-done.8, f32[1024]{0:T(1024)S(1)} %copy-done.31, f32[1024]{0:T(1024)S(1)} %copy-done.23, f32[1024]{0:T(1024)S(1)} %bitcast.539, ...), kind=kOutput, calls=%fused_computation.58 | convolution fusion | flops 2156916736 | bytes 12611584 | tf_op jit(solution)/shard_map/dot_general | solution.py:372
  491.2 25.2 %self_backward.1 = (bf16[1024,1024]{1,0:T(8,128)(2,1)}, bf16[1024,1024]{1,0:T(8,128)(2,1)}, bf16[1024,1024]{1,0:T(8,128)(2,1)}) custom-call(s32[5]{0:T(128)} %convert_reduce_fusion.1.starts, bf16[1024,1024]{1,0:T(8,128)(2,1)} %convolution_convert_fusion.13.q_ref, bf16[1024,1024]{1,0:T(8,128)(2,1)} %convolution_convert_fusion.12.k_ref, ...), custom_call_target="tpu_custom_call" | custom-call | flops 13421772800 | bytes 16777216 | tf_op jit(solution)/shard_map/self_backward/pallas_call | solution.py:341
  587.1 15.6 %fusion.36 = f32[4,588,1024]{2,1,0:T(8,128)} fusion(bf16[2048,1024,1]{1,0,2:T(8,128)(2,1)S(1)} %bitcast.500, bf16[4,588,1024]{2,1,0:T(8,128)(2,1)} %get-tuple-element.134, bf16[4,588,1024]{2,1,0:T(8,128)(2,1)} %get-tuple-element.133), kind=kOutput, calls=%fused_computation.76 | convolution fusion | flops 9884270592 | bytes 23461888 | tf_op jit(solution)/shard_map/dot_general | solution.py:372
  607.3 8.9 %collective-permute-done.20 = bf16[2,2,2,2,32,1024]{5,4,0,3,2,1:T(8,128)(2,1)S(1)} collective-permute-done((bf16[2,2,2,2,32,1024]{5,4,0,3,2,1:T(8,128)(2,1)S(1)}, bf16[2,2,2,2,32,1024]{5,4,0,3,2,1:T(8,128)(2,1)S(1)}, u32[]{:S(2)}, u32[]{:S(2)}) %collective-permute-start.20) | collective-permute-done | bytes 1048608 | tf_op jit(solution)/shard_map/ppermute | solution.py:399
  620.4 12.6 %add_convert_fusion = bf16[1024,1024]{1,0:T(8,128)(2,1)} fusion(f32[1024,1024]{1,0:T(8,128)S(1)} %copy-done.7, bf16[1024,4096]{1,0:T(8,128)(2,1)} %get-tuple-element.139, bf16[1024,4096]{1,0:T(8,128)(2,1)S(1)} %bitcast.481), kind=kOutput, calls=%fused_computation.59 | convolution fusion | flops 8592031744 | bytes 23068672 | tf_op jit(solution)/shard_map/dot_general | solution.py:372
  648.1 13.8 %copy.117 = f32[4,588,1024]{2,0,1:T(4,128)} copy(f32[4,588,1024]{2,1,0:T(8,128)} %fusion.36) | data formatting | bytes 19267584
  (327 shorter events, 234.1 us)
Async XLA Ops:
  7.3 121.9 %all-gather.3.cloned.1.call-start = ((), (), s32[]{:S(2)}) async-start(), calls=%async_computation.3 | async-start | bytes 17301504 | tf_op jit(solution)/shard_map/all_gather | solution.py:533
  9.6 235.8 %all-gather.5.cloned.1.call-start = ((), (), s32[]{:S(2)}) async-start(), calls=%async_computation.4 | async-start | bytes 17301504 | tf_op jit(solution)/shard_map/all_gather | solution.py:550
  12.8 623.1 %reduce-scatter.8.cloned.1.call-start = ((), (), s32[]{:S(2)}) async-start(), calls=%async_computation.6 | async-start | bytes 2359296 | tf_op jit(solution)/shard_map/reduce_scatter | solution.py:472
  280.2 27.1 %collective-permute-start.5 = (bf16[1,2,2,2,2,32,4096]{6,5,4,3,2,1,0:T(8,128)(2,1)}, bf16[1,2,2,2,2,32,4096]{6,5,4,3,2,1,0:T(8,128)(2,1)}, u32[]{:S(2)}, u32[]{:S(2)}) collective-permute-start(bf16[1,2,2,2,2,32,4096]{6,5,4,3,2,1,0:T(8,128)(2,1)} %dynamic-slice_bitcast_fusion.1), channel_id=1, source_target_pairs={{0,8},{8,0},{16,24},{24,16},{1,9},{9,1},{17,25},{25,17},{2,10},{10... | collective-permute-start | bytes 12582920 | tf_op jit(solution)/shard_map/ppermute | solution.py:399
  324.4 24.3 %collective-permute-start.6 = (bf16[1,2,2,2,2,128,1024]{6,5,4,3,2,1,0:T(8,128)(2,1)}, bf16[1,2,2,2,2,128,1024]{6,5,4,3,2,1,0:T(8,128)(2,1)}, u32[]{:S(2)}, u32[]{:S(2)}) collective-permute-start(bf16[1,2,2,2,2,128,1024]{6,5,4,3,2,1,0:T(8,128)(2,1)} %dynamic-slice_bitcast_fusion), channel_id=1, source_target_pairs={{0,8},{8,0},{16,24},{24,16},{1,9},{9,1},{17,25},{25,17},{2,10},{10... | collective-permute-start | bytes 12582920 | tf_op jit(solution)/shard_map/ppermute | solution.py:399
  329.1 82.7 %collective-permute-start.7 = (bf16[1,2,2,2,32,4096]{5,4,3,2,1,0:T(8,128)(2,1)}, bf16[1,2,2,2,32,4096]{5,4,3,2,1,0:T(8,128)(2,1)}, u32[]{:S(2)}, u32[]{:S(2)}) collective-permute-start(bf16[1,2,2,2,32,4096]{5,4,3,2,1,0:T(8,128)(2,1)} %fusion.35), channel_id=1, source_target_pairs={{0,16},{8,24},{16,0},{24,8},{1,17},{9,25},{17,1},{25,9},{2,18},{10... | collective-permute-start | bytes 6291464 | tf_op jit(solution)/shard_map/ppermute | solution.py:399
  354.4 67.6 %collective-permute-start.8 = (bf16[1,2,2,2,128,1024]{5,4,3,2,1,0:T(8,128)(2,1)}, bf16[1,2,2,2,128,1024]{5,4,3,2,1,0:T(8,128)(2,1)S(1)}, u32[]{:S(2)}, u32[]{:S(2)}) collective-permute-start(bf16[1,2,2,2,128,1024]{5,4,3,2,1,0:T(8,128)(2,1)} %fusion.34), channel_id=1, source_target_pairs={{0,16},{8,24},{16,0},{24,8},{1,17},{9,25},{17,1},{25,9},{2,18},{10... | collective-permute-start | bytes 6291464 | tf_op jit(solution)/shard_map/ppermute | solution.py:399
  427.4 210.2 %reduce-scatter.10.cloned.1.call-start = ((), (), s32[]{:S(2)}) async-start(), calls=%async_computation.7 | async-start | bytes 2359296
  454.4 20.3 %collective-permute-start.9 = (bf16[1,2,2,2,2,32,1024]{6,5,4,3,2,1,0:T(8,128)(2,1)S(1)}, bf16[1,2,2,2,2,32,1024]{6,5,4,3,2,1,0:T(8,128)(2,1)}, u32[]{:S(2)}, u32[]{:S(2)}) collective-permute-start(bf16[1,2,2,2,2,32,1024]{6,5,4,3,2,1,0:T(8,128)(2,1)S(1)} %dynamic-slice_bitcast_fusion.5), channel_id=1, source_target_pairs={{0,8},{8,0},{16,24},{24,16},{1,9},{9,1},{17,25},{25,17},{2,10},{10... | collective-permute-start | bytes 3145736 | tf_op jit(solution)/shard_map/ppermute | solution.py:399
  455.6 19.1 %collective-permute-start.10 = (bf16[1,2,2,2,2,32,1024]{6,5,4,3,2,1,0:T(8,128)(2,1)}, bf16[1,2,2,2,2,32,1024]{6,5,4,3,2,1,0:T(8,128)(2,1)}, u32[]{:S(2)}, u32[]{:S(2)}) collective-permute-start(bf16[1,2,2,2,2,32,1024]{6,5,4,3,2,1,0:T(8,128)(2,1)} %dynamic-slice_bitcast_fusion.4), channel_id=1, source_target_pairs={{0,8},{8,0},{16,24},{24,16},{1,9},{9,1},{17,25},{25,17},{2,10},{10... | collective-permute-start | bytes 3145736 | tf_op jit(solution)/shard_map/ppermute | solution.py:399
  457.2 17.5 %collective-permute-start.11 = (bf16[1,2,2,2,2,32,1024]{6,5,4,3,2,1,0:T(8,128)(2,1)}, bf16[1,2,2,2,2,32,1024]{6,5,4,3,2,1,0:T(8,128)(2,1)}, u32[]{:S(2)}, u32[]{:S(2)}) collective-permute-start(bf16[1,2,2,2,2,32,1024]{6,5,4,3,2,1,0:T(8,128)(2,1)} %dynamic-slice_bitcast_fusion.3), channel_id=1, source_target_pairs={{0,8},{8,0},{16,24},{24,16},{1,9},{9,1},{17,25},{25,17},{2,10},{10... | collective-permute-start | bytes 3145736 | tf_op jit(solution)/shard_map/ppermute | solution.py:399
  458.3 16.4 %collective-permute-start.12 = (bf16[1,2,2,2,2,32,1024]{6,5,4,3,2,1,0:T(8,128)(2,1)}, bf16[1,2,2,2,2,32,1024]{6,5,4,3,2,1,0:T(8,128)(2,1)}, u32[]{:S(2)}, u32[]{:S(2)}) collective-permute-start(bf16[1,2,2,2,2,32,1024]{6,5,4,3,2,1,0:T(8,128)(2,1)} %dynamic-slice_bitcast_fusion.2), channel_id=1, source_target_pairs={{0,8},{8,0},{16,24},{24,16},{1,9},{9,1},{17,25},{25,17},{2,10},{10... | collective-permute-start | bytes 3145736 | tf_op jit(solution)/shard_map/ppermute | solution.py:399
  464.0 208.2 %reduce-scatter.6.cloned.1.call-start = ((), (), s32[]{:S(2)}) async-start(), calls=%async_computation.5 | async-start | bytes 2359296 | tf_op jit(solution)/shard_map/reduce_scatter | solution.py:472
  477.6 43.8 %collective-permute-start.13 = (bf16[1,2,2,2,32,1024]{5,4,3,2,1,0:T(8,128)(2,1)S(1)}, bf16[1,2,2,2,32,1024]{5,4,3,2,1,0:T(8,128)(2,1)}, u32[]{:S(2)}, u32[]{:S(2)}) collective-permute-start(bf16[1,2,2,2,32,1024]{5,4,3,2,1,0:T(8,128)(2,1)S(1)} %fusion.72), channel_id=1, source_target_pairs={{0,16},{8,24},{16,0},{24,8},{1,17},{9,25},{17,1},{25,9},{2,18},{10... | collective-permute-start | bytes 1572872 | tf_op jit(solution)/shard_map/ppermute | solution.py:399
  480.5 41.0 %collective-permute-start.14 = (bf16[1,2,2,2,32,1024]{5,4,3,2,1,0:T(8,128)(2,1)S(1)}, bf16[1,2,2,2,32,1024]{5,4,3,2,1,0:T(8,128)(2,1)}, u32[]{:S(2)}, u32[]{:S(2)}) collective-permute-start(bf16[1,2,2,2,32,1024]{5,4,3,2,1,0:T(8,128)(2,1)S(1)} %fusion.71), channel_id=1, source_target_pairs={{0,16},{8,24},{16,0},{24,8},{1,17},{9,25},{17,1},{25,9},{2,18},{10... | collective-permute-start | bytes 1572872 | tf_op jit(solution)/shard_map/ppermute | solution.py:399
  483.3 38.1 %collective-permute-start.15 = (bf16[1,2,2,2,32,1024]{5,4,3,2,1,0:T(8,128)(2,1)}, bf16[1,2,2,2,32,1024]{5,4,3,2,1,0:T(8,128)(2,1)}, u32[]{:S(2)}, u32[]{:S(2)}) collective-permute-start(bf16[1,2,2,2,32,1024]{5,4,3,2,1,0:T(8,128)(2,1)} %fusion.70), channel_id=1, source_target_pairs={{0,16},{8,24},{16,0},{24,8},{1,17},{9,25},{17,1},{25,9},{2,18},{10... | collective-permute-start | bytes 1572872 | tf_op jit(solution)/shard_map/ppermute | solution.py:399
  487.0 38.3 %collective-permute-start.16 = (bf16[1,2,2,2,32,1024]{5,4,3,2,1,0:T(8,128)(2,1)}, bf16[1,2,2,2,32,1024]{5,4,3,2,1,0:T(8,128)(2,1)}, u32[]{:S(2)}, u32[]{:S(2)}) collective-permute-start(bf16[1,2,2,2,32,1024]{5,4,3,2,1,0:T(8,128)(2,1)} %fusion.69), channel_id=1, source_target_pairs={{0,16},{8,24},{16,0},{24,8},{1,17},{9,25},{17,1},{25,9},{2,18},{10... | collective-permute-start | bytes 1572872 | tf_op jit(solution)/shard_map/ppermute | solution.py:399
  537.6 43.1 %collective-permute-start.17 = (bf16[2,2,2,2,2,32,1024]{6,5,0,2,4,3,1:T(8,128)(2,1)}, bf16[2,2,2,2,2,32,1024]{6,5,0,2,4,3,1:T(8,128)(2,1)}, u32[]{:S(2)}, u32[]{:S(2)}) collective-permute-start(bf16[2,2,2,2,2,32,1024]{6,5,0,2,4,3,1:T(8,128)(2,1)} %copy_bitcast_fusion.1), channel_id=1, source_target_pairs={{0,8},{8,0},{16,24},{24,16},{1,9},{9,1},{17,25},{25,17},{2,10},{10... | collective-permute-start | bytes 6291464 | tf_op jit(solution)/shard_map/ppermute | solution.py:399
  540.1 40.7 %collective-permute-start.18 = (bf16[2,2,2,2,2,32,1024]{6,5,0,2,4,3,1:T(8,128)(2,1)}, bf16[2,2,2,2,2,32,1024]{6,5,0,2,4,3,1:T(8,128)(2,1)}, u32[]{:S(2)}, u32[]{:S(2)}) collective-permute-start(bf16[2,2,2,2,2,32,1024]{6,5,0,2,4,3,1:T(8,128)(2,1)} %copy_bitcast_fusion), channel_id=1, source_target_pairs={{0,8},{8,0},{16,24},{24,16},{1,9},{9,1},{17,25},{25,17},{2,10},{10... | collective-permute-start | bytes 6291464 | tf_op jit(solution)/shard_map/ppermute | solution.py:399
  584.9 22.4 %collective-permute-start.19 = (bf16[2,2,2,2,32,1024]{5,4,0,3,2,1:T(8,128)(2,1)S(1)}, bf16[2,2,2,2,32,1024]{5,4,0,3,2,1:T(8,128)(2,1)S(1)}, u32[]{:S(2)}, u32[]{:S(2)}) collective-permute-start(bf16[2,2,2,2,32,1024]{5,4,0,3,2,1:T(8,128)(2,1)S(1)} %copy.103), channel_id=1, source_target_pairs={{0,16},{8,24},{16,0},{24,8},{1,17},{9,25},{17,1},{25,9},{2,18},{10... | collective-permute-start | bytes 3145736 | tf_op jit(solution)/shard_map/ppermute | solution.py:399
  587.0 29.2 %collective-permute-start.20 = (bf16[2,2,2,2,32,1024]{5,4,0,3,2,1:T(8,128)(2,1)S(1)}, bf16[2,2,2,2,32,1024]{5,4,0,3,2,1:T(8,128)(2,1)S(1)}, u32[]{:S(2)}, u32[]{:S(2)}) collective-permute-start(bf16[2,2,2,2,32,1024]{5,4,0,3,2,1:T(8,128)(2,1)S(1)} %copy.104), channel_id=1, source_target_pairs={{0,1},{1,0},{2,3},{3,2},{4,5},{5,4},{6,7},{7,6},{8,9},{9,8},{10,11... | collective-permute-start | bytes 3145736 | tf_op jit(solution)/shard_map/ppermute | solution.py:399
  619.2 13.8 %collective-permute-start.21 = (bf16[2,2,2,32,1024]{4,3,0,2,1:T(8,128)(2,1)S(1)}, bf16[2,2,2,32,1024]{4,3,0,2,1:T(8,128)(2,1)S(1)}, u32[]{:S(2)}, u32[]{:S(2)}) collective-permute-start(bf16[2,2,2,32,1024]{4,3,0,2,1:T(8,128)(2,1)S(1)} %copy.108), channel_id=1, source_target_pairs={{0,1},{1,0},{2,3},{3,2},{4,5},{5,4},{6,7},{7,6},{8,9},{9,8},{10,11... | collective-permute-start | bytes 1572872 | tf_op jit(solution)/shard_map/ppermute | solution.py:399
  640.7 21.2 %collective-permute-start.30 = (bf16[2,2,32,1024]{3,2,0,1:T(8,128)(2,1)}, bf16[2,2,32,1024]{3,2,0,1:T(8,128)(2,1)}, u32[]{:S(2)}, u32[]{:S(2)}) collective-permute-start(bf16[2,2,32,1024]{3,2,0,1:T(8,128)(2,1)} %fusion.73), channel_id=1, source_target_pairs={{0,16},{8,24},{16,0},{24,8},{1,17},{9,25},{17,1},{25,9},{2,18},{10... | collective-permute-start | bytes 786440 | tf_op jit(solution)/shard_map/ppermute | solution.py:399
  645.2 18.7 %collective-permute-start.29 = (bf16[2,32,1024]{2,1,0:T(8,128)(2,1)}, bf16[2,32,1024]{2,1,0:T(8,128)(2,1)S(1)}, u32[]{:S(2)}, u32[]{:S(2)}) collective-permute-start(bf16[2,32,1024]{2,1,0:T(8,128)(2,1)} %fusion.77), channel_id=1, source_target_pairs={{0,4},{1,5},{2,6},{3,7},{4,0},{5,1},{6,2},{7,3},{8,12},{9,13},{10,... | collective-permute-start | bytes 393224 | tf_op jit(solution)/shard_map/ppermute | solution.py:399
  (84 other events, 1386.9 us)
Sparse Core Ops, SparseCore 0:
  11.7 117.4 all-gather.2
  132.8 112.5 all-gather.4
  427.5 66.4 reduce-scatter.7
  497.4 67.3 reduce-scatter.9
  571.9 71.5 reduce-scatter.5

commit v8 on v7

--- a/solution.py
+++ b/solution.py
@@ -656,7 +656,10 @@
         return (x2 + contract(hidden, w_out, (1,), (1,))).astype(low)
 
     grad_in, gg1, gs1 = norm_one(d1)
-    grad_in, hidden, dck, dcv, *flights = fence(grad_in, hidden, dck, dcv, *flights)
+    norm_grads = jnp.stack([gg1, gs1, gg2, gs2, gg3, gs3])
+    grad_in, norm_grads, hidden, dck, dcv, *flights = fence(
+        grad_in, norm_grads, hidden, dck, dcv, *flights
+    )
     for stage in range(len(keys) + 1):
         for g, f in zip(groups, flights):
             g.take(f)
@@ -668,13 +671,17 @@
         flights = [g.fly(load, o[stage]) for g, load, o in zip(groups, loads, orders)]
         if stage == 0:
             grad_images = image_grads(dck, dcv).transpose(1, 0, 2)
-            grad_images, *flights = fence(grad_images, *flights)
+            other = swap(norm_grads, "dp", dp_size, 1)
+            grad_images, other, *flights = fence(grad_images, other, *flights)
+            norm_grads = norm_grads + other
         if stage == 1:
-            block_out, *flights = fence(finish(hidden), *flights)
+            other = swap(norm_grads, "dp", dp_size, 2)
+            block_out, other, *flights = fence(finish(hidden), other, *flights)
+            norm_grads = norm_grads + other
     for g, f in zip(groups, flights):
         g.take(f)
     g_self = [g.total(g.terms)[i] for g in groups for i in range(2)]
-    norm_grads = butterfly_sum(jnp.stack([gg1, gs1, gg2, gs2, gg3, gs3]), axes)
+    norm_grads = butterfly_sum(norm_grads, axes[1:])
     norm_grads = lax.dynamic_slice(norm_grads, (0, offset), (6, mine))
     weight_grads = [g.T for g in g_self + g_cross + [g_mlp_in, g_mlp_out]]
     return (

time: 688 us -> 686 us (level)
  waiting for transfers between devices: 158 us -> 143 us
  Pallas kernels: 134 us -> 144 us
    ppermute x32, waiting for transfers between devices: 50.9 us -> 39.5 us  [swap(): return lax.ppermute(value, axis, [(i, i ^ bit) for i in range(size)])]
    unnamed x143 -> x141, local copies, waits for them, and re-layouts: 30.8 us -> 29 us
  transfers between devices with their start and end apart: 37 -> 37, of which waited for: 16 -> 15; matrix products, arithmetic and copies ran while one was open for 40% -> 40% of each run, Pallas kernels for 19% -> 21%
where the time goes in v8:
time: 686 us; the launch traced here: 679 us
  matrix products  224 us (33%)
  Pallas kernels  144 us (21%)
  waiting for transfers between devices  143 us (21%)
  other arithmetic  73.8 us (11%)
  local copies, waits for them, and re-layouts  45.5 us (7%)
  starting transfers between devices  33.5 us (5%)
  between operations  15.3 us (2%)
    dot_general x29, matrix products, contract(): lax.dot_general(a, b, ((left, right), ((), ())), preferred_element_type=j...  224 us
    all_gather x1, waiting for transfers between devices, gather(): lax.all_gather(lower_stack([m.T for m in masters]), AXES, axis=1, tiled=T...  92.6 us
    pallas_call x1, Pallas kernels, cross_backward(): pl.pallas_call(functools.partial(cross_backward_kernel, pairs), out_shape...  53.3 us
    ppermute x32, waiting for transfers between devices, swap(): return lax.ppermute(value, axis, [(i, i ^ bit) for i in range(size)])  39.5 us
    ppermute x32, starting transfers between devices, swap(): return lax.ppermute(value, axis, [(i, i ^ bit) for i in range(size)])  32.9 us
    pallas_call x1, Pallas kernels, cross_forward(): pl.pallas_call(functools.partial(cross_forward_kernel, pairs), out_shape=...  32.1 us
    convert_element_type x14, other arithmetic, cut(): return out.astype(jnp.bfloat16)  31.2 us
    unnamed x141, local copies, waits for them, and re-layouts  29 us
  transfers between devices with their start and end apart: 37, of which 15 were waited for; matrix products, arithmetic and copies ran while one was open for 40% of the time, Pallas kernels for 21%

profile of v8, /device:TPU:0, one launch (start us, length us, event | category | flops | bytes accessed | tf_op | source)
XLA Modules:
  0.0 679.0 jit_solution(16525250164220422184)
XLA Ops:
  36.6 92.6 %all-gather.3.cloned.1.call-done = bf16[8,1024,1024]{2,1,0:T(8,128)(2,1)} async-done(((bf16[8,32,1024]{2,1,0:T(8,128)(2,1)}), bf16[8,1024,1024]{2,1,0:T(8,128)(2,1)}) %all-gather.3.cloned.1.call-update) | async-done | bytes 16777232 | tf_op jit(solution)/shard_map/all_gather | solution.py:533
  143.8 19.1 %self_forward.1 = (bf16[1024,1024]{1,0:T(8,128)(2,1)}, f32[2,8,1024]{2,1,0:T(8,128)}) custom-call(s32[5]{0:T(128)} %convert_reduce_fusion.1.starts, bf16[1024,1024]{1,0:T(8,128)(2,1)} %convolution_convert_fusion.13.q_ref, bf16[1024,1024]{1,0:T(8,128)(2,1)} %convolution_convert_fusion.12.k_ref, bf16[1024,1024]{1,0:T(8,128)(2,1)} %convolution_convert_fusion.11.v_ref), custom_call_target="tpu_custom_call" | custom-call | flops 5368709120 | bytes 10485760 | tf_op jit(solution)/shard_map/self_forward/pallas_call | solution.py:318
  169.8 6.2 convolution_convert_fusion.10.q_ref
  177.8 7.7 %convert_bitcast_fusion.2.k_ref = bf16[4,588,1024]{2,1,0:T(8,128)(2,1)} fusion(bf16[4,588,1024]{2,0,1:T(4,128)(2,1)S(1)} %bitcast.561, bf16[8,1024,1024]{2,1,0:T(8,128)(2,1)S(1)} %bitcast.491), kind=kOutput, calls=%fused_computation.30 | convolution fusion | flops 4934909952 | bytes 11730944 | tf_op jit(solution)/shard_map/dot_general | solution.py:372
  185.5 7.9 %convert_bitcast_fusion.1.v_ref = bf16[4,588,1024]{2,1,0:T(8,128)(2,1)} fusion(bf16[4,588,1024]{2,0,1:T(4,128)(2,1)S(1)} %bitcast.561, bf16[8,1024,1024]{2,1,0:T(8,128)(2,1)S(1)} %bitcast.491), kind=kOutput, calls=%fused_computation.29 | convolution fusion | flops 4934909952 | bytes 11730944 | tf_op jit(solution)/shard_map/dot_general | solution.py:372
  193.4 32.1 %cross_forward.1 = (bf16[1024,1024]{1,0:T(8,128)(2,1)}, f32[2,8,1024]{2,1,0:T(8,128)}) custom-call(s32[5]{0:T(128)} %convert_reduce_fusion.1.starts, s32[4]{0:T(128)} %bitcast.562, bf16[1024,1024]{1,0:T(8,128)(2,1)} %convolution_convert_fusion.10.q_ref, bf16[4,588,1024]{2,1,0:T(8,128)(2,1)} %convert_bitcast_fusion.2.k_ref, ...), custom_call_target="tpu_custom_call" | custom-call | flops 13564379136 | bytes 20971520 | tf_op jit(solution)/shard_map/cross_forward/pallas_call | solution.py:266
  225.5 6.1 fusion.93
  234.3 11.2 %all-gather.5.cloned.1.call-done.rows_ref = bf16[2,4096,1024]{2,1,0:T(8,128)(2,1)} async-done(((bf16[2,128,1024]{2,1,0:T(8,128)(2,1)}), bf16[2,4096,1024]{2,1,0:T(8,128)(2,1)}) %all-gather.5.cloned.1.call-update) | async-done | bytes 16777232 | tf_op jit(solution)/shard_map/all_gather | solution.py:550
  245.5 18.8 %multiply_convert_fusion.1 = (bf16[1024,4096]{1,0:T(8,128)(2,1)}, f32[1024,4096]{1,0:T(8,128)}) fusion(bf16[2,4096,1024]{2,1,0:T(8,128)(2,1)} %all-gather.5.cloned.1.call-done.rows_ref, f32[1024,1024]{1,0:T(8,128)} %copy-done.4, f32[1024]{0:T(1024)S(1)} %bitcast.557, f32[1024]{0:T(1024)S(1)} %bitcast.539, f32[1024]{0:T(1024)S(1)} %add_rsqrt_fusion, ...), kind=kOutput, calls=%fused_computation.7 | convolution fusion | flops 8616148992 | bytes 37765120 | tf_op jit(solution)/shard_map/dot_general | solution.py:372
  264.2 11.3 %convolution_convert_fusion.1 = bf16[4096,1024]{0,1:T(8,128)(2,1)S(1)} fusion(bf16[1024,4096]{1,0:T(8,128)(2,1)} %get-tuple-element.143, bf16[1,1024,1024]{2,1,0:T(8,128)(2,1)S(1)} %copy-done.19), kind=kOutput, calls=%fused_computation.15 | convolution fusion | flops 8594128896 | bytes 18874368 | tf_op jit(solution)/shard_map/dot_general | solution.py:372
  280.4 9.0 %side_by_side.1 = bf16[1024,4096]{1,0:T(8,128)(2,1)} custom-call(bf16[2,4096,1024]{2,1,0:T(8,128)(2,1)} %all-gather.5.cloned.1.call-done.rows_ref), custom_call_target="tpu_custom_call" | custom-call | bytes 16777216 | tf_op jit(solution)/shard_map/side_by_side/pallas_call | solution.py:492
  289.4 17.8 %multiply_convert_fusion = bf16[1024,4096]{1,0:T(8,128)(2,1)} fusion(bf16[1024,1024]{1,0:T(8,128)(2,1)S(1)} %bitcast.515, bf16[1024,4096]{1,0:T(8,128)(2,1)} %side_by_side.1, f32[1024,4096]{1,0:T(8,128)} %get-tuple-element.257), kind=kOutput, calls=%fused_computation.6 | convolution fusion | flops 8640266240 | bytes 35651584 | tf_op jit(solution)/shard_map/dot_general | solution.py:372
  307.2 12.7 %convolution_convert_fusion = bf16[4096,1024]{1,0:T(8,128)(2,1)S(1)} fusion(bf16[1024,4096]{1,0:T(8,128)(2,1)} %multiply_convert_fusion, f32[1024,1024]{1,0:T(8,128)S(1)} %copy-done.5, f32[1024]{0:T(1024)S(1)} %bitcast.558, f32[1024]{0:T(1024)S(1)} %bitcast.540, f32[1024]{0:T(1024)S(1)} %add_rsqrt_fusion, f32[1024]{0:T(1024)S(1)} %broadcast_multiply_fusion.6), kind=kOutput, calls=%fused_computation.14 | convolution fusion | flops 8599371776 | bytes 20987904 | tf_op jit(solution)/shard_map/dot_general | solution.py:372
  330.5 15.4 %multiply_reduce_fusion = (f32[1024]{0:T(1024)}, f32[1024]{0:T(1024)S(1)}, f32[1024]{0:T(1024)S(1)}, f32[1024]{0:T(1024)}, f32[1024,1024]{1,0:T(8,128)S(1)}) fusion(f32[1024,1024]{1,0:T(8,128)S(1)} %copy-done.6, f32[1024]{0:T(1024)S(1)} %add_rsqrt_fusion, f32[1024]{0:T(1024)S(1)} %broadcast_multiply_fusion.6, f32[1024]{0:T(1024)S(1)} %bitcast.541, ...), kind=kOutput, calls=%fused_computation.58 | convolution fusion | flops 8599367680 | bytes 25194496 | tf_op jit(solution)/shard_map/dot_general | solution.py:372
  363.1 53.3 %cross_backward.1 = (bf16[1024,1024]{1,0:T(8,128)(2,1)}, bf16[4,588,1024]{2,1,0:T(8,128)(2,1)}, bf16[4,588,1024]{2,1,0:T(8,128)(2,1)}) custom-call(s32[5]{0:T(128)} %convert_reduce_fusion.1.starts, s32[4]{0:T(128)} %bitcast.563, bf16[1024,1024]{1,0:T(8,128)(2,1)} %convolution_convert_fusion.10.q_ref, bf16[4,588,1024]{2,1,0:T(8,128)(2,1)} %convert_bitcast_fusion.2.k_ref, ...), custom_call_target="tpu_custom_call" | custom-call | flops 33910947840 | bytes 31457280 | tf_op jit(solution)/shard_map/cross_backward/pallas_call | solution.py:290
  433.3 10.4 %bitcast_convert_fusion.1 = bf16[1024,1024]{1,0:T(8,128)(2,1)S(1)} fusion(bf16[4,588,1024]{2,1,0:T(8,128)(2,1)} %get-tuple-element.136, bf16[4,588,1024]{2,0,1:T(4,128)(2,1)} %param.22), kind=kOutput, calls=%fused_computation.56 | convolution fusion | flops 4933550080 | bytes 11730944 | tf_op jit(solution)/shard_map/dot_general | solution.py:372
  443.7 10.6 %bitcast_convert_fusion = bf16[1024,1024]{1,0:T(8,128)(2,1)S(1)} fusion(bf16[4,588,1024]{2,1,0:T(8,128)(2,1)} %get-tuple-element.137, bf16[4,588,1024]{2,0,1:T(4,128)(2,1)} %param.22), kind=kOutput, calls=%fused_computation.55 | convolution fusion | flops 4933550080 | bytes 11730944 | tf_op jit(solution)/shard_map/dot_general | solution.py:372
  464.0 7.4 %multiply_reduce_fusion.1 = (f32[1024]{0:T(1024)S(1)}, f32[1024]{0:T(1024)S(1)}, f32[1024]{0:T(1024)S(1)}, f32[1024]{0:T(1024)S(1)}, f32[1024,1024]{1,0:T(8,128)S(1)}) fusion(f32[1024,1024]{1,0:T(8,128)} %copy-done.8, f32[1024]{0:T(1024)S(1)} %copy-done.31, f32[1024]{0:T(1024)S(1)} %copy-done.23, f32[1024]{0:T(1024)S(1)} %bitcast.537, ...), kind=kOutput, calls=%fused_computation.59 | convolution fusion | flops 2156916736 | bytes 12611584 | tf_op jit(solution)/shard_map/dot_general | solution.py:372
  491.2 28.2 %self_backward.1 = (bf16[1024,1024]{1,0:T(8,128)(2,1)}, bf16[1024,1024]{1,0:T(8,128)(2,1)}, bf16[1024,1024]{1,0:T(8,128)(2,1)}) custom-call(s32[5]{0:T(128)} %convert_reduce_fusion.1.starts, bf16[1024,1024]{1,0:T(8,128)(2,1)} %convolution_convert_fusion.13.q_ref, bf16[1024,1024]{1,0:T(8,128)(2,1)} %convolution_convert_fusion.12.k_ref, ...), custom_call_target="tpu_custom_call" | custom-call | flops 13421772800 | bytes 16777216 | tf_op jit(solution)/shard_map/self_backward/pallas_call | solution.py:341
  575.8 15.4 %fusion.36 = f32[4,588,1024]{2,1,0:T(8,128)} fusion(bf16[2048,1024,1]{1,0,2:T(8,128)(2,1)S(1)} %bitcast.498, bf16[4,588,1024]{2,1,0:T(8,128)(2,1)} %get-tuple-element.137, bf16[4,588,1024]{2,1,0:T(8,128)(2,1)} %get-tuple-element.136), kind=kOutput, calls=%fused_computation.76 | convolution fusion | flops 9884270592 | bytes 23461888 | tf_op jit(solution)/shard_map/dot_general | solution.py:372
  598.3 8.8 %collective-permute-done.21 = bf16[2,2,2,2,32,1024]{5,4,0,3,2,1:T(8,128)(2,1)S(1)} collective-permute-done((bf16[2,2,2,2,32,1024]{5,4,0,3,2,1:T(8,128)(2,1)}, bf16[2,2,2,2,32,1024]{5,4,0,3,2,1:T(8,128)(2,1)S(1)}, u32[]{:S(2)}, u32[]{:S(2)}) %collective-permute-start.21) | collective-permute-done | bytes 1048608 | tf_op jit(solution)/shard_map/ppermute | solution.py:399
  614.1 15.0 %add_convert_fusion = bf16[1024,1024]{1,0:T(8,128)(2,1)} fusion(f32[1024,1024]{1,0:T(8,128)S(1)} %copy-done.7, bf16[1024,4096]{1,0:T(8,128)(2,1)} %get-tuple-element.143, bf16[1024,4096]{1,0:T(8,128)(2,1)} %side_by_side.1), kind=kOutput, calls=%fused_computation.57 | convolution fusion | flops 8592031744 | bytes 23068672 | tf_op jit(solution)/shard_map/dot_general | solution.py:372
  635.4 13.8 %copy.117 = f32[4,588,1024]{2,0,1:T(4,128)} copy(f32[4,588,1024]{2,1,0:T(8,128)} %fusion.36) | data formatting | bytes 19267584
  661.0 5.8 collective-permute-done.29
  (324 shorter events, 227.2 us)
Async XLA Ops:
  7.3 121.9 %all-gather.3.cloned.1.call-start = ((), (), s32[]{:S(2)}) async-start(), calls=%async_computation.3 | async-start | bytes 17301504 | tf_op jit(solution)/shard_map/all_gather | solution.py:533
  9.6 235.8 %all-gather.5.cloned.1.call-start = ((), (), s32[]{:S(2)}) async-start(), calls=%async_computation.4 | async-start | bytes 17301504 | tf_op jit(solution)/shard_map/all_gather | solution.py:550
  12.8 578.4 %reduce-scatter.8.cloned.1.call-start = ((), (), s32[]{:S(2)}) async-start(), calls=%async_computation.6 | async-start | bytes 2359296 | tf_op jit(solution)/shard_map/reduce_scatter | solution.py:472
  280.2 27.1 %collective-permute-start.5 = (bf16[1,2,2,2,2,32,4096]{6,5,4,3,2,1,0:T(8,128)(2,1)}, bf16[1,2,2,2,2,32,4096]{6,5,4,3,2,1,0:T(8,128)(2,1)}, u32[]{:S(2)}, u32[]{:S(2)}) collective-permute-start(bf16[1,2,2,2,2,32,4096]{6,5,4,3,2,1,0:T(8,128)(2,1)} %dynamic-slice_bitcast_fusion.1), channel_id=1, source_target_pairs={{0,8},{8,0},{16,24},{24,16},{1,9},{9,1},{17,25},{25,17},{2,10},{10... | collective-permute-start | bytes 12582920 | tf_op jit(solution)/shard_map/ppermute | solution.py:399
  324.4 24.9 %collective-permute-start.6 = (bf16[1,2,2,2,2,128,1024]{6,5,4,3,2,1,0:T(8,128)(2,1)}, bf16[1,2,2,2,2,128,1024]{6,5,4,3,2,1,0:T(8,128)(2,1)}, u32[]{:S(2)}, u32[]{:S(2)}) collective-permute-start(bf16[1,2,2,2,2,128,1024]{6,5,4,3,2,1,0:T(8,128)(2,1)} %dynamic-slice_bitcast_fusion), channel_id=1, source_target_pairs={{0,8},{8,0},{16,24},{24,16},{1,9},{9,1},{17,25},{25,17},{2,10},{10... | collective-permute-start | bytes 12582920 | tf_op jit(solution)/shard_map/ppermute | solution.py:399
  329.1 87.3 %collective-permute-start.7 = (bf16[1,2,2,2,32,4096]{5,4,3,2,1,0:T(8,128)(2,1)}, bf16[1,2,2,2,32,4096]{5,4,3,2,1,0:T(8,128)(2,1)}, u32[]{:S(2)}, u32[]{:S(2)}) collective-permute-start(bf16[1,2,2,2,32,4096]{5,4,3,2,1,0:T(8,128)(2,1)} %fusion.35), channel_id=1, source_target_pairs={{0,16},{8,24},{16,0},{24,8},{1,17},{9,25},{17,1},{25,9},{2,18},{10... | collective-permute-start | bytes 6291464 | tf_op jit(solution)/shard_map/ppermute | solution.py:399
  355.0 67.0 %collective-permute-start.8 = (bf16[1,2,2,2,128,1024]{5,4,3,2,1,0:T(8,128)(2,1)}, bf16[1,2,2,2,128,1024]{5,4,3,2,1,0:T(8,128)(2,1)S(1)}, u32[]{:S(2)}, u32[]{:S(2)}) collective-permute-start(bf16[1,2,2,2,128,1024]{5,4,3,2,1,0:T(8,128)(2,1)} %fusion.34), channel_id=1, source_target_pairs={{0,16},{8,24},{16,0},{24,8},{1,17},{9,25},{17,1},{25,9},{2,18},{10... | collective-permute-start | bytes 6291464 | tf_op jit(solution)/shard_map/ppermute | solution.py:399
  427.4 165.6 %reduce-scatter.10.cloned.1.call-start = ((), (), s32[]{:S(2)}) async-start(), calls=%async_computation.7 | async-start | bytes 2359296
  454.4 20.2 %collective-permute-start.9 = (bf16[1,2,2,2,2,32,1024]{6,5,4,3,2,1,0:T(8,128)(2,1)S(1)}, bf16[1,2,2,2,2,32,1024]{6,5,4,3,2,1,0:T(8,128)(2,1)}, u32[]{:S(2)}, u32[]{:S(2)}) collective-permute-start(bf16[1,2,2,2,2,32,1024]{6,5,4,3,2,1,0:T(8,128)(2,1)S(1)} %dynamic-slice_bitcast_fusion.5), channel_id=1, source_target_pairs={{0,8},{8,0},{16,24},{24,16},{1,9},{9,1},{17,25},{25,17},{2,10},{10... | collective-permute-start | bytes 3145736 | tf_op jit(solution)/shard_map/ppermute | solution.py:399
  455.6 19.0 %collective-permute-start.10 = (bf16[1,2,2,2,2,32,1024]{6,5,4,3,2,1,0:T(8,128)(2,1)}, bf16[1,2,2,2,2,32,1024]{6,5,4,3,2,1,0:T(8,128)(2,1)}, u32[]{:S(2)}, u32[]{:S(2)}) collective-permute-start(bf16[1,2,2,2,2,32,1024]{6,5,4,3,2,1,0:T(8,128)(2,1)} %dynamic-slice_bitcast_fusion.4), channel_id=1, source_target_pairs={{0,8},{8,0},{16,24},{24,16},{1,9},{9,1},{17,25},{25,17},{2,10},{10... | collective-permute-start | bytes 3145736 | tf_op jit(solution)/shard_map/ppermute | solution.py:399
  457.2 17.4 %collective-permute-start.11 = (bf16[1,2,2,2,2,32,1024]{6,5,4,3,2,1,0:T(8,128)(2,1)}, bf16[1,2,2,2,2,32,1024]{6,5,4,3,2,1,0:T(8,128)(2,1)}, u32[]{:S(2)}, u32[]{:S(2)}) collective-permute-start(bf16[1,2,2,2,2,32,1024]{6,5,4,3,2,1,0:T(8,128)(2,1)} %dynamic-slice_bitcast_fusion.3), channel_id=1, source_target_pairs={{0,8},{8,0},{16,24},{24,16},{1,9},{9,1},{17,25},{25,17},{2,10},{10... | collective-permute-start | bytes 3145736 | tf_op jit(solution)/shard_map/ppermute | solution.py:399
  463.9 206.6 %reduce-scatter.6.cloned.1.call-start = ((), (), s32[]{:S(2)}) async-start(), calls=%async_computation.5 | async-start | bytes 2359296 | tf_op jit(solution)/shard_map/reduce_scatter | solution.py:472
  477.5 46.7 %collective-permute-start.13 = (bf16[1,2,2,2,32,1024]{5,4,3,2,1,0:T(8,128)(2,1)S(1)}, bf16[1,2,2,2,32,1024]{5,4,3,2,1,0:T(8,128)(2,1)}, u32[]{:S(2)}, u32[]{:S(2)}) collective-permute-start(bf16[1,2,2,2,32,1024]{5,4,3,2,1,0:T(8,128)(2,1)S(1)} %fusion.72), channel_id=1, source_target_pairs={{0,16},{8,24},{16,0},{24,8},{1,17},{9,25},{17,1},{25,9},{2,18},{10... | collective-permute-start | bytes 1572872 | tf_op jit(solution)/shard_map/ppermute | solution.py:399
  480.4 43.8 %collective-permute-start.14 = (bf16[1,2,2,2,32,1024]{5,4,3,2,1,0:T(8,128)(2,1)S(1)}, bf16[1,2,2,2,32,1024]{5,4,3,2,1,0:T(8,128)(2,1)}, u32[]{:S(2)}, u32[]{:S(2)}) collective-permute-start(bf16[1,2,2,2,32,1024]{5,4,3,2,1,0:T(8,128)(2,1)S(1)} %fusion.71), channel_id=1, source_target_pairs={{0,16},{8,24},{16,0},{24,8},{1,17},{9,25},{17,1},{25,9},{2,18},{10... | collective-permute-start | bytes 1572872 | tf_op jit(solution)/shard_map/ppermute | solution.py:399
  483.3 41.0 %collective-permute-start.15 = (bf16[1,2,2,2,32,1024]{5,4,3,2,1,0:T(8,128)(2,1)}, bf16[1,2,2,2,32,1024]{5,4,3,2,1,0:T(8,128)(2,1)}, u32[]{:S(2)}, u32[]{:S(2)}) collective-permute-start(bf16[1,2,2,2,32,1024]{5,4,3,2,1,0:T(8,128)(2,1)} %fusion.70), channel_id=1, source_target_pairs={{0,16},{8,24},{16,0},{24,8},{1,17},{9,25},{17,1},{25,9},{2,18},{10... | collective-permute-start | bytes 1572872 | tf_op jit(solution)/shard_map/ppermute | solution.py:399
  486.9 38.3 %collective-permute-start.16 = (bf16[1,2,2,2,32,1024]{5,4,3,2,1,0:T(8,128)(2,1)}, bf16[1,2,2,2,32,1024]{5,4,3,2,1,0:T(8,128)(2,1)}, u32[]{:S(2)}, u32[]{:S(2)}) collective-permute-start(bf16[1,2,2,2,32,1024]{5,4,3,2,1,0:T(8,128)(2,1)} %fusion.69), channel_id=1, source_target_pairs={{0,16},{8,24},{16,0},{24,8},{1,17},{9,25},{17,1},{25,9},{2,18},{10... | collective-permute-start | bytes 1572872 | tf_op jit(solution)/shard_map/ppermute | solution.py:399
  537.1 31.3 %collective-permute-start.17 = (bf16[2,2,2,2,2,32,1024]{6,5,0,2,4,3,1:T(8,128)(2,1)}, bf16[2,2,2,2,2,32,1024]{6,5,0,2,4,3,1:T(8,128)(2,1)}, u32[]{:S(2)}, u32[]{:S(2)}) collective-permute-start(bf16[2,2,2,2,2,32,1024]{6,5,0,2,4,3,1:T(8,128)(2,1)} %copy_bitcast_fusion.1), channel_id=1, source_target_pairs={{0,8},{8,0},{16,24},{24,16},{1,9},{9,1},{17,25},{25,17},{2,10},{10... | collective-permute-start | bytes 6291464 | tf_op jit(solution)/shard_map/ppermute | solution.py:399
  538.7 29.7 %collective-permute-start.18 = (bf16[2,2,2,2,2,32,1024]{6,5,0,2,4,3,1:T(8,128)(2,1)}, bf16[2,2,2,2,2,32,1024]{6,5,0,2,4,3,1:T(8,128)(2,1)}, u32[]{:S(2)}, u32[]{:S(2)}) collective-permute-start(bf16[2,2,2,2,2,32,1024]{6,5,0,2,4,3,1:T(8,128)(2,1)} %copy_bitcast_fusion), channel_id=1, source_target_pairs={{0,8},{8,0},{16,24},{24,16},{1,9},{9,1},{17,25},{25,17},{2,10},{10... | collective-permute-start | bytes 6291464 | tf_op jit(solution)/shard_map/ppermute | solution.py:399
  572.5 21.7 %collective-permute-start.19 = (f32[6,1024]{1,0:T(8,128)S(1)}, f32[6,1024]{1,0:T(8,128)S(1)}, u32[]{:S(2)}, u32[]{:S(2)}) collective-permute-start(f32[6,1024]{1,0:T(8,128)S(1)} %stack.70), channel_id=1, source_target_pairs={{0,8},{8,0},{16,24},{24,16},{1,9},{9,1},{17,25},{25,17},{2,10},{10... | collective-permute-start | bytes 73736 | tf_op jit(solution)/shard_map/ppermute | solution.py:399
  572.7 25.6 %collective-permute-start.20 = (bf16[2,2,2,2,32,1024]{5,4,0,3,2,1:T(8,128)(2,1)S(1)}, bf16[2,2,2,2,32,1024]{5,4,0,3,2,1:T(8,128)(2,1)S(1)}, u32[]{:S(2)}, u32[]{:S(2)}) collective-permute-start(bf16[2,2,2,2,32,1024]{5,4,0,3,2,1:T(8,128)(2,1)S(1)} %copy.103), channel_id=1, source_target_pairs={{0,16},{8,24},{16,0},{24,8},{1,17},{9,25},{17,1},{25,9},{2,18},{10... | collective-permute-start | bytes 3145736 | tf_op jit(solution)/shard_map/ppermute | solution.py:399
  575.2 31.9 %collective-permute-start.21 = (bf16[2,2,2,2,32,1024]{5,4,0,3,2,1:T(8,128)(2,1)}, bf16[2,2,2,2,32,1024]{5,4,0,3,2,1:T(8,128)(2,1)S(1)}, u32[]{:S(2)}, u32[]{:S(2)}) collective-permute-start(bf16[2,2,2,2,32,1024]{5,4,0,3,2,1:T(8,128)(2,1)} %copy.104), channel_id=1, source_target_pairs={{0,1},{1,0},{2,3},{3,2},{4,5},{5,4},{6,7},{7,6},{8,9},{9,8},{10,11... | collective-permute-start | bytes 3145736 | tf_op jit(solution)/shard_map/ppermute | solution.py:399
  610.1 19.0 %collective-permute-start.22 = (f32[6,1024]{1,0:T(8,128)S(1)}, f32[6,1024]{1,0:T(8,128)S(1)}, u32[]{:S(2)}, u32[]{:S(2)}) collective-permute-start(f32[6,1024]{1,0:T(8,128)S(1)} %add.994), channel_id=1, source_target_pairs={{0,16},{8,24},{16,0},{24,8},{1,17},{9,25},{17,1},{25,9},{2,18},{10... | collective-permute-start | bytes 73736 | tf_op jit(solution)/shard_map/ppermute | solution.py:399
  611.5 17.6 %collective-permute-start.23 = (bf16[2,2,2,32,1024]{4,3,0,2,1:T(8,128)(2,1)S(1)}, bf16[2,2,2,32,1024]{4,3,0,2,1:T(8,128)(2,1)S(1)}, u32[]{:S(2)}, u32[]{:S(2)}) collective-permute-start(bf16[2,2,2,32,1024]{4,3,0,2,1:T(8,128)(2,1)S(1)} %copy.108), channel_id=1, source_target_pairs={{0,1},{1,0},{2,3},{3,2},{4,5},{5,4},{6,7},{7,6},{8,9},{9,8},{10,11... | collective-permute-start | bytes 1572872 | tf_op jit(solution)/shard_map/ppermute | solution.py:399
  632.5 22.0 %collective-permute-start.28 = (bf16[2,2,32,1024]{3,2,0,1:T(8,128)(2,1)}, bf16[2,2,32,1024]{3,2,0,1:T(8,128)(2,1)}, u32[]{:S(2)}, u32[]{:S(2)}) collective-permute-start(bf16[2,2,32,1024]{3,2,0,1:T(8,128)(2,1)} %fusion.74), channel_id=1, source_target_pairs={{0,2},{1,3},{2,0},{3,1},{4,6},{5,7},{6,4},{7,5},{8,10},{9,11},{10,... | collective-permute-start | bytes 786440 | tf_op jit(solution)/shard_map/ppermute | solution.py:399
  (83 other events, 1327.9 us)
Sparse Core Ops, SparseCore 0:
  11.7 117.4 all-gather.2
  132.8 112.5 all-gather.4
  427.6 66.4 reduce-scatter.7
  497.5 67.4 reduce-scatter.9
  568.3 74.1 reduce-scatter.5
